TPU v7x, 32 devices: a whole 2x2x4 slice. The times are simulated.
32 devices in a mesh: ty: 4 (over y, x), tx: 8 (over z, core).
Axes of the slice: x: 2, y: 2, z: 4, core: 2. Of those that a mesh axis runs over, the one named last changes fastest.
Arguments:
- adjoint: float32 [4, 36, 256, 1024], P(None, None, 'ty', 'tx'), may hold values from -6 to 6
- background_flow: float32 [2, 36, 256, 1024], P(None, None, 'ty', 'tx'), may hold values from -3 to 3
- vert_diff: float32 [36, 256, 1024], P(None, 'ty', 'tx'), may hold values from 0.05 to 4
- wet_levels: int32 [256, 1024], P('ty', 'tx'), may hold values from 0 to 36
- rotation: int32 [4, 8], P('ty', 'tx'), may hold values from 0 to 3
- face_map: int32 [4, 8], P('ty', 'tx'), may hold values from 0 to 3, as said below
- ctrl_owner: int32 [32], replicated, may hold values from 0 to 31, each once
Outputs:
- adjoint_out: float32 [4, 36, 256, 1024], P(None, None, 'ty', 'tx')
- sensitivity: float32 [32, 8192], P(('ty', 'tx'))
Inputs may be any that keep to these rules, and one draw needn't show every extreme that they name: `rotation`: quarter turns from the common frame to the tile's frame. `wet_levels`: levels below the wet ones are land. `face_map`: each face is a band of 2 neighbouring whole tile columns, neighbouring with wrap-around; every face appears. A permutation: control tile j of face f belongs to the device of flat index ctrl_owner[f * 8 + j].
All inputs are finite; a program needn't handle non-finite values.
Results may differ from a plain program's by a relative error of at most 0.0003.
Values sent between devices are 32-bit elements; how exact they have to be, the bound alone decides.
No kernel may reach another device: no remote copies, remote signals or barrier semaphores. Data moves between devices by JAX's collectives and lax.ppermute only.
A program may use at most 192 MiB of HBM per device.

v0:
```python
import math

import jax
import jax.numpy as jnp
from jax import lax
from jax.sharding import PartitionSpec as P

STEPS = 2
KY = 128
KX = 128
NFACE = 4


ADVECT_COEF = 0.3
DIFFUSE_COEF = 0.12
VISCOUS_COEF = 0.1
THERMAL_COEF = 0.4
HALINE_COEF = 0.3
PRESSURE_COEF = 0.4
SALINE_WEIGHT = 0.8
CORIOLIS_PEAK = 0.5
MOMENTUM_RATIO = 1.5


def padded_2(block, sides, width, periodic):
    for axis, dim in sides:
        count = lax.axis_size(axis)
        forward = [(i, i + 1) for i in range(count - 1)]
        if periodic:
            forward.append((count - 1, 0))
        backward = [(target, source) for source, target in forward]
        low = lax.ppermute(
            lax.slice_in_dim(block, block.shape[dim] - width, None, axis=dim), axis, forward
        )
        high = lax.ppermute(lax.slice_in_dim(block, 0, width, axis=dim), axis, backward)
        block = jnp.concatenate([low, block, high], axis=dim)
    return block


def turn_of(turn_codes):
    cosine = jnp.where(turn_codes == 0, 1.0, jnp.where(turn_codes == 2, -1.0, 0.0)).astype(
        jnp.float32
    )
    sine_part = jnp.where(turn_codes == 1, 1.0, jnp.where(turn_codes == 3, -1.0, 0.0)).astype(
        jnp.float32
    )
    return (cosine, sine_part)


def to_common(fields, cosine, sine_part):
    east_vel = fields[2]
    north_vel = fields[3]
    return jnp.stack(
        [
            fields[0],
            fields[1],
            cosine * east_vel - sine_part * north_vel,
            sine_part * east_vel + cosine * north_vel,
        ]
    )


def from_common(fields, cosine, sine_part):
    east_vel = fields[2]
    north_vel = fields[3]
    return jnp.stack(
        [
            fields[0],
            fields[1],
            cosine * east_vel + sine_part * north_vel,
            cosine * north_vel - sine_part * east_vel,
        ]
    )


def coriolis_rows(first_row, row_count, row_total):
    rows = (first_row + jnp.arange(row_count, dtype=jnp.int32)).astype(jnp.float32)
    return (CORIOLIS_PEAK * jnp.sin(math.pi * (rows + 0.5) / row_total - 0.5 * math.pi))[:, None]


def cosine_table(first_row, row_count, row_total, mode_count):
    rows = first_row + jnp.arange(row_count, dtype=jnp.int32)
    modes = jnp.arange(mode_count, dtype=jnp.int32)
    phase_index = (2 * rows[:, None] + 1) * modes[None, :] % (4 * row_total)
    return jnp.cos(phase_index.astype(jnp.float32) * (math.pi / (2 * row_total)))


def explicit(padded, background_flow, wet_mask, coriolis):
    height = padded.shape[2] - 4
    width = padded.shape[3] - 4

    def nearby(shift_y, shift_x, start_comp, stop_comp):
        return padded[
            start_comp:stop_comp,
            :,
            2 + shift_y : 2 + shift_y + height,
            2 + shift_x : 2 + shift_x + width,
        ]

    centre = nearby(0, 0, 0, 4)
    east_one = nearby(0, 1, 0, 4)
    west_one = nearby(0, -1, 0, 4)
    north_one = nearby(1, 0, 0, 4)
    south_one = nearby(-1, 0, 0, 4)
    east_two = nearby(0, 2, 0, 2)
    west_two = nearby(0, -2, 0, 2)
    north_two = nearby(2, 0, 0, 2)
    south_two = nearby(-2, 0, 0, 2)
    grad_x = (8.0 * (east_one[:2] - west_one[:2]) - (east_two - west_two)) / 12.0
    grad_y = (8.0 * (north_one[:2] - south_one[:2]) - (north_two - south_two)) / 12.0
    spread = east_one + west_one + north_one + south_one - 4.0 * centre
    inflow = 0.5 * (east_one[2] - west_one[2] + north_one[3] - south_one[3])
    buoy_x = 0.5 * (
        east_one[0] - SALINE_WEIGHT * east_one[1] - (west_one[0] - SALINE_WEIGHT * west_one[1])
    )
    buoy_y = 0.5 * (
        north_one[0] - SALINE_WEIGHT * north_one[1] - (south_one[0] - SALINE_WEIGHT * south_one[1])
    )
    carried = background_flow[0][None] * grad_x + background_flow[1][None] * grad_y
    heat_new = (
        centre[0] + ADVECT_COEF * carried[0] + DIFFUSE_COEF * spread[0] + THERMAL_COEF * inflow
    )
    salt_new = (
        centre[1] + ADVECT_COEF * carried[1] + DIFFUSE_COEF * spread[1] - HALINE_COEF * inflow
    )
    zonal_new = centre[2] + VISCOUS_COEF * spread[2] + coriolis * centre[3] - PRESSURE_COEF * buoy_x
    merid_new = centre[3] + VISCOUS_COEF * spread[3] - coriolis * centre[2] - PRESSURE_COEF * buoy_y
    return jnp.stack([heat_new, salt_new, zonal_new, merid_new]) * wet_mask[None]


def vertical(rhs_fields, vert_diff, wet_mask):
    levels = rhs_fields.shape[1]
    factor = jnp.array([1.0, 1.0, MOMENTUM_RATIO, MOMENTUM_RATIO], dtype=jnp.float32)[:, None, None]
    links = [
        factor * (vert_diff[level_index] * wet_mask[level_index + 1])[None]
        for level_index in range(levels - 1)
    ]
    ratios = []
    values = []
    for level_index in range(levels):
        centre_coef = jnp.ones_like(rhs_fields[:, 0])
        if level_index > 0:
            centre_coef = centre_coef + links[level_index - 1]
        if level_index < levels - 1:
            centre_coef = centre_coef + links[level_index]
        if level_index == 0:
            pivot_value = centre_coef
            value_now = rhs_fields[:, 0] / pivot_value
        else:
            link_above = links[level_index - 1]
            pivot_value = centre_coef + link_above * ratios[-1]
            value_now = (rhs_fields[:, level_index] + link_above * values[-1]) / pivot_value
        if level_index < levels - 1:
            ratios.append(-links[level_index] / pivot_value)
        else:
            ratios.append(jnp.zeros_like(pivot_value))
        values.append(value_now)
    result = [values[-1]]
    for level_index in range(levels - 2, -1, -1):
        result.insert(0, values[level_index] - ratios[level_index] * result[0])
    return jnp.stack(result, 1)


def body(adjoint, background_flow, vert_diff, wet_levels, rotation, face_map, ctrl_owner):
    levels = adjoint.shape[1]
    height = adjoint.shape[2]
    width = adjoint.shape[3]
    row_first = lax.axis_index("ty") * height
    col_first = lax.axis_index("tx") * width
    rows_total = height * lax.axis_size("ty")
    cols_total = width * lax.axis_size("tx")
    wet_mask = (jnp.arange(levels, dtype=jnp.int32)[:, None, None] < wet_levels[None]).astype(
        jnp.float32
    )
    cosine, sine_part = turn_of(rotation[0, 0])
    fields = to_common(adjoint, cosine, sine_part)
    surfaces = []
    coriolis = coriolis_rows(row_first, height, rows_total)
    for step_index in range(STEPS):
        rows_done = padded_2(fields, (("ty", 2),), 2, False)
        padded = padded_2(rows_done, (("tx", 3),), 2, True)
        fields = vertical(
            explicit(padded, background_flow, wet_mask, coriolis), vert_diff, wet_mask
        )
        surfaces.append(fields[:2, 0])
    adjoint_out = from_common(fields, cosine, sine_part)
    surface_all = jnp.stack(surfaces)
    row_modes = cosine_table(row_first, height, rows_total, KY)
    col_modes = cosine_table(col_first, width, cols_total, KX)
    along_rows = jnp.einsum(
        "yk,rfyx->rfkx", row_modes, surface_all, precision=lax.Precision.HIGHEST
    )
    coefficients = jnp.einsum(
        "rfkx,xj->rfkj", along_rows, col_modes, precision=lax.Precision.HIGHEST
    )
    norm_factor = math.sqrt(2.0 * NFACE / (rows_total * cols_total))
    per_face = ctrl_owner.shape[0] // NFACE
    blocks = (coefficients * norm_factor).reshape(per_face, -1)
    owners_here = lax.dynamic_slice_in_dim(ctrl_owner, face_map[0, 0] * per_face, per_face)
    rows_each = ctrl_owner.shape[0] // lax.axis_size(("ty", "tx"))
    targets = jnp.arange(rows_each * lax.axis_size(("ty", "tx")), dtype=jnp.int32)
    selector = (owners_here[None, :] == targets[:, None]).astype(jnp.float32)
    sensitivity = lax.psum_scatter(
        jnp.dot(
            selector, blocks, precision=lax.Precision.HIGHEST, preferred_element_type=jnp.float32
        ),
        ("ty", "tx"),
        scatter_dimension=0,
        tiled=True,
    )
    return (adjoint_out, sensitivity)


def solution(mesh):
    return jax.shard_map(
        body,
        mesh=mesh,
        in_specs=(
            P(None, None, "ty", "tx"),
            P(None, None, "ty", "tx"),
            P(None, "ty", "tx"),
            P("ty", "tx"),
            P("ty", "tx"),
            P("ty", "tx"),
            P(),
        ),
        out_specs=(P(None, None, "ty", "tx"), P(("ty", "tx"), None)),
        check_vma=False,
    )
```

profile of v0, /device:TPU:0, one launch (start us, length us, event | category | flops | bytes accessed | tf_op | source)
XLA Modules:
  0.0 370.9 jit_solution(5219375492486317422)
XLA Ops:
  12.5 5.5 %collective-permute-start = (f32[4,36,2,128]{3,0,2,1:T(4,128)S(1)}, f32[4,36,2,128]{3,0,2,1:T(4,128)S(1)}, u32[]{:S(2)}, u32[]{:S(2)}) collective-permute-start(f32[4,36,2,128]{3,0,2,1:T(4,128)S(1)} %copy.164), channel_id=1, source_target_pairs={{0,8},{8,16},{16,24},{1,9},{9,17},{17,25},{2,10},{10,18},{18,26},{... | collective-permute-start | bytes 442376 | tf_op jit(solution)/shard_map/ppermute | solution.py:32
  23.0 2.3 pad_maximum_fusion.2
  25.3 5.9 %fusion.682 = (f32[4,36,68,2]{3,2,0,1:T(8,128)}, f32[4,36,68,2]{3,2,0,1:T(8,128)}) fusion(f32[4,36,68,128]{3,2,0,1:T(8,128)S(1)} %pad_maximum_fusion.2), kind=kLoop, calls=%fused_computation.1301 | loop fusion | bytes 313344 | tf_op jit(solution)/shard_map/slice | solution.py:35
  31.2 3.5 copy.168
  34.7 3.1 collective-permute-start.2
  37.8 3.5 copy.170
  41.8 6.2 %pad_maximum_fusion.3 = (f32[4,36,66,128]{3,2,0,1:T(8,128)}, f32[4,36,66,128]{3,2,0,1:T(8,128)}) fusion(f32[4,36,2,128]{3,2,0,1:T(2,128)S(1)} %copy.167, f32[1,36,64,128]{3,2,0,1:T(8,128)S(1)} %get-tuple-element.137, f32[1,36,64,128]{3,2,0,1:T(8,128)S(1)} %get-tuple-element.136, f32[4,36,2,128]{3,2,0,1:T(2,128)S(1)} %copy.166, f32[4,36,64,128]{3,2,1,0:T(8,128)} %param.9), kind=kLoop, calls=%fused_computation.15 | loop fusion | flops 7299072 | bytes 14745600 | tf_op jit(solution)/shard_map/concatenate | solution.py:36
  48.0 3.4 copy.169
  51.4 3.4 copy.171
  54.8 17.8 %pad_maximum_fusion = (f32[4,36,68,130]{3,2,0,1:T(8,128)}, f32[4,36,68,130]{3,2,0,1:T(8,128)}) fusion(f32[4,36,68,2]{3,2,0,1:T(8,128)} %copy.169, f32[4,36,2,128]{3,2,0,1:T(2,128)S(1)} %copy.167, f32[1,36,64,128]{3,2,0,1:T(8,128)S(1)} %get-tuple-element.137, f32[1,36,64,128]{3,2,0,1:T(8,128)S(1)} %get-tuple-element.136, f32[4,36,2,128]{3,2,0,1:T(2,128)S(1)} %copy.166, ...), kind=kLoop, calls=%fused_computation.10 | loop fusion | flops 12729600 | bytes 25814016 | tf_op jit(solution)/shard_map/concatenate | solution.py:36
  72.6 14.0 %fusion.5 = f32[4,36,64,128]{3,2,0,1:T(8,128)} fusion(f32[4,36,66,128]{3,2,0,1:T(8,128)} %get-tuple-element.133, f32[4,36,66,128]{3,2,0,1:T(8,128)} %get-tuple-element.132, f32[4,36,68,130]{3,2,0,1:T(8,128)} %get-tuple-element.125, f32[4,36,68,130]{3,2,0,1:T(8,128)} %get-tuple-element.124, f32[1,36,64,128]{3,2,0,1:T(8,128)S(1)} %get-tuple-element.137, ...), kind=kLoop, calls=%fused_computation.35 | loop fusion | flops 8257536 | bytes 28311552 | tf_op jit(solution)/shard_map/sub | solution.py:111
  86.7 11.7 %fusion.21 = f32[2,36,64,128]{3,2,0,1:T(8,128)S(1)} fusion(f32[4,36,66,128]{3,2,0,1:T(8,128)} %get-tuple-element.133, f32[4,36,66,128]{3,2,0,1:T(8,128)} %get-tuple-element.132, f32[4,36,68,130]{3,2,0,1:T(8,128)} %get-tuple-element.125, f32[4,36,68,130]{3,2,0,1:T(8,128)} %get-tuple-element.124, f32[36,64,128]{2,1,0:T(8,128)} %get-tuple-element.174, ...), kind=kLoop, calls=%fused_computation.60 | loop fusion | flops 6488064 | bytes 23592960 | tf_op jit(solution)/shard_map/add | solution.py:119
  98.4 4.8 %fusion.72 = (f32[1,36,64,128]{3,2,0,1:T(8,128)}, f32[1,36,64,128]{3,2,0,1:T(8,128)S(1)}) fusion(f32[4,36,64,128]{3,2,0,1:T(8,128)} %fusion.5, f32[2,36,64,128]{3,2,0,1:T(8,128)S(1)} %fusion.21, f32[4,36,64,128]{3,2,1,0:T(8,128)S(1)} %bitcast.404, f32[4,36,66,128]{3,2,0,1:T(8,128)} %get-tuple-element.133, f32[4,36,66,128]{3,2,0,1:T(8,128)} %get-tuple-element.132, ...), kind=kLoop, calls=%fused_computation.137 | loop fusion | flops 5603328 | bytes 23887872 | tf_op jit(solution)/shard_map/add | solution.py:121
  103.1 6.7 %fusion.64 = f32[1,36,64,128]{3,2,0,1:T(8,128)} fusion(f32[4,36,68,2]{3,2,0,1:T(8,128)S(1)} %copy-done.2, f32[4,36,2,128]{3,2,0,1:T(2,128)S(1)} %copy.167, f32[4,36,2,128]{3,2,0,1:T(2,128)S(1)} %copy.166, f32[1,36,64,128]{3,2,0,1:T(8,128)S(1)} %get-tuple-element.137, f32[1,36,64,128]{3,2,0,1:T(8,128)S(1)} %get-tuple-element.136, ...), kind=kLoop, calls=%fused_computation.121 | loop fusion | flops 9142272 | bytes 17990144 | tf_op jit(solution)/shard_map/sub | solution.py:126
  109.8 4.8 %fusion.69 = (f32[1,36,64,128]{3,2,0,1:T(8,128)S(1)}, f32[1,36,64,128]{3,2,0,1:T(8,128)S(1)}) fusion(f32[4,36,64,128]{3,2,0,1:T(8,128)} %fusion.5, f32[2,36,64,128]{3,2,0,1:T(8,128)S(1)} %fusion.21, f32[1,36,64,128]{3,2,0,1:T(8,128)S(1)} %get-tuple-element.115, f32[4,36,64,128]{3,2,1,0:T(8,128)S(1)} %bitcast.404, f32[4,36,66,128]{3,2,0,1:T(8,128)} %get-tuple-element.133, ...), kind=kLoop, calls=%fused_computation.129 | loop fusion | flops 5013504 | bytes 15335680 | tf_op jit(solution)/shard_map/sub | solution.py:124
  124.0 4.3 %collective-permute-start.4 = (f32[4,36,2,128]{3,0,2,1:T(4,128)S(1)}, f32[4,36,2,128]{3,0,2,1:T(4,128)S(1)}, u32[]{:S(2)}, u32[]{:S(2)}) collective-permute-start(f32[4,36,2,128]{3,0,2,1:T(4,128)S(1)} %copy.175), channel_id=1, source_target_pairs={{0,8},{8,16},{16,24},{1,9},{9,17},{17,25},{2,10},{10,18},{18,26},{... | collective-permute-start | bytes 442376 | tf_op jit(solution)/shard_map/ppermute | solution.py:32
  131.1 4.6 %collective-permute-done.5 = f32[4,36,2,128]{3,0,2,1:T(4,128)S(1)} collective-permute-done((f32[4,36,2,128]{3,0,2,1:T(4,128)S(1)}, f32[4,36,2,128]{3,0,2,1:T(4,128)S(1)}, u32[]{:S(2)}, u32[]{:S(2)}) %collective-permute-start.5) | collective-permute-done | bytes 147488 | tf_op jit(solution)/shard_map/ppermute | solution.py:35
  135.7 3.0 pad_maximum_fusion.4
  138.7 5.9 %fusion.681 = (f32[4,36,68,2]{3,2,0,1:T(8,128)}, f32[4,36,68,2]{3,2,0,1:T(8,128)}) fusion(f32[4,36,68,128]{3,2,0,1:T(8,128)S(1)} %pad_maximum_fusion.4), kind=kLoop, calls=%fused_computation.1300 | loop fusion | bytes 313344 | tf_op jit(solution)/shard_map/slice | solution.py:35
  144.6 3.5 copy.179
  148.2 2.8 collective-permute-start.6
  151.0 3.5 copy.181
  154.6 5.6 %multiply_subtract_fusion.2 = (f32[4,64,128]{2,1,0:T(8,128)}, f32[4,64,128]{2,1,0:T(8,128)}, f32[4,64,128]{2,1,0:T(8,128)}) fusion(f32[4,36,64,128]{3,2,0,1:T(8,128)} %copy-done.3, f32[64,128]{1,0:T(8,128)S(1)} %copy-done.33, f32[64,128]{1,0:T(8,128)S(1)} %copy-done.31, f32[64,128]{1,0:T(8,128)S(1)} %copy-done.20, f32[64,128]{1,0:T(8,128)S(1)} %get-tuple-element.141, ...), kind=kLoop, calls=%fused_computation.1098 | loop fusion | flops 13565952 | bytes 6258704 | tf_op jit(solution)/shard_map/sub | solution.py:160
  160.2 3.4 copy.180
  163.6 4.3 %copy.182 = f32[4,36,68,2]{3,2,0,1:T(8,128)} copy(f32[4,36,68,2]{2,0,3,1:T(4,128)} %collective-permute-done.7) | data formatting | bytes 156672 | tf_op jit(solution)/shard_map/ppermute | solution.py:32
  167.9 18.3 %pad_maximum_fusion.1 = (f32[4,36,68,130]{3,2,0,1:T(8,128)}, f32[4,36,68,130]{3,2,0,1:T(8,128)}) fusion(f32[4,36,68,2]{3,2,0,1:T(8,128)} %copy.180, f32[4,36,2,128]{3,2,0,1:T(2,128)S(1)} %copy.178, f32[4,36,64,128]{3,2,0,1:T(8,128)} %copy-done, f32[4,36,2,128]{3,2,0,1:T(2,128)S(1)} %copy.177, f32[4,36,68,2]{3,2,0,1:T(8,128)} %copy.182), kind=kLoop, calls=%fused_computation.12 | loop fusion | flops 7637760 | bytes 15353856 | tf_op jit(solution)/shard_map/concatenate | solution.py:36
  186.3 10.8 %fusion.2 = f32[4,36,64,128]{3,2,0,1:T(8,128)} fusion(f32[4,36,64,128]{3,2,0,1:T(8,128)S(1)} %bitcast.402, f32[4,36,2,128]{3,2,0,1:T(2,128)S(1)} %copy.177, f32[4,36,2,128]{3,2,0,1:T(2,128)S(1)} %copy.178, f32[4,36,68,130]{3,2,0,1:T(8,128)} %get-tuple-element.123, f32[4,36,68,130]{3,2,0,1:T(8,128)} %get-tuple-element.122), kind=kLoop, calls=%fused_computation.30 | loop fusion | flops 8257536 | bytes 19169280 | tf_op jit(solution)/shard_map/sub | solution.py:111
  197.1 9.3 %fusion.11 = f32[2,36,64,128]{3,2,0,1:T(8,128)} fusion(f32[4,36,64,128]{3,2,0,1:T(8,128)S(1)} %bitcast.402, f32[4,36,2,128]{3,2,0,1:T(2,128)S(1)} %copy.177, f32[4,36,2,128]{3,2,0,1:T(2,128)S(1)} %copy.178, f32[4,36,68,130]{3,2,0,1:T(8,128)} %get-tuple-element.123, f32[4,36,68,130]{3,2,0,1:T(8,128)} %get-tuple-element.122, f32[36,64,128]{2,1,0:T(8,128)S(1)} %copy-done.9, ...), kind=kLoop, calls=%fused_computation.47 | loop fusion | flops 8847360 | bytes 19169280 | tf_op jit(solution)/shard_map/add | solution.py:119
  206.5 4.6 %fusion.44 = f32[1,36,64,128]{3,2,0,1:T(8,128)S(1)} fusion(f32[4,36,68,2]{3,2,0,1:T(8,128)S(1)} %bitcast.410, f32[4,36,2,128]{3,2,0,1:T(2,128)S(1)} %copy.178, f32[4,36,64,128]{3,2,0,1:T(8,128)S(1)} %bitcast.402, f32[4,36,2,128]{3,2,0,1:T(2,128)S(1)} %copy.177, f32[4,36,68,2]{3,2,0,1:T(8,128)S(1)} %bitcast.408, f32[4,36,64,128]{3,2,0,1:T(8,128)} %fusion.2, ...), kind=kLoop, calls=%fused_computation.90 | loop fusion | flops 6782976 | bytes 20349440 | tf_op jit(solution)/shard_map/sub | solution.py:126
  219.2 3.0 multiply_subtract_fusion.1
  234.4 2.9 copy.186
  237.3 124.7 %all-reduce.3.cloned.1.call-done = f32[32,8192]{1,0:T(8,128)} async-done(((f32[32,8192]{1,0:T(8,128)}), f32[32,8192]{1,0:T(8,128)}) %all-reduce.3.cloned.1.call-update) | async-done | bytes 1048592
  (325 shorter events, 41.9 us)
Async XLA Ops:
  7.2 354.9 %all-reduce.3.cloned.1.call-start = ((), (), s32[]{:S(2)}) async-start(), calls=%async_computation | async-start | bytes 2097152
  10.3 7.7 %copy-start.83 = (s32[64,128]{1,0:T(8,128)S(1)}, s32[64,128]{1,0:T(8,128)}, u32[]{:S(2)}) copy-start(s32[64,128]{1,0:T(8,128)} %param.12) | copy-start | bytes 98308
  10.3 7.9 %copy-start.78 = (f32[36,64,128]{2,1,0:T(8,128)S(1)}, f32[36,64,128]{2,1,0:T(8,128)}, u32[]{:S(2)}) copy-start(f32[36,64,128]{2,1,0:T(8,128)} %param.11) | copy-start | bytes 3538948
  10.8 9.5 %copy-start.35 = (f32[2,36,64,128]{3,2,1,0:T(8,128)S(1)}, f32[2,36,64,128]{3,2,1,0:T(8,128)}, u32[]{:S(2)}) copy-start(f32[2,36,64,128]{3,2,1,0:T(8,128)} %param.10) | copy-start | bytes 7077892
  11.0 11.8 %collective-permute-start.1 = (f32[4,36,2,128]{3,0,2,1:T(4,128)S(1)}, f32[4,36,2,128]{3,0,2,1:T(4,128)S(1)}, u32[]{:S(2)}, u32[]{:S(2)}) collective-permute-start(f32[4,36,2,128]{3,0,2,1:T(4,128)S(1)} %copy.165), channel_id=1, source_target_pairs={{8,0},{16,8},{24,16},{9,1},{17,9},{25,17},{10,2},{18,10},{26,18},{... | collective-permute-start | bytes 442376 | tf_op jit(solution)/shard_map/ppermute | solution.py:35
  12.5 10.4 %collective-permute-start = (f32[4,36,2,128]{3,0,2,1:T(4,128)S(1)}, f32[4,36,2,128]{3,0,2,1:T(4,128)S(1)}, u32[]{:S(2)}, u32[]{:S(2)}) collective-permute-start(f32[4,36,2,128]{3,0,2,1:T(4,128)S(1)} %copy.164), channel_id=1, source_target_pairs={{0,8},{8,16},{16,24},{1,9},{9,17},{17,25},{2,10},{10,18},{18,26},{... | collective-permute-start | bytes 442376 | tf_op jit(solution)/shard_map/ppermute | solution.py:32
  34.7 13.3 %collective-permute-start.2 = (f32[4,36,68,2]{2,0,3,1:T(4,128)S(1)}, f32[4,36,68,2]{2,0,3,1:T(4,128)S(1)}, u32[]{:S(2)}, u32[]{:S(2)}) collective-permute-start(f32[4,36,68,2]{2,0,3,1:T(4,128)S(1)} %copy.168), channel_id=1, source_target_pairs={{1,0},{2,1},{3,2},{4,3},{5,4},{6,5},{7,6},{0,7},{9,8},{10,9},{11,1... | collective-permute-start | bytes 235016 | tf_op jit(solution)/shard_map/ppermute | solution.py:35
  41.3 10.0 %collective-permute-start.3 = (f32[4,36,68,2]{2,0,3,1:T(4,128)S(1)}, f32[4,36,68,2]{2,0,3,1:T(4,128)S(1)}, u32[]{:S(2)}, u32[]{:S(2)}) collective-permute-start(f32[4,36,68,2]{2,0,3,1:T(4,128)S(1)} %copy.170), channel_id=1, source_target_pairs={{0,1},{1,2},{2,3},{3,4},{4,5},{5,6},{6,7},{7,0},{8,9},{9,10},{10,1... | collective-permute-start | bytes 235016 | tf_op jit(solution)/shard_map/ppermute | solution.py:32
  51.4 21.2 %slice-start.2 = ((s8[4718592]{0:T(1024)(128)(4,1)}), s8[524288]{0:T(1024)(128)(4,1)S(1)}, s32[]{:S(2)}) async-start(s8[4718592]{0:T(1024)(128)(4,1)} %bitcast.403), calls=%async_computation.3 | async-start | bytes 1048576
  54.8 17.8 %slice-start.3 = ((s8[4718592]{0:T(1024)(128)(4,1)}), s8[4194304]{0:T(1024)(128)(4,1)S(1)}, s32[]{:S(2)}) async-start(s8[4718592]{0:T(1024)(128)(4,1)} %bitcast.403), calls=%async_computation.4 | async-start | bytes 8388608
  54.8 43.6 %slice-start.4 = ((s8[5308416]{0:T(1024)(128)(4,1)}), s8[4194304]{0:T(1024)(128)(4,1)S(1)}, s32[]{:S(2)}) async-start(s8[5308416]{0:T(1024)(128)(4,1)} %bitcast.405), calls=%async_computation.5 | async-start | bytes 8388608
  72.6 14.1 %copy-start.7 = (f32[36,64,128]{2,1,0:T(8,128)S(1)}, f32[36,64,128]{2,1,0:T(8,128)}, u32[]{:S(2)}) copy-start(f32[36,64,128]{2,1,0:T(8,128)} %get-tuple-element.173) | copy-start | bytes 3538948
  72.6 25.7 %slice-start.5 = ((s8[5308416]{0:T(1024)(128)(4,1)}), s8[1114112]{0:T(1024)(128)(4,1)S(1)}, s32[]{:S(2)}) async-start(s8[5308416]{0:T(1024)(128)(4,1)} %bitcast.405), calls=%async_computation.6 | async-start | bytes 2228224
  86.7 11.7 %copy-start.2 = (f32[4,36,68,2]{3,2,0,1:T(8,128)S(1)}, f32[4,36,68,2]{3,2,0,1:T(8,128)}, u32[]{:S(2)}) copy-start(f32[4,36,68,2]{3,2,0,1:T(8,128)} %copy.171) | copy-start | bytes 235012
  109.8 4.8 %copy-start.5 = (f32[36,64,128]{2,1,0:T(8,128)S(1)}, f32[36,64,128]{2,1,0:T(8,128)}, u32[]{:S(2)}) copy-start(f32[36,64,128]{2,1,0:T(8,128)} %copy-done.4) | copy-start | bytes 3538948
  109.8 4.8 %copy-start.17 = (f32[1,36,64,128]{3,2,0,1:T(8,128)S(1)}, f32[1,36,64,128]{3,2,0,1:T(8,128)}, u32[]{:S(2)}) copy-start(f32[1,36,64,128]{3,2,0,1:T(8,128)} %get-tuple-element.114) | copy-start | bytes 3538948
  109.8 4.8 %copy-start.18 = (f32[1,36,64,128]{3,2,0,1:T(8,128)S(1)}, f32[1,36,64,128]{3,2,0,1:T(8,128)}, u32[]{:S(2)}) copy-start(f32[1,36,64,128]{3,2,0,1:T(8,128)} %fusion.64) | copy-start | bytes 3538948
  115.6 5.8 %copy-start.3 = (f32[4,36,64,128]{3,2,0,1:T(8,128)}, f32[4,36,64,128]{3,2,0,1:T(8,128)S(1)}, u32[]{:S(2)}) copy-start(f32[4,36,64,128]{3,2,0,1:T(8,128)S(1)} %maximum_multiply_fusion) | copy-start | bytes 14155780
  120.5 9.8 %copy-start.85 = (s32[32]{0:T(128)S(1)}, s32[32]{0:T(128)}, u32[]{:S(2)}) copy-start(s32[32]{0:T(128)} %param.15) | copy-start | bytes 388
  124.0 7.0 %collective-permute-start.4 = (f32[4,36,2,128]{3,0,2,1:T(4,128)S(1)}, f32[4,36,2,128]{3,0,2,1:T(4,128)S(1)}, u32[]{:S(2)}, u32[]{:S(2)}) collective-permute-start(f32[4,36,2,128]{3,0,2,1:T(4,128)S(1)} %copy.175), channel_id=1, source_target_pairs={{0,8},{8,16},{16,24},{1,9},{9,17},{17,25},{2,10},{10,18},{18,26},{... | collective-permute-start | bytes 442376 | tf_op jit(solution)/shard_map/ppermute | solution.py:32
  128.4 7.3 %collective-permute-start.5 = (f32[4,36,2,128]{3,0,2,1:T(4,128)S(1)}, f32[4,36,2,128]{3,0,2,1:T(4,128)S(1)}, u32[]{:S(2)}, u32[]{:S(2)}) collective-permute-start(f32[4,36,2,128]{3,0,2,1:T(4,128)S(1)} %copy.176), channel_id=1, source_target_pairs={{8,0},{16,8},{24,16},{9,1},{17,9},{25,17},{10,2},{18,10},{26,18},{... | collective-permute-start | bytes 442376 | tf_op jit(solution)/shard_map/ppermute | solution.py:35
  148.2 12.0 %collective-permute-start.6 = (f32[4,36,68,2]{2,0,3,1:T(4,128)S(1)}, f32[4,36,68,2]{2,0,3,1:T(4,128)S(1)}, u32[]{:S(2)}, u32[]{:S(2)}) collective-permute-start(f32[4,36,68,2]{2,0,3,1:T(4,128)S(1)} %copy.179), channel_id=1, source_target_pairs={{1,0},{2,1},{3,2},{4,3},{5,4},{6,5},{7,6},{0,7},{9,8},{10,9},{11,1... | collective-permute-start | bytes 235016 | tf_op jit(solution)/shard_map/ppermute | solution.py:35
  154.6 9.0 %collective-permute-start.7 = (f32[4,36,68,2]{2,0,3,1:T(4,128)S(1)}, f32[4,36,68,2]{2,0,3,1:T(4,128)}, u32[]{:S(2)}, u32[]{:S(2)}) collective-permute-start(f32[4,36,68,2]{2,0,3,1:T(4,128)S(1)} %copy.181), channel_id=1, source_target_pairs={{0,1},{1,2},{2,3},{3,4},{4,5},{5,6},{6,7},{7,0},{8,9},{9,10},{10,1... | collective-permute-start | bytes 235016 | tf_op jit(solution)/shard_map/ppermute | solution.py:32
  163.6 22.6 %slice-start = ((s8[4718592]{0:T(1024)(128)(4,1)}), s8[524288]{0:T(1024)(128)(4,1)S(1)}, s32[]{:S(2)}) async-start(s8[4718592]{0:T(1024)(128)(4,1)} %bitcast.401), calls=%async_computation.1 | async-start | bytes 1048576
  167.9 18.4 %slice-start.1 = ((s8[4718592]{0:T(1024)(128)(4,1)}), s8[4194304]{0:T(1024)(128)(4,1)S(1)}, s32[]{:S(2)}) async-start(s8[4718592]{0:T(1024)(128)(4,1)} %bitcast.401), calls=%async_computation.2 | async-start | bytes 8388608
  186.2 10.8 %copy-start.8 = (f32[36,64,128]{2,1,0:T(8,128)S(1)}, f32[36,64,128]{2,1,0:T(8,128)}, u32[]{:S(2)}) copy-start(f32[36,64,128]{2,1,0:T(8,128)} %get-tuple-element.173) | copy-start | bytes 3538948
  186.2 10.8 %copy-start.9 = (f32[36,64,128]{2,1,0:T(8,128)S(1)}, f32[36,64,128]{2,1,0:T(8,128)}, u32[]{:S(2)}) copy-start(f32[36,64,128]{2,1,0:T(8,128)} %get-tuple-element.174) | copy-start | bytes 3538948
  186.3 20.2 %slice-start.6 = ((s8[5308416]{0:T(1024)(128)(4,1)}), s8[1114112]{0:T(1024)(128)(4,1)S(1)}, s32[]{:S(2)}) async-start(s8[5308416]{0:T(1024)(128)(4,1)} %bitcast.407), calls=%async_computation.7 | async-start | bytes 2228224
  186.3 20.2 %slice-start.8 = ((s8[5308416]{0:T(1024)(128)(4,1)}), s8[4194304]{0:T(1024)(128)(4,1)S(1)}, s32[]{:S(2)}) async-start(s8[5308416]{0:T(1024)(128)(4,1)} %bitcast.409), calls=%async_computation.9 | async-start | bytes 8388608
  197.1 9.4 %slice-start.7 = ((s8[5308416]{0:T(1024)(128)(4,1)}), s8[4194304]{0:T(1024)(128)(4,1)S(1)}, s32[]{:S(2)}) async-start(s8[5308416]{0:T(1024)(128)(4,1)} %bitcast.407), calls=%async_computation.8 | async-start | bytes 8388608
  197.1 9.4 %slice-start.9 = ((s8[5308416]{0:T(1024)(128)(4,1)}), s8[1114112]{0:T(1024)(128)(4,1)S(1)}, s32[]{:S(2)}) async-start(s8[5308416]{0:T(1024)(128)(4,1)} %bitcast.409), calls=%async_computation.10 | async-start | bytes 2228224
  197.1 14.0 %slice-start.10 = ((s8[4718592]{0:T(1024)(128)(4,1)}), s8[524288]{0:T(1024)(128)(4,1)S(1)}, s32[]{:S(2)}) async-start(s8[4718592]{0:T(1024)(128)(4,1)} %bitcast.411), calls=%async_computation.11 | async-start | bytes 1048576
  (75 other events, 110.5 us)
Sparse Core Ops, SparseCore 0:
  231.8 130.1 all-reduce.2
where the time goes:
time: 375 us; the launch traced here: 371 us
  other arithmetic  151 us (40%)
  waiting for transfers between devices  129 us (34%)
  local copies, waits for them, and re-layouts  51.1 us (14%)
  starting transfers between devices  19 us (5%)
  between operations  18 us (5%)
    unnamed x2, waiting for transfers between devices  125 us
    concatenate x5, other arithmetic, padded_2(): block = jnp.concatenate([low, block, high], axis=dim)  47.6 us
    sub x2, other arithmetic, explicit(): spread = east_one + west_one + north_one + south_one - 4.0 * centre  24.8 us
    add x2, other arithmetic, explicit(): background_flow[0][None] * grad_x + background_flow[1][None] * grad_y  21 us
    slice x8, local copies, waits for them, and re-layouts, padded_2(): lax.slice_in_dim(block, 0, width, axis=dim)  19.2 us
    sub x2, other arithmetic, explicit(): centre[2] + VISCOUS_COEF * spread[2] + coriolis * centre[3]  11.3 us
    ppermute x4, starting transfers between devices, padded_2(): lax.ppermute(lax.slice_in_dim(block, block.shape[dim] - width, None, axis...  10.4 us
    unnamed x232, local copies, waits for them, and re-layouts  9.77 us
  transfers between devices with their start and end apart: 9, of which 2 were waited for; matrix products, arithmetic and copies ran while one was open for 10% of the time, Pallas kernels for 0%

commit v1 on v0

v1 whole, which is shorter than its diff:
```python
import functools
import math

import jax
import jax.numpy as jnp
from jax import lax
from jax.experimental import pallas as pl
from jax.experimental.pallas import tpu as pltpu
from jax.sharding import PartitionSpec as P

KY = 128
KX = 128
NFACE = 4

ADVECT_COEF = 0.3
DIFFUSE_COEF = 0.12
VISCOUS_COEF = 0.1
THERMAL_COEF = 0.4
HALINE_COEF = 0.3
PRESSURE_COEF = 0.4
SALINE_WEIGHT = 0.8
CORIOLIS_PEAK = 0.5
MOMENTUM_RATIO = 1.5

TILE = 8
LANES = 128
VMEM = pl.BlockSpec(memory_space=pltpu.VMEM)
SMEM = pl.BlockSpec(memory_space=pltpu.SMEM)
LIMIT = 56 << 20
F32 = jnp.float32
PREP_ROWS, PREP_UNROLL = 64, 6
FACTOR_ROWS, FACTOR_UNROLL = 64, 2
STEP_ROWS, UP_UNROLL, DOWN_UNROLL = 64, 4, 6


def shape(*dims):
    return jax.ShapeDtypeStruct(dims, F32)


def lanes_of(rows):
    return lax.broadcasted_iota(jnp.int32, (rows, LANES), 1)


def rows_of(rows):
    return lax.broadcasted_iota(jnp.int32, (rows, LANES), 0)


def loop(count, load, body, init, unroll):
    while count % unroll:
        unroll -= 1

    def several(i, carry):
        steps = [i * unroll + j for j in range(unroll)]
        loaded = [load(step) for step in steps]
        stores = []
        for step, values in zip(steps, loaded):
            carry, store = body(step, values, carry)
            stores.append(store)
        for store in stores:
            store()
        return carry

    return lax.fori_loop(0, count // unroll, several, init)


def turn_scalars(code):
    cosine = jnp.where(code == 0, 1.0, jnp.where(code == 2, -1.0, 0.0)).astype(F32)
    sine = jnp.where(code == 1, 1.0, jnp.where(code == 3, -1.0, 0.0)).astype(F32)
    return cosine, sine


def pack_columns(acc, k, fields, lane):
    at = 3 * k
    first, second, third = lane >= at, lane >= at + 1, lane >= at + 2
    east, west = [], []
    for g in range(2):
        tracer, flow = fields[g], fields[g + 2]
        rolled = pltpu.roll(tracer, at + 2, 1)
        east.append(jnp.where(first, jnp.where(third, pltpu.roll(flow, at + 3, 1), rolled), acc[g]))
        west.append(jnp.where(second, jnp.where(third, rolled, pltpu.roll(flow, at + 1, 1)), acc[g + 2]))
    return tuple(east + west)


def store_edge_rows(k, fields, block, last, south_ref, north_ref):
    size = fields[0].shape[0]
    for c in range(4):
        if block == 0:
            south_ref[k, 2 * c : 2 * c + 2, :] = fields[c][0:2, :]
        if block == last:
            north_ref[k, 2 * c : 2 * c + 2, :] = fields[c][size - 2 : size, :]


def prep_kernel(rot_ref, adj_ref, uv_ref, south_ref, north_ref, east_ref, west_ref):
    levels, height = adj_ref.shape[1], adj_ref.shape[2]
    cosine, sine = turn_scalars(rot_ref[0, 0])
    size = PREP_ROWS
    lane = lanes_of(size)
    blocks = height // size
    for block in range(blocks):
        rows = pl.ds(block * size, size)

        def load(k, rows=rows):
            return [adj_ref[c, k, rows, :] for c in range(4)]

        def level(k, loaded, acc, rows=rows, block=block):
            t, s, a, b = loaded
            u = cosine * a - sine * b
            v = sine * a + cosine * b
            fields = (t, s, u, v)

            def store():
                uv_ref[0, k, rows, :] = u
                uv_ref[1, k, rows, :] = v
                store_edge_rows(k, fields, block, blocks - 1, south_ref, north_ref)

            return pack_columns(acc, k, fields, lane), store

        zero = jnp.zeros((size, LANES), F32)
        acc = loop(levels, load, level, (zero,) * 4, PREP_UNROLL)
        for g in range(2):
            east_ref[g, rows, :] = acc[g]
            west_ref[g, rows, :] = acc[g + 2]


def factor_kernel(vd_ref, wet_ref, w1_ref, w2_ref, h1_ref, h2_ref, g1_ref, g2_ref):
    levels, height = vd_ref.shape[0], vd_ref.shape[1]
    out = ((w1_ref, h1_ref, g1_ref, 1.0), (w2_ref, h2_ref, g2_ref, MOMENTUM_RATIO))
    size = FACTOR_ROWS
    for block in range(height // size):
        rows = pl.ds(block * size, size)
        wet = wet_ref[rows, :]
        zero = jnp.zeros((size, LANES), F32)

        def load(i, rows=rows):
            return vd_ref[jnp.maximum(levels - 2 - i, 0), rows, :]

        def level(i, loaded, carry, rows=rows, wet=wet):
            k = levels - 1 - i
            below, inverses = carry
            mask = jnp.where(k < wet, 1.0, 0.0).astype(F32)
            above = jnp.where(k > 0, loaded * mask, 0.0)
            kept, stores = [], []
            for (w_ref, h_ref, g_ref, factor), inverse in zip(out, inverses):
                low, high = factor * below, factor * above
                pivot = 1.0 + high + low - low * (low * inverse)
                inverse = 1.0 / pivot
                masked = inverse * mask
                stores += [(w_ref, masked), (h_ref, low * masked), (g_ref, high * masked)]
                kept.append(inverse)

            def store():
                for ref, value in stores:
                    ref[k, rows, :] = value

            return (above, tuple(kept)), store

        loop(levels, load, level, (zero, (zero, zero)), FACTOR_UNROLL)


def step_kernel(final, *refs):
    refs = list(refs)
    rot_ref = refs.pop(0) if final else None
    ts_ref, uv_ref, flow_ref, w1_ref, w2_ref, h1_ref, h2_ref, g1_ref, g2_ref, cor_ref = refs[:10]
    south_ref, north_ref, east_ref, west_ref = refs[10:14]
    if final:
        out_ref, surface_ref, value_ref = refs[14:]
    else:
        ts_out, uv_out, surface_ref, south_out, north_out, east_out, west_out, value_ref = refs[14:]
    levels, height = ts_ref.shape[1], ts_ref.shape[2]
    size = STEP_ROWS
    blocks = height // size
    lane, row = lanes_of(size), rows_of(size)
    low_two, high_two = lane < 2, lane >= LANES - 2
    low_one, high_one = lane < 1, lane >= LANES - 1
    zero = jnp.zeros((size, LANES), F32)
    if final:
        cosine, sine = turn_scalars(rot_ref[0, 0])

    def get(c, k, start):
        rows = pl.ds(start, TILE)
        return ts_ref[c, k, rows, :] if c < 2 else uv_ref[c - 2, k, rows, :]

    def line(c, k, start, halos):
        if 0 <= start <= height - TILE:
            return get(c, k, start)
        south, north = halos
        part = rows_of(TILE)
        if start < 0:
            halo = pltpu.roll(south, (-2 * c - 2 - start) % TILE, 0)
            return jnp.where(part < -start, halo, pltpu.roll(get(c, k, 0), -start, 0))
        over = start + TILE - height
        halo = pltpu.roll(north, (TILE - over - 2 * c) % TILE, 0)
        return jnp.where(part >= TILE - over, halo, pltpu.roll(get(c, k, height - TILE), TILE - over, 0))

    for block in range(blocks):
        rows = pl.ds(block * size, size)
        first_row = block * size
        cor = cor_ref[rows, :]

        def fetch(c, k, shift, halos, first_row=first_row):
            start = first_row + shift
            if 0 <= start <= height - size:
                part = pl.ds(start, size)
                return ts_ref[c, k, part, :] if c < 2 else uv_ref[c - 2, k, part, :]
            lines = [line(c, k, start + i, halos) for i in range(0, size, TILE)]
            return lines[0] if len(lines) == 1 else jnp.concatenate(lines, axis=0)

        def load_up(i, rows=rows, block=block, fetch=fetch):
            k = levels - 1 - i
            halos = (south_ref[k] if block == 0 else None, north_ref[k] if block == blocks - 1 else None)
            turn = LANES - 2 - 3 * k
            east = [pltpu.roll(east_ref[g, rows, :], turn, 1) for g in range(2)]
            west = [pltpu.roll(west_ref[g, rows, :], turn, 1) for g in range(2)]
            lines = [{s: fetch(c, k, s, halos) for s in ((0, 1, -1, 2, -2) if c < 2 else (0, 1, -1))} for c in range(4)]
            flow = [flow_ref[i, k, rows, :] for i in range(2)]
            factors = [ref[k, rows, :] for ref in (w1_ref, w2_ref, h1_ref, h2_ref)]
            return east, west, lines, flow, factors

        def upward(i, loaded, below, cor=cor):
            k = levels - 1 - i
            east, west, lines, flow, factors = loaded
            flow_x = flow[0] * (ADVECT_COEF / 12.0)
            flow_y = flow[1] * (ADVECT_COEF / 12.0)
            rhs, diff_x, diff_y = [], [], []
            for c in range(2):
                mid = lines[c][0]
                e1 = pltpu.roll(jnp.where(low_one, east[c], mid), LANES - 1, 1)
                w1 = pltpu.roll(jnp.where(high_one, west[c], mid), 1, 1)
                e2 = pltpu.roll(jnp.where(low_two, east[c], mid), LANES - 2, 1)
                w2 = pltpu.roll(jnp.where(high_two, west[c], mid), 2, 1)
                n1, s1, n2, s2 = (lines[c][s] for s in (1, -1, 2, -2))
                dx, dy = e1 - w1, n1 - s1
                grad = flow_x * (8.0 * dx - (e2 - w2)) + flow_y * (8.0 * dy - (n2 - s2))
                near = (e1 + w1) + (n1 + s1)
                rhs.append((1.0 - 4.0 * DIFFUSE_COEF) * mid + DIFFUSE_COEF * near + grad)
                diff_x.append(dx)
                diff_y.append(dy)
            push = [
                (0.5 * PRESSURE_COEF) * (d[0] - SALINE_WEIGHT * d[1]) for d in (diff_x, diff_y)
            ]
            sides = []
            for c in range(2, 4):
                mid = lines[c][0]
                e1 = jnp.where(high_one, east[c - 2], pltpu.roll(mid, LANES - 1, 1))
                w1 = jnp.where(low_one, west[c - 2], pltpu.roll(mid, 1, 1))
                n1, s1 = lines[c][1], lines[c][-1]
                near = (e1 + w1) + (n1 + s1)
                sides.append(e1 - w1 if c == 2 else n1 - s1)
                rhs.append((1.0 - 4.0 * VISCOUS_COEF) * mid + VISCOUS_COEF * near - push[c - 2])
            spread = sides[0] + sides[1]
            rhs[0] = rhs[0] + (0.5 * THERMAL_COEF) * spread
            rhs[1] = rhs[1] - (0.5 * HALINE_COEF) * spread
            rhs[2] = rhs[2] + cor * lines[3][0]
            rhs[3] = rhs[3] - cor * lines[2][0]
            values = tuple(
                factors[c // 2] * rhs[c] + factors[2 + c // 2] * below[c] for c in range(4)
            )

            def store():
                for c in range(4):
                    value_ref[c, k] = values[c]

            return values, store

        top = loop(levels, load_up, upward, (zero,) * 4, UP_UNROLL)
        for c in range(2):
            surface_ref[c, rows, :] = top[c]

        def load_down(k, rows=rows):
            return [value_ref[c, k] for c in range(4)], (g1_ref[k, rows, :], g2_ref[k, rows, :])

        def downward(k, loaded, carry, rows=rows, block=block):
            above, acc = carry
            values, gains = loaded
            fields = tuple(values[c] + gains[c // 2] * above[c] for c in range(4))

            def store():
                if final:
                    u, v = fields[2], fields[3]
                    out_ref[0, k, rows, :] = fields[0]
                    out_ref[1, k, rows, :] = fields[1]
                    out_ref[2, k, rows, :] = cosine * u + sine * v
                    out_ref[3, k, rows, :] = cosine * v - sine * u
                    return
                for c in range(2):
                    ts_out[c, k, rows, :] = fields[c]
                    uv_out[c, k, rows, :] = fields[c + 2]
                store_edge_rows(k, fields, block, blocks - 1, south_out, north_out)

            return (fields, acc if final else pack_columns(acc, k, fields, lane)), store

        acc = () if final else (zero,) * 4
        _, acc = loop(levels, load_down, downward, ((zero,) * 4, acc), DOWN_UNROLL)
        if not final:
            for g in range(2):
                east_out[g, rows, :] = acc[g]
                west_out[g, rows, :] = acc[g + 2]


HIGHEST = lax.Precision.HIGHEST


def transform(parts, row_table_ref, col_table_ref, norm):
    height = parts[0].shape[1]
    out = []
    for c in range(2):
        total = None
        for i, part in enumerate(parts):
            table = row_table_ref[i * height : (i + 1) * height, :]
            piece = lax.dot_general(table, part[c], (((0,), (0,)), ((), ())), precision=HIGHEST, preferred_element_type=F32)
            total = piece if total is None else total + piece
        out.append(norm * jnp.dot(total, col_table_ref[...], precision=HIGHEST, preferred_element_type=F32))
    return out


def first_transform_kernel(norm, *refs):
    *parts, row_table_ref, col_table_ref, out_ref = refs
    for c, block in enumerate(transform(parts, row_table_ref, col_table_ref, norm)):
        out_ref[c * KY : (c + 1) * KY, :] = block


def second_transform_kernel(norm, count, slot_ref, valid_ref, *refs):
    refs, sends, table = refs[: -count - 1], refs[-count - 1 : -1], refs[-1]
    *parts, row_table_ref, col_table_ref, early_ref = refs
    table[0 : 2 * KY, :] = early_ref[...]
    for c, block in enumerate(transform(parts, row_table_ref, col_table_ref, norm)):
        table[(2 + c) * KY : (3 + c) * KY, :] = block
    for i, send in enumerate(sends):
        size = send.shape[0]
        start = pl.multiple_of(slot_ref[i] * size, TILE)
        mine = jnp.full((size, LANES), valid_ref[i], jnp.int32) > 0
        send[...] = jnp.where(mine, table[pl.ds(start, size), :], 0.0)


def call(kernel, outs, in_specs, scratch=()):
    many = isinstance(outs, (list, tuple))
    return pl.pallas_call(
        kernel,
        out_shape=outs,
        in_specs=in_specs,
        out_specs=[VMEM] * len(outs) if many else VMEM,
        scratch_shapes=list(scratch),
        compiler_params=pltpu.CompilerParams(vmem_limit_bytes=LIMIT),
    )


def exchange(south, north, east, west):
    ty, tx = lax.axis_size("ty"), lax.axis_size("tx")
    up = [(i, i + 1) for i in range(ty - 1)]
    down = [(i + 1, i) for i in range(ty - 1)]
    right = [(i, (i + 1) % tx) for i in range(tx)]
    left = [((i + 1) % tx, i) for i in range(tx)]
    return (
        lax.ppermute(north, "ty", up),
        lax.ppermute(south, "ty", down),
        lax.ppermute(west, "tx", left),
        lax.ppermute(east, "tx", right),
    )


def gather_rows(block):
    ty = lax.axis_size("ty")
    return [block] + [
        lax.ppermute(block, "ty", [(i, (i + s) % ty) for i in range(ty)]) for s in range(1, ty)
    ]


def cosine_table(rows, row_total, mode_count):
    modes = jnp.arange(mode_count, dtype=jnp.int32)
    phase_index = (2 * rows[:, None] + 1) * modes[None, :] % (4 * row_total)
    return jnp.cos(phase_index.astype(F32) * (math.pi / (2 * row_total)))


def body(adjoint, background_flow, vert_diff, wet_levels, rotation, face_map, ctrl_owner):
    _, levels, height, width = adjoint.shape
    ty, tx = lax.axis_size("ty"), lax.axis_size("tx")
    here_y, here_x = lax.axis_index("ty"), lax.axis_index("tx")
    rows_total, cols_total = height * ty, width * tx
    full = shape(levels, height, width)
    pair = shape(2, levels, height, width)
    edge_rows = [shape(levels, TILE, width)] * 2
    edge_cols = [shape(2, height, LANES)] * 2

    uv, *edges = call(prep_kernel, [pair] + edge_rows + edge_cols, [SMEM, VMEM])(rotation, adjoint)
    halos = exchange(*edges)
    factors = call(factor_kernel, [full] * 6, [VMEM] * 2)(vert_diff, wet_levels)

    rows = (here_y * height + jnp.arange(height, dtype=jnp.int32)).astype(F32)
    coriolis = CORIOLIS_PEAK * jnp.sin(math.pi * (rows + 0.5) / rows_total - 0.5 * math.pi)
    coriolis = jnp.broadcast_to(coriolis[:, None], (height, width))
    origin = (here_y - jnp.arange(ty, dtype=jnp.int32)) % ty
    source_rows = (origin[:, None] * height + jnp.arange(height, dtype=jnp.int32)[None, :]).reshape(-1)
    row_table = cosine_table(source_rows, rows_total, KY)
    col_table = cosine_table(here_x * width + jnp.arange(width, dtype=jnp.int32), cols_total, KX)
    norm = math.sqrt(2.0 * NFACE / (rows_total * cols_total))
    per_face = ctrl_owner.shape[0] // NFACE
    targets = here_y * tx + (here_x + jnp.arange(tx, dtype=jnp.int32)) % tx
    numbers = jnp.arange(ctrl_owner.shape[0], dtype=jnp.int32)
    owned = jnp.sum(jnp.where(ctrl_owner[None, :] == targets[:, None], numbers[None, :], 0), axis=1)
    slots = owned % per_face
    valid = (owned // per_face == face_map[0, 0]).astype(jnp.int32)

    scratch = [pltpu.VMEM((4, levels, STEP_ROWS, width), F32)]
    surface = shape(2, height, width)
    ts, uv, first, *edges = call(
        functools.partial(step_kernel, False),
        [pair, pair, surface] + edge_rows + edge_cols,
        [VMEM] * 14,
        scratch,
    )(adjoint, uv, background_flow, *factors, coriolis, *halos)
    halos = exchange(*edges)
    first_parts = gather_rows(first)
    early = call(
        functools.partial(first_transform_kernel, norm), shape(2 * KY, KX), [VMEM] * (ty + 2)
    )(*first_parts, row_table, col_table)
    adjoint_out, second = call(
        functools.partial(step_kernel, True),
        [shape(*adjoint.shape), surface],
        [SMEM] + [VMEM] * 14,
        scratch,
    )(rotation, ts, uv, background_flow, *factors, coriolis, *halos)
    second_parts = gather_rows(second)
    size = 4 * KY // per_face
    sends = call(
        functools.partial(second_transform_kernel, norm, tx),
        [shape(size, KX)] * tx,
        [SMEM] * 2 + [VMEM] * (ty + 3),
        [pltpu.VMEM((4 * KY, KX), F32)],
    )(slots, valid, *second_parts, row_table, col_table, early)
    total = sends[0]
    for s in range(1, tx):
        total = total + lax.ppermute(sends[s], "tx", [(i, (i + s) % tx) for i in range(tx)])
    return adjoint_out, total.reshape(1, -1)


def solution(mesh):
    return jax.shard_map(
        body,
        mesh=mesh,
        in_specs=(
            P(None, None, "ty", "tx"),
            P(None, None, "ty", "tx"),
            P(None, "ty", "tx"),
            P("ty", "tx"),
            P("ty", "tx"),
            P("ty", "tx"),
            P(),
        ),
        out_specs=(P(None, None, "ty", "tx"), P(("ty", "tx"), None)),
        check_vma=False,
    )
```

time: 375 us -> 101 us (0.27)
  other arithmetic: 151 us -> 4.98 us
  waiting for transfers between devices: 129 us -> 4.96 us
  Pallas kernels: 0 us -> 49.6 us
  local copies, waits for them, and re-layouts: 51.1 us -> 4.02 us
  starting transfers between devices: 19 us -> 34.9 us
  between operations: 18 us -> 2.14 us
    unnamed x2 -> x0, waiting for transfers between devices: 125 us -> none
    sub x9 -> x0, other arithmetic: 53.6 us -> none  [the longest x2 24.8 us: explicit(): spread = east_one + west_one + north_one + south_one - 4.0 * centre]
    pallas_call x0 -> x6, Pallas kernels: none -> 49.6 us  [the longest x1 17.2 us: body(): call(functools.partial(step_kernel, False), [pair, pair, surface] + edge_...]
    concatenate x5 -> x0, other arithmetic: 47.6 us -> none  [padded_2(): block = jnp.concatenate([low, block, high], axis=dim)]
    add x5 -> x2, other arithmetic: 29.8 us -> 1.4 us  [the longest x1 1.39 us: body(): total + lax.ppermute(sends[s], 'tx', [(i, (i + s) % tx) for i in range(tx)])]
    slice x13 -> x0, local copies, waits for them, and re-layouts: 26.5 us -> none  [the longest x8 19.2 us: padded_2(): lax.slice_in_dim(block, 0, width, axis=dim)]
    ppermute x8 -> x21, starting transfers between devices: 19 us -> 34.9 us  [the longest x6 11.9 us: gather_rows(): lax.ppermute(block, 'ty', [(i, (i + s) % ty) for i in range(ty)])]
    ppermute x8 -> x0, local copies, waits for them, and re-layouts: 14.7 us -> none  [the longest x4 7.82 us: padded_2(): lax.ppermute(lax.slice_in_dim(block, block.shape[dim] - width, None, axis...]
  transfers between devices with their start and end apart: 9 -> 21, of which waited for: 2 -> 4; matrix products, arithmetic and copies ran while one was open for 10% -> 4% of each run, Pallas kernels for 0% -> 23%
where the time goes in v1:
time: 101 us
  Pallas kernels  49.6 us (49%)
  starting transfers between devices  34.9 us (35%)
  other arithmetic  4.98 us (5%)
  waiting for transfers between devices  4.96 us (5%)
  local copies, waits for them, and re-layouts  4.02 us (4%)
  between operations  2.14 us (2%)
    pallas_call x1, Pallas kernels, body(): call(functools.partial(step_kernel, False), [pair, pair, surface] + edge_...  17.2 us
    pallas_call x1, Pallas kernels, body(): call(functools.partial(step_kernel, True), [shape(*adjoint.shape), surfac...  14.6 us
    ppermute x6, starting transfers between devices, gather_rows(): lax.ppermute(block, 'ty', [(i, (i + s) % ty) for i in range(ty)])  11.9 us
    ppermute x2, starting transfers between devices, exchange(): lax.ppermute(north, 'ty', up)  9.1 us
    ppermute x2, starting transfers between devices, exchange(): lax.ppermute(west, 'tx', left)  6.13 us
    pallas_call x1, Pallas kernels, body(): call(prep_kernel, [pair] + edge_rows + edge_cols, [SMEM, VMEM])  6.03 us
    pallas_call x1, Pallas kernels, body(): factors = call(factor_kernel, [full] * 6, [VMEM] * 2)(vert_diff, wet_levels)  5.37 us
    ppermute x7, starting transfers between devices, body(): lax.ppermute(sends[s], 'tx', [(i, (i + s) % tx) for i in range(tx)])  5.24 us
  transfers between devices with their start and end apart: 21, of which 4 were waited for; matrix products, arithmetic and copies ran while one was open for 4% of the time, Pallas kernels for 23%

profile of v1, /device:TPU:0, one launch (start us, length us, event | category | flops | bytes accessed | tf_op | source)
XLA Modules:
  0.0 100.7 jit_solution(8747453849754674695)
XLA Ops:
  1.3 6.0 %shard_map.86 = (f32[2,36,64,128]{3,2,1,0:T(8,128)}, f32[36,8,128]{2,1,0:T(8,128)}, f32[36,8,128]{2,1,0:T(8,128)}, f32[2,64,128]{2,1,0:T(8,128)}, f32[2,64,128]{2,1,0:T(8,128)}) custom-call(s32[1,1]{1,0:T(1,128)S(6)} %copy.9.rot_ref.refs_0_, f32[4,36,64,128]{3,2,1,0:T(8,128)} %refs_0_.2), custom_call_target="tpu_custom_call" | custom-call | tf_op jit(solution)/shard_map/pallas_call | solution.py:384
  7.3 4.8 %collective-permute-start = (f32[36,8,128]{2,1,0:T(8,128)}, f32[36,8,128]{2,1,0:T(8,128)S(1)}, u32[]{:S(2)}, u32[]{:S(2)}) collective-permute-start(f32[36,8,128]{2,1,0:T(8,128)} %get-tuple-element.37), channel_id=1, source_target_pairs={{0,8},{8,16},{16,24},{1,9},{9,17},{17,25},{2,10},{10,18},{18,26},{... | collective-permute-start | bytes 442376 | tf_op jit(solution)/shard_map/ppermute | solution.py:354
  12.2 1.3 %collective-permute-start.1 = (f32[36,8,128]{2,1,0:T(8,128)}, f32[36,8,128]{2,1,0:T(8,128)S(1)}, u32[]{:S(2)}, u32[]{:S(2)}) collective-permute-start(f32[36,8,128]{2,1,0:T(8,128)} %get-tuple-element.38), channel_id=1, source_target_pairs={{8,0},{16,8},{24,16},{9,1},{17,9},{25,17},{10,2},{18,10},{26,18},{... | collective-permute-start | bytes 442376 | tf_op jit(solution)/shard_map/ppermute | solution.py:355
  13.5 2.8 %collective-permute-start.2 = (f32[2,64,128]{2,1,0:T(8,128)}, f32[2,64,128]{2,1,0:T(8,128)S(1)}, u32[]{:S(2)}, u32[]{:S(2)}) collective-permute-start(f32[2,64,128]{2,1,0:T(8,128)} %get-tuple-element.39), channel_id=1, source_target_pairs={{1,0},{2,1},{3,2},{4,3},{5,4},{6,5},{7,6},{0,7},{9,8},{10,9},{11,1... | collective-permute-start | bytes 196616 | tf_op jit(solution)/shard_map/ppermute | solution.py:356
  16.5 1.2 %fusion.3.refs_4_ = f32[256,128]{1,0:T(8,128)} fusion(s32[256]{0:T(256)S(1)} %add.169), kind=kLoop, calls=%fused_computation.6 | loop fusion | flops 458752 | bytes 132096 | tf_op jit(solution)/shard_map/cos | solution.py:371
  17.7 1.0 fusion.10.refs_5_
  18.8 5.4 %shard_map.87 = (f32[36,64,128]{2,1,0:T(8,128)}, f32[36,64,128]{2,1,0:T(8,128)}, f32[36,64,128]{2,1,0:T(8,128)}, f32[36,64,128]{2,1,0:T(8,128)}, f32[36,64,128]{2,1,0:T(8,128)}, /*index=5*/f32[36,64,128]{2,1,0:T(8,128)}) custom-call(f32[36,64,128]{2,1,0:T(8,128)} %vd_ref.1, s32[64,128]{1,0:T(8,128)} %wet_ref.1), custom_call_target="tpu_custom_call" | custom-call | tf_op jit(solution)/shard_map/pallas_call | solution.py:386
  24.3 0.7 broadcast_in_dim.10.refs_9_.refs_10_
  25.1 17.2 %shard_map.88 = (f32[2,36,64,128]{3,2,1,0:T(8,128)}, f32[2,36,64,128]{3,2,1,0:T(8,128)}, f32[2,64,128]{2,1,0:T(8,128)}, f32[36,8,128]{2,1,0:T(8,128)}, f32[36,8,...) custom-call(f32[4,36,64,128]{3,2,1,0:T(8,128)} %refs_0_.2, ...), custom_call_target="tpu_custom_call" | custom-call | tf_op jit(solution)/shard_map/pallas_call | solution.py:405
  42.3 4.3 %collective-permute-start.4 = (f32[36,8,128]{2,1,0:T(8,128)}, f32[36,8,128]{2,1,0:T(8,128)S(1)}, u32[]{:S(2)}, u32[]{:S(2)}) collective-permute-start(f32[36,8,128]{2,1,0:T(8,128)} %get-tuple-element.43), channel_id=1, source_target_pairs={{0,8},{8,16},{16,24},{1,9},{9,17},{17,25},{2,10},{10,18},{18,26},{... | collective-permute-start | bytes 442376 | tf_op jit(solution)/shard_map/ppermute | solution.py:354
  46.6 1.3 %collective-permute-start.5 = (f32[36,8,128]{2,1,0:T(8,128)}, f32[36,8,128]{2,1,0:T(8,128)S(1)}, u32[]{:S(2)}, u32[]{:S(2)}) collective-permute-start(f32[36,8,128]{2,1,0:T(8,128)} %get-tuple-element.44), channel_id=1, source_target_pairs={{8,0},{16,8},{24,16},{9,1},{17,9},{25,17},{10,2},{18,10},{26,18},{... | collective-permute-start | bytes 442376 | tf_op jit(solution)/shard_map/ppermute | solution.py:355
  47.9 3.3 %collective-permute-start.6 = (f32[2,64,128]{2,1,0:T(8,128)}, f32[2,64,128]{2,1,0:T(8,128)S(1)}, u32[]{:S(2)}, u32[]{:S(2)}) collective-permute-start(f32[2,64,128]{2,1,0:T(8,128)} %get-tuple-element.45), channel_id=1, source_target_pairs={{1,0},{2,1},{3,2},{4,3},{5,4},{6,5},{7,6},{0,7},{9,8},{10,9},{11,1... | collective-permute-start | bytes 196616 | tf_op jit(solution)/shard_map/ppermute | solution.py:356
  51.2 3.0 %collective-permute-start.11 = (f32[2,64,128]{2,1,0:T(8,128)}, f32[2,64,128]{2,1,0:T(8,128)S(1)}, u32[]{:S(2)}, u32[]{:S(2)}) collective-permute-start(f32[2,64,128]{2,1,0:T(8,128)} %get-tuple-element.49.refs_0_), channel_id=1, source_target_pairs={{0,8},{8,16},{16,24},{24,0},{1,9},{9,17},{17,25},{25,1},{2,10},{10... | collective-permute-start | bytes 196616 | tf_op jit(solution)/shard_map/ppermute | solution.py:364
  55.4 2.2 %collective-permute-start.12 = (f32[2,64,128]{2,1,0:T(8,128)}, f32[2,64,128]{2,1,0:T(8,128)S(1)}, u32[]{:S(2)}, u32[]{:S(2)}) collective-permute-start(f32[2,64,128]{2,1,0:T(8,128)} %get-tuple-element.49.refs_0_), channel_id=1, source_target_pairs={{0,16},{8,24},{16,0},{24,8},{1,17},{9,25},{17,1},{25,9},{2,18},{10... | collective-permute-start | bytes 196616 | tf_op jit(solution)/shard_map/ppermute | solution.py:364
  57.6 2.6 %collective-permute-start.13 = (f32[2,64,128]{2,1,0:T(8,128)}, f32[2,64,128]{2,1,0:T(8,128)S(1)}, u32[]{:S(2)}, u32[]{:S(2)}) collective-permute-start(f32[2,64,128]{2,1,0:T(8,128)} %get-tuple-element.49.refs_0_), channel_id=1, source_target_pairs={{0,24},{8,0},{16,8},{24,16},{1,25},{9,1},{17,9},{25,17},{2,26},{10... | collective-permute-start | bytes 196616 | tf_op jit(solution)/shard_map/ppermute | solution.py:364
  60.2 0.6 copy-done.2
  60.9 14.6 %shard_map.89 = (f32[4,36,64,128]{3,2,1,0:T(8,128)}, f32[2,64,128]{2,1,0:T(8,128)}) custom-call(s32[1,1]{1,0:T(1,128)S(6)} %copy.9.rot_ref.refs_0_, f32[2,36,64,128]{3,2,1,0:T(8,128)} %get-tuple-element.41.refs_1_, f32[2,36,64,128]{3,2,1,0:T(8,128)} %get-tuple-element.42.refs_2_, f32[2,36,64,128]{3,2,1,0:T(8,128)} %refs_3_.1, ...), custom_call_target="tpu_custom_call" | custom-call | tf_op jit(solution)/shard_map/pallas_call | solution.py:416
  75.6 2.9 %collective-permute-start.9 = (f32[2,64,128]{2,1,0:T(8,128)}, f32[2,64,128]{2,1,0:T(8,128)S(1)}, u32[]{:S(2)}, u32[]{:S(2)}) collective-permute-start(f32[2,64,128]{2,1,0:T(8,128)} %get-tuple-element.48.refs_0_), channel_id=1, source_target_pairs={{0,16},{8,24},{16,0},{24,8},{1,17},{9,25},{17,1},{25,9},{2,18},{10... | collective-permute-start | bytes 196616 | tf_op jit(solution)/shard_map/ppermute | solution.py:364
  78.4 1.2 %collective-permute-start.10 = (f32[2,64,128]{2,1,0:T(8,128)}, f32[2,64,128]{2,1,0:T(8,128)S(1)}, u32[]{:S(2)}, u32[]{:S(2)}) collective-permute-start(f32[2,64,128]{2,1,0:T(8,128)} %get-tuple-element.48.refs_0_), channel_id=1, source_target_pairs={{0,24},{8,0},{16,8},{24,16},{1,25},{9,1},{17,9},{25,17},{2,26},{10... | collective-permute-start | bytes 196616 | tf_op jit(solution)/shard_map/ppermute | solution.py:364
  79.6 0.5 compare_convert_fusion.valid_ref
  80.2 0.6 copy-done.9
  80.8 0.6 copy-done.10
  81.4 3.1 %shard_map.90.refs_6_ = f32[256,128]{1,0:T(8,128)} custom-call(f32[2,64,128]{2,1,0:T(8,128)} %get-tuple-element.49.refs_0_, f32[2,64,128]{2,1,0:T(8,128)} %copy-done.8, f32[2,64,128]{2,1,0:T(8,128)} %copy-done.9, f32[2,64,128]{2,1,0:T(8,128)} %copy-done.10, f32[256,128]{1,0:T(8,128)} %fusion.3.refs_4_, f32[128,128]{1,0:T(8,128)} %fusion.10.refs_5_), custom_call_target="tpu_custom_call" | custom-call | tf_op jit(solution)/shard_map/pallas_call | solution.py:413
  84.6 0.6 copy-done.11
  85.2 0.6 copy-done.13
  85.8 3.3 %shard_map.91 = (f32[64,128]{1,0:T(8,128)}, f32[64,128]{1,0:T(8,128)}, f32[64,128]{1,0:T(8,128)}, f32[64,128]{1,0:T(8,128)}, f32[64,128]{1,0:T(8,128)}, /*index=...) custom-call(s32[8]{0:T(128)} %and_select_fusion.2.slot_ref, s32[8]{0:T(128)} %compare_convert_fusion.valid_ref, ...), custom_call_target="tpu_custom_call" | custom-call | tf_op jit(solution)/shard_map/pallas_call | solution.py:424
  89.6 2.7 %collective-permute-start.17 = (f32[64,128]{1,0:T(8,128)}, f32[64,128]{1,0:T(8,128)S(1)}, u32[]{:S(2)}, u32[]{:S(2)}) collective-permute-start(f32[64,128]{1,0:T(8,128)} %get-tuple-element.54), channel_id=1, source_target_pairs={{0,4},{1,5},{2,6},{3,7},{4,0},{5,1},{6,2},{7,3},{8,12},{9,13},{10,... | collective-permute-start | bytes 98312 | tf_op jit(solution)/shard_map/ppermute | solution.py:432
  92.3 1.7 %collective-permute-start.15 = (f32[64,128]{1,0:T(8,128)}, f32[64,128]{1,0:T(8,128)S(1)}, u32[]{:S(2)}, u32[]{:S(2)}) collective-permute-start(f32[64,128]{1,0:T(8,128)} %get-tuple-element.52), channel_id=1, source_target_pairs={{0,2},{1,3},{2,4},{3,5},{4,6},{5,7},{6,0},{7,1},{8,10},{9,11},{10,... | collective-permute-start | bytes 98312 | tf_op jit(solution)/shard_map/ppermute | solution.py:432
  94.4 1.9 %collective-permute-done.17 = f32[64,128]{1,0:T(8,128)S(1)} collective-permute-done((f32[64,128]{1,0:T(8,128)}, f32[64,128]{1,0:T(8,128)S(1)}, u32[]{:S(2)}, u32[]{:S(2)}) %collective-permute-start.17) | collective-permute-done | bytes 32800 | tf_op jit(solution)/shard_map/ppermute | solution.py:432
  96.3 0.6 collective-permute-done.16
  96.8 2.0 %collective-permute-done.15 = f32[64,128]{1,0:T(8,128)S(1)} collective-permute-done((f32[64,128]{1,0:T(8,128)}, f32[64,128]{1,0:T(8,128)S(1)}, u32[]{:S(2)}, u32[]{:S(2)}) %collective-permute-start.15) | collective-permute-done | bytes 32800 | tf_op jit(solution)/shard_map/ppermute | solution.py:432
  99.3 1.4 %add_add_fusion = f32[64,128]{1,0:T(8,128)} fusion(f32[64,128]{1,0:T(8,128)S(1)} %collective-permute-done.20, f32[64,128]{1,0:T(8,128)S(1)} %collective-permute-done.19, f32[64,128]{1,0:T(8,128)S(1)} %collective-permute-done.18, f32[64,128]{1,0:T(8,128)S(1)} %collective-permute-done.17, f32[64,128]{1,0:T(8,128)S(1)} %collective-permute-done.16, ...), kind=kLoop, calls=%fused_computation.20 | loop fusion | flops 57344 | bytes 294912 | tf_op jit(solution)/shard_map/add | solution.py:432
  (59 shorter events, 2.4 us)
Async XLA Ops:
  1.3 17.4 %copy-start.14 = (s32[32]{0:T(128)S(1)}, s32[32]{0:T(128)}, u32[]{:S(2)}) copy-start(s32[32]{0:T(128)} %param.13) | copy-start | bytes 388
  7.3 17.0 %collective-permute-start = (f32[36,8,128]{2,1,0:T(8,128)}, f32[36,8,128]{2,1,0:T(8,128)S(1)}, u32[]{:S(2)}, u32[]{:S(2)}) collective-permute-start(f32[36,8,128]{2,1,0:T(8,128)} %get-tuple-element.37), channel_id=1, source_target_pairs={{0,8},{8,16},{16,24},{1,9},{9,17},{17,25},{2,10},{10,18},{18,26},{... | collective-permute-start | bytes 442376 | tf_op jit(solution)/shard_map/ppermute | solution.py:354
  12.2 12.2 %collective-permute-start.1 = (f32[36,8,128]{2,1,0:T(8,128)}, f32[36,8,128]{2,1,0:T(8,128)S(1)}, u32[]{:S(2)}, u32[]{:S(2)}) collective-permute-start(f32[36,8,128]{2,1,0:T(8,128)} %get-tuple-element.38), channel_id=1, source_target_pairs={{8,0},{16,8},{24,16},{9,1},{17,9},{25,17},{10,2},{18,10},{26,18},{... | collective-permute-start | bytes 442376 | tf_op jit(solution)/shard_map/ppermute | solution.py:355
  13.5 10.8 %collective-permute-start.2 = (f32[2,64,128]{2,1,0:T(8,128)}, f32[2,64,128]{2,1,0:T(8,128)S(1)}, u32[]{:S(2)}, u32[]{:S(2)}) collective-permute-start(f32[2,64,128]{2,1,0:T(8,128)} %get-tuple-element.39), channel_id=1, source_target_pairs={{1,0},{2,1},{3,2},{4,3},{5,4},{6,5},{7,6},{0,7},{9,8},{10,9},{11,1... | collective-permute-start | bytes 196616 | tf_op jit(solution)/shard_map/ppermute | solution.py:356
  16.3 8.0 %collective-permute-start.3 = (f32[2,64,128]{2,1,0:T(8,128)}, f32[2,64,128]{2,1,0:T(8,128)S(1)}, u32[]{:S(2)}, u32[]{:S(2)}) collective-permute-start(f32[2,64,128]{2,1,0:T(8,128)} %get-tuple-element.40), channel_id=1, source_target_pairs={{0,1},{1,2},{2,3},{3,4},{4,5},{5,6},{6,7},{7,0},{8,9},{9,10},{10,1... | collective-permute-start | bytes 196616 | tf_op jit(solution)/shard_map/ppermute | solution.py:357
  24.3 0.8 copy-start.4
  24.3 0.8 copy-start.5
  24.3 0.8 copy-start
  24.3 0.7 copy-start.1
  42.3 17.9 %collective-permute-start.4 = (f32[36,8,128]{2,1,0:T(8,128)}, f32[36,8,128]{2,1,0:T(8,128)S(1)}, u32[]{:S(2)}, u32[]{:S(2)}) collective-permute-start(f32[36,8,128]{2,1,0:T(8,128)} %get-tuple-element.43), channel_id=1, source_target_pairs={{0,8},{8,16},{16,24},{1,9},{9,17},{17,25},{2,10},{10,18},{18,26},{... | collective-permute-start | bytes 442376 | tf_op jit(solution)/shard_map/ppermute | solution.py:354
  46.6 13.6 %collective-permute-start.5 = (f32[36,8,128]{2,1,0:T(8,128)}, f32[36,8,128]{2,1,0:T(8,128)S(1)}, u32[]{:S(2)}, u32[]{:S(2)}) collective-permute-start(f32[36,8,128]{2,1,0:T(8,128)} %get-tuple-element.44), channel_id=1, source_target_pairs={{8,0},{16,8},{24,16},{9,1},{17,9},{25,17},{10,2},{18,10},{26,18},{... | collective-permute-start | bytes 442376 | tf_op jit(solution)/shard_map/ppermute | solution.py:355
  47.9 7.5 %collective-permute-start.6 = (f32[2,64,128]{2,1,0:T(8,128)}, f32[2,64,128]{2,1,0:T(8,128)S(1)}, u32[]{:S(2)}, u32[]{:S(2)}) collective-permute-start(f32[2,64,128]{2,1,0:T(8,128)} %get-tuple-element.45), channel_id=1, source_target_pairs={{1,0},{2,1},{3,2},{4,3},{5,4},{6,5},{7,6},{0,7},{9,8},{10,9},{11,1... | collective-permute-start | bytes 196616 | tf_op jit(solution)/shard_map/ppermute | solution.py:356
  51.2 6.4 %collective-permute-start.7 = (f32[2,64,128]{2,1,0:T(8,128)}, f32[2,64,128]{2,1,0:T(8,128)S(1)}, u32[]{:S(2)}, u32[]{:S(2)}) collective-permute-start(f32[2,64,128]{2,1,0:T(8,128)} %get-tuple-element.46), channel_id=1, source_target_pairs={{0,1},{1,2},{2,3},{3,4},{4,5},{5,6},{6,7},{7,0},{8,9},{9,10},{10,1... | collective-permute-start | bytes 196616 | tf_op jit(solution)/shard_map/ppermute | solution.py:357
  51.2 27.3 %collective-permute-start.11 = (f32[2,64,128]{2,1,0:T(8,128)}, f32[2,64,128]{2,1,0:T(8,128)S(1)}, u32[]{:S(2)}, u32[]{:S(2)}) collective-permute-start(f32[2,64,128]{2,1,0:T(8,128)} %get-tuple-element.49.refs_0_), channel_id=1, source_target_pairs={{0,8},{8,16},{16,24},{24,0},{1,9},{9,17},{17,25},{25,1},{2,10},{10... | collective-permute-start | bytes 196616 | tf_op jit(solution)/shard_map/ppermute | solution.py:364
  55.4 4.8 %copy-start.6 = (f32[2,64,128]{2,1,0:T(8,128)}, f32[2,64,128]{2,1,0:T(8,128)S(1)}, u32[]{:S(2)}) copy-start(f32[2,64,128]{2,1,0:T(8,128)S(1)} %collective-permute-done.6.refs_13_) | copy-start | bytes 196612
  55.4 24.8 %collective-permute-start.12 = (f32[2,64,128]{2,1,0:T(8,128)}, f32[2,64,128]{2,1,0:T(8,128)S(1)}, u32[]{:S(2)}, u32[]{:S(2)}) collective-permute-start(f32[2,64,128]{2,1,0:T(8,128)} %get-tuple-element.49.refs_0_), channel_id=1, source_target_pairs={{0,16},{8,24},{16,0},{24,8},{1,17},{9,25},{17,1},{25,9},{2,18},{10... | collective-permute-start | bytes 196616 | tf_op jit(solution)/shard_map/ppermute | solution.py:364
  57.6 2.6 %copy-start.7 = (f32[2,64,128]{2,1,0:T(8,128)}, f32[2,64,128]{2,1,0:T(8,128)S(1)}, u32[]{:S(2)}) copy-start(f32[2,64,128]{2,1,0:T(8,128)S(1)} %collective-permute-done.7.refs_14_) | copy-start | bytes 196612
  57.6 22.6 %collective-permute-start.13 = (f32[2,64,128]{2,1,0:T(8,128)}, f32[2,64,128]{2,1,0:T(8,128)S(1)}, u32[]{:S(2)}, u32[]{:S(2)}) collective-permute-start(f32[2,64,128]{2,1,0:T(8,128)} %get-tuple-element.49.refs_0_), channel_id=1, source_target_pairs={{0,24},{8,0},{16,8},{24,16},{1,25},{9,1},{17,9},{25,17},{2,26},{10... | collective-permute-start | bytes 196616 | tf_op jit(solution)/shard_map/ppermute | solution.py:364
  60.2 0.7 copy-start.2
  60.2 0.7 copy-start.3
  75.6 9.0 %collective-permute-start.8 = (f32[2,64,128]{2,1,0:T(8,128)}, f32[2,64,128]{2,1,0:T(8,128)S(1)}, u32[]{:S(2)}, u32[]{:S(2)}) collective-permute-start(f32[2,64,128]{2,1,0:T(8,128)} %get-tuple-element.48.refs_0_), channel_id=1, source_target_pairs={{0,8},{8,16},{16,24},{24,0},{1,9},{9,17},{17,25},{25,1},{2,10},{10... | collective-permute-start | bytes 196616 | tf_op jit(solution)/shard_map/ppermute | solution.py:364
  75.6 9.0 %collective-permute-start.9 = (f32[2,64,128]{2,1,0:T(8,128)}, f32[2,64,128]{2,1,0:T(8,128)S(1)}, u32[]{:S(2)}, u32[]{:S(2)}) collective-permute-start(f32[2,64,128]{2,1,0:T(8,128)} %get-tuple-element.48.refs_0_), channel_id=1, source_target_pairs={{0,16},{8,24},{16,0},{24,8},{1,17},{9,25},{17,1},{25,9},{2,18},{10... | collective-permute-start | bytes 196616 | tf_op jit(solution)/shard_map/ppermute | solution.py:364
  78.4 1.8 %copy-start.8 = (f32[2,64,128]{2,1,0:T(8,128)}, f32[2,64,128]{2,1,0:T(8,128)S(1)}, u32[]{:S(2)}) copy-start(f32[2,64,128]{2,1,0:T(8,128)S(1)} %collective-permute-done.11.refs_1_) | copy-start | bytes 196612
  78.4 6.1 %collective-permute-start.10 = (f32[2,64,128]{2,1,0:T(8,128)}, f32[2,64,128]{2,1,0:T(8,128)S(1)}, u32[]{:S(2)}, u32[]{:S(2)}) collective-permute-start(f32[2,64,128]{2,1,0:T(8,128)} %get-tuple-element.48.refs_0_), channel_id=1, source_target_pairs={{0,24},{8,0},{16,8},{24,16},{1,25},{9,1},{17,9},{25,17},{2,26},{10... | collective-permute-start | bytes 196616 | tf_op jit(solution)/shard_map/ppermute | solution.py:364
  84.6 0.7 copy-start.12
  89.1 3.2 %collective-permute-start.20 = (f32[64,128]{1,0:T(8,128)}, f32[64,128]{1,0:T(8,128)S(1)}, u32[]{:S(2)}, u32[]{:S(2)}) collective-permute-start(f32[64,128]{1,0:T(8,128)} %get-tuple-element.57), channel_id=1, source_target_pairs={{0,7},{1,0},{2,1},{3,2},{4,3},{5,4},{6,5},{7,6},{8,15},{9,8},{10,9... | collective-permute-start | bytes 98312 | tf_op jit(solution)/shard_map/ppermute | solution.py:432
  89.6 4.4 %collective-permute-start.19 = (f32[64,128]{1,0:T(8,128)}, f32[64,128]{1,0:T(8,128)S(1)}, u32[]{:S(2)}, u32[]{:S(2)}) collective-permute-start(f32[64,128]{1,0:T(8,128)} %get-tuple-element.56), channel_id=1, source_target_pairs={{0,6},{1,7},{2,0},{3,1},{4,2},{5,3},{6,4},{7,5},{8,14},{9,15},{10,... | collective-permute-start | bytes 98312 | tf_op jit(solution)/shard_map/ppermute | solution.py:432
  89.6 4.8 %collective-permute-start.18 = (f32[64,128]{1,0:T(8,128)}, f32[64,128]{1,0:T(8,128)S(1)}, u32[]{:S(2)}, u32[]{:S(2)}) collective-permute-start(f32[64,128]{1,0:T(8,128)} %get-tuple-element.55), channel_id=1, source_target_pairs={{0,5},{1,6},{2,7},{3,0},{4,1},{5,2},{6,3},{7,4},{8,13},{9,14},{10,... | collective-permute-start | bytes 98312 | tf_op jit(solution)/shard_map/ppermute | solution.py:432
  89.6 6.7 %collective-permute-start.17 = (f32[64,128]{1,0:T(8,128)}, f32[64,128]{1,0:T(8,128)S(1)}, u32[]{:S(2)}, u32[]{:S(2)}) collective-permute-start(f32[64,128]{1,0:T(8,128)} %get-tuple-element.54), channel_id=1, source_target_pairs={{0,4},{1,5},{2,6},{3,7},{4,0},{5,1},{6,2},{7,3},{8,12},{9,13},{10,... | collective-permute-start | bytes 98312 | tf_op jit(solution)/shard_map/ppermute | solution.py:432
  92.3 4.6 %collective-permute-start.16 = (f32[64,128]{1,0:T(8,128)}, f32[64,128]{1,0:T(8,128)S(1)}, u32[]{:S(2)}, u32[]{:S(2)}) collective-permute-start(f32[64,128]{1,0:T(8,128)} %get-tuple-element.53), channel_id=1, source_target_pairs={{0,3},{1,4},{2,5},{3,6},{4,7},{5,0},{6,1},{7,2},{8,11},{9,12},{10,... | collective-permute-start | bytes 98312 | tf_op jit(solution)/shard_map/ppermute | solution.py:432
  92.3 6.6 %collective-permute-start.15 = (f32[64,128]{1,0:T(8,128)}, f32[64,128]{1,0:T(8,128)S(1)}, u32[]{:S(2)}, u32[]{:S(2)}) collective-permute-start(f32[64,128]{1,0:T(8,128)} %get-tuple-element.52), channel_id=1, source_target_pairs={{0,2},{1,3},{2,4},{3,5},{4,6},{5,7},{6,0},{7,1},{8,10},{9,11},{10,... | collective-permute-start | bytes 98312 | tf_op jit(solution)/shard_map/ppermute | solution.py:432
  93.9 5.3 %collective-permute-start.14 = (f32[64,128]{1,0:T(8,128)}, f32[64,128]{1,0:T(8,128)S(1)}, u32[]{:S(2)}, u32[]{:S(2)}) collective-permute-start(f32[64,128]{1,0:T(8,128)} %get-tuple-element.51), channel_id=1, source_target_pairs={{0,1},{1,2},{2,3},{3,4},{4,5},{5,6},{6,7},{7,0},{8,9},{9,10},{10,1... | collective-permute-start | bytes 98312 | tf_op jit(solution)/shard_map/ppermute | solution.py:432
  (4 other events, 2.5 us)

commit v2 on v1

--- a/solution.py
+++ b/solution.py
@@ -26,7 +26,7 @@
 LANES = 128
 VMEM = pl.BlockSpec(memory_space=pltpu.VMEM)
 SMEM = pl.BlockSpec(memory_space=pltpu.SMEM)
-LIMIT = 56 << 20
+LIMIT = 16 << 20
 F32 = jnp.float32
 PREP_ROWS, PREP_UNROLL = 64, 6
 FACTOR_ROWS, FACTOR_UNROLL = 64, 2

time: 101 us -> 83.2 us (0.82)
  Pallas kernels: 49.6 us -> 27.2 us
  local copies, waits for them, and re-layouts: 4.02 us -> 8.67 us
  waiting for transfers between devices: 4.96 us -> 7.96 us
  other arithmetic: 4.98 us -> 3.14 us
  starting transfers between devices: 34.9 us -> 33.7 us
    pallas_call x1, Pallas kernels: 17.2 us -> 10.1 us  [body(): call(functools.partial(step_kernel, False), [pair, pair, surface] + edge_...]
    unnamed x30 -> x20, local copies, waits for them, and re-layouts: 3.22 us -> 8.52 us
    pallas_call x1, Pallas kernels: 14.6 us -> 9.54 us  [body(): call(functools.partial(step_kernel, True), [shape(*adjoint.shape), surfac...]
    pallas_call x1, Pallas kernels: 5.37 us -> 1.21 us  [body(): factors = call(factor_kernel, [full] * 6, [VMEM] * 2)(vert_diff, wet_levels)]
    pallas_call x1, Pallas kernels: 6.03 us -> 2.93 us  [body(): call(prep_kernel, [pair] + edge_rows + edge_cols, [SMEM, VMEM])]
    pallas_call x1, Pallas kernels: 3.11 us -> 1.42 us  [body(): call(functools.partial(first_transform_kernel, norm), shape(2 * KY, KX),...]
    ppermute x6, waiting for transfers between devices: 0.02 us -> 1.6 us  [gather_rows(): lax.ppermute(block, 'ty', [(i, (i + s) % ty) for i in range(ty)])]
    pallas_call x1, Pallas kernels: 3.26 us -> 1.98 us  [body(): call(functools.partial(second_transform_kernel, norm, tx), [shape(size, K...]
  transfers between devices with their start and end apart: 21 -> 21, of which waited for: 4 -> 7; matrix products, arithmetic and copies ran while one was open for 4% -> 3% of each run, Pallas kernels for 23% -> 15%
where the time goes in v2:
time: 83.2 us; the launch traced here: 82.8 us
  starting transfers between devices  33.7 us (41%)
  Pallas kernels  27.2 us (33%)
  local copies, waits for them, and re-layouts  8.67 us (10%)
  waiting for transfers between devices  7.96 us (10%)
  other arithmetic  3.14 us (4%)
  between operations  2.11 us (3%)
    ppermute x6, starting transfers between devices, gather_rows(): lax.ppermute(block, 'ty', [(i, (i + s) % ty) for i in range(ty)])  11.5 us
    pallas_call x1, Pallas kernels, body(): call(functools.partial(step_kernel, False), [pair, pair, surface] + edge_...  10.1 us
    ppermute x2, starting transfers between devices, exchange(): lax.ppermute(north, 'ty', up)  9.77 us
    pallas_call x1, Pallas kernels, body(): call(functools.partial(step_kernel, True), [shape(*adjoint.shape), surfac...  9.54 us
    unnamed x20, local copies, waits for them, and re-layouts  8.52 us
    ppermute x7, waiting for transfers between devices, body(): lax.ppermute(sends[s], 'tx', [(i, (i + s) % tx) for i in range(tx)])  5.07 us
    ppermute x2, starting transfers between devices, exchange(): lax.ppermute(west, 'tx', left)  4.92 us
    ppermute x7, starting transfers between devices, body(): lax.ppermute(sends[s], 'tx', [(i, (i + s) % tx) for i in range(tx)])  4.89 us
  transfers between devices with their start and end apart: 21, of which 7 were waited for; matrix products, arithmetic and copies ran while one was open for 3% of the time, Pallas kernels for 15%

profile of v2, /device:TPU:0, one launch (start us, length us, event | category | flops | bytes accessed | tf_op | source)
XLA Modules:
  0.0 82.8 jit_solution(11235115440617482782)
XLA Ops:
  1.3 2.3 %copy-done = f32[4,36,64,128]{3,2,1,0:T(8,128)S(1)} copy-done((f32[4,36,64,128]{3,2,1,0:T(8,128)S(1)}, f32[4,36,64,128]{3,2,1,0:T(8,128)}, u32[]{:S(2)}) %copy-start) | copy-done | bytes 4718616
  3.6 2.9 %shard_map.86 = (f32[2,36,64,128]{3,2,1,0:T(8,128)S(1)}, f32[36,8,128]{2,1,0:T(8,128)}, f32[36,8,128]{2,1,0:T(8,128)}, f32[2,64,128]{2,1,0:T(8,128)}, f32[2,64,128]{2,1,0:T(8,128)}) custom-call(s32[1,1]{1,0:T(1,128)S(6)} %copy.9.rot_ref.refs_0_, f32[4,36,64,128]{3,2,1,0:T(8,128)S(1)} %copy-done), custom_call_target="tpu_custom_call" | custom-call | tf_op jit(solution)/shard_map/pallas_call | solution.py:384
  6.6 1.4 %copy-done.3 = f32[2,36,64,128]{3,2,1,0:T(8,128)} copy-done((f32[2,36,64,128]{3,2,1,0:T(8,128)}, f32[2,36,64,128]{3,2,1,0:T(8,128)S(1)}, u32[]{:S(2)}) %copy-start.3) | copy-done | bytes 2359320
  8.0 5.5 %collective-permute-start = (f32[36,8,128]{2,1,0:T(8,128)}, f32[36,8,128]{2,1,0:T(8,128)}, u32[]{:S(2)}, u32[]{:S(2)}) collective-permute-start(f32[36,8,128]{2,1,0:T(8,128)} %get-tuple-element.37), channel_id=1, source_target_pairs={{0,8},{8,16},{16,24},{1,9},{9,17},{17,25},{2,10},{10,18},{18,26},{... | collective-permute-start | bytes 442376 | tf_op jit(solution)/shard_map/ppermute | solution.py:354
  13.5 1.3 %collective-permute-start.1 = (f32[36,8,128]{2,1,0:T(8,128)}, f32[36,8,128]{2,1,0:T(8,128)}, u32[]{:S(2)}, u32[]{:S(2)}) collective-permute-start(f32[36,8,128]{2,1,0:T(8,128)} %get-tuple-element.38), channel_id=1, source_target_pairs={{8,0},{16,8},{24,16},{9,1},{17,9},{25,17},{10,2},{18,10},{26,18},{... | collective-permute-start | bytes 442376 | tf_op jit(solution)/shard_map/ppermute | solution.py:355
  14.7 2.8 %collective-permute-start.2 = (f32[2,64,128]{2,1,0:T(8,128)}, f32[2,64,128]{2,1,0:T(8,128)}, u32[]{:S(2)}, u32[]{:S(2)}) collective-permute-start(f32[2,64,128]{2,1,0:T(8,128)} %get-tuple-element.39), channel_id=1, source_target_pairs={{1,0},{2,1},{3,2},{4,3},{5,4},{6,5},{7,6},{0,7},{9,8},{10,9},{11,1... | collective-permute-start | bytes 196616 | tf_op jit(solution)/shard_map/ppermute | solution.py:356
  17.7 1.2 %fusion.3.refs_4_ = f32[256,128]{1,0:T(8,128)} fusion(s32[256]{0:T(256)S(1)} %add.169), kind=kLoop, calls=%fused_computation.6 | loop fusion | flops 458752 | bytes 132096 | tf_op jit(solution)/shard_map/cos | solution.py:371
  19.0 1.0 %fusion.10.refs_5_ = f32[128,128]{1,0:T(8,128)} fusion(s32[128]{0:T(128)S(1)} %multiply_add_fusion.1), kind=kLoop, calls=%fused_computation.16 | loop fusion | flops 229376 | bytes 66048 | tf_op jit(solution)/shard_map/cos | solution.py:371
  20.1 0.7 copy-done.8
  20.9 1.2 %shard_map.87 = (f32[36,64,128]{2,1,0:T(8,128)S(1)}, f32[36,64,128]{2,1,0:T(8,128)S(1)}, f32[36,64,128]{2,1,0:T(8,128)S(1)}, f32[36,64,128]{2,1,0:T(8,128)S(1)},...) custom-call(f32[36,64,128]{2,1,0:T(8,128)S(1)} %copy-done.5, s32[64,128]{1,0:T(8,128)S(1)} %copy-done.8), custom_call_target="tpu_custom_call" | custom-call | tf_op jit(solution)/shard_map/pallas_call | solution.py:386
  22.1 1.2 %collective-permute-done.3.refs_13_ = f32[2,64,128]{2,1,0:T(8,128)} collective-permute-done((f32[2,64,128]{2,1,0:T(8,128)}, f32[2,64,128]{2,1,0:T(8,128)}, u32[]{:S(2)}, u32[]{:S(2)}) %collective-permute-start.3) | collective-permute-done | bytes 65568 | tf_op jit(solution)/shard_map/ppermute | solution.py:357
  23.4 2.3 %copy-done.1 = f32[4,36,64,128]{3,2,1,0:T(8,128)S(1)} copy-done((f32[4,36,64,128]{3,2,1,0:T(8,128)S(1)}, f32[4,36,64,128]{3,2,1,0:T(8,128)}, u32[]{:S(2)}) %copy-start.1) | copy-done | bytes 4718616
  25.8 1.7 %copy-done.4 = f32[2,36,64,128]{3,2,1,0:T(8,128)S(1)} copy-done((f32[2,36,64,128]{3,2,1,0:T(8,128)S(1)}, f32[2,36,64,128]{3,2,1,0:T(8,128)}, u32[]{:S(2)}) %copy-start.4) | copy-done | bytes 2359320
  27.5 10.1 %shard_map.88 = (f32[2,36,64,128]{3,2,1,0:T(8,128)S(1)}, f32[2,36,64,128]{3,2,1,0:T(8,128)S(1)}, f32[2,64,128]{2,1,0:T(8,128)S(1)}, f32[36,8,128]{2,1,0:T(8,128)...) custom-call(f32[4,36,64,128]{3,2,1,0:T(8,128)S(1)} %copy-done.1, ...), custom_call_target="tpu_custom_call" | custom-call | tf_op jit(solution)/shard_map/pallas_call | solution.py:405
  37.6 4.3 %collective-permute-start.4 = (f32[36,8,128]{2,1,0:T(8,128)S(1)}, f32[36,8,128]{2,1,0:T(8,128)S(1)}, u32[]{:S(2)}, u32[]{:S(2)}) collective-permute-start(f32[36,8,128]{2,1,0:T(8,128)S(1)} %get-tuple-element.43), channel_id=1, source_target_pairs={{0,8},{8,16},{16,24},{1,9},{9,17},{17,25},{2,10},{10,18},{18,26},{... | collective-permute-start | bytes 442376 | tf_op jit(solution)/shard_map/ppermute | solution.py:354
  41.9 1.3 %collective-permute-start.5 = (f32[36,8,128]{2,1,0:T(8,128)S(1)}, f32[36,8,128]{2,1,0:T(8,128)S(1)}, u32[]{:S(2)}, u32[]{:S(2)}) collective-permute-start(f32[36,8,128]{2,1,0:T(8,128)S(1)} %get-tuple-element.44), channel_id=1, source_target_pairs={{8,0},{16,8},{24,16},{9,1},{17,9},{25,17},{10,2},{18,10},{26,18},{... | collective-permute-start | bytes 442376 | tf_op jit(solution)/shard_map/ppermute | solution.py:355
  43.2 2.1 %collective-permute-start.6 = (f32[2,64,128]{2,1,0:T(8,128)S(1)}, f32[2,64,128]{2,1,0:T(8,128)S(1)}, u32[]{:S(2)}, u32[]{:S(2)}) collective-permute-start(f32[2,64,128]{2,1,0:T(8,128)S(1)} %get-tuple-element.45), channel_id=1, source_target_pairs={{1,0},{2,1},{3,2},{4,3},{5,4},{6,5},{7,6},{0,7},{9,8},{10,9},{11,1... | collective-permute-start | bytes 196616 | tf_op jit(solution)/shard_map/ppermute | solution.py:356
  45.3 2.4 %collective-permute-start.11 = (f32[2,64,128]{2,1,0:T(8,128)S(1)}, f32[2,64,128]{2,1,0:T(8,128)S(1)}, u32[]{:S(2)}, u32[]{:S(2)}) collective-permute-start(f32[2,64,128]{2,1,0:T(8,128)S(1)} %get-tuple-element.49.refs_0_), channel_id=1, source_target_pairs={{0,8},{8,16},{16,24},{24,0},{1,9},{9,17},{17,25},{25,1},{2,10},{10... | collective-permute-start | bytes 196616 | tf_op jit(solution)/shard_map/ppermute | solution.py:364
  48.3 2.4 %collective-permute-start.12 = (f32[2,64,128]{2,1,0:T(8,128)S(1)}, f32[2,64,128]{2,1,0:T(8,128)S(1)}, u32[]{:S(2)}, u32[]{:S(2)}) collective-permute-start(f32[2,64,128]{2,1,0:T(8,128)S(1)} %get-tuple-element.49.refs_0_), channel_id=1, source_target_pairs={{0,16},{8,24},{16,0},{24,8},{1,17},{9,25},{17,1},{25,9},{2,18},{10... | collective-permute-start | bytes 196616 | tf_op jit(solution)/shard_map/ppermute | solution.py:364
  50.8 3.3 %collective-permute-start.13 = (f32[2,64,128]{2,1,0:T(8,128)S(1)}, f32[2,64,128]{2,1,0:T(8,128)S(1)}, u32[]{:S(2)}, u32[]{:S(2)}) collective-permute-start(f32[2,64,128]{2,1,0:T(8,128)S(1)} %get-tuple-element.49.refs_0_), channel_id=1, source_target_pairs={{0,24},{8,0},{16,8},{24,16},{1,25},{9,1},{17,9},{25,17},{2,26},{10... | collective-permute-start | bytes 196616 | tf_op jit(solution)/shard_map/ppermute | solution.py:364
  54.1 9.5 %shard_map.89 = (f32[4,36,64,128]{3,2,1,0:T(8,128)}, f32[2,64,128]{2,1,0:T(8,128)S(1)}) custom-call(s32[1,1]{1,0:T(1,128)S(6)} %copy.9.rot_ref.refs_0_, f32[2,36,64,128]{3,2,1,0:T(8,128)S(1)} %get-tuple-element.41.refs_1_, f32[2,36,64,128]{3,2,1,0:T(8,128)S(1)} %get-tuple-element.42.refs_2_, f32[2,36,64,128]{3,2,1,0:T(8,128)S(1)} %copy-done.2, ...), custom_call_target="tpu_custom_call" | custom-call | tf_op jit(solution)/shard_map/pallas_call | solution.py:416
  63.6 2.3 %collective-permute-start.9 = (f32[2,64,128]{2,1,0:T(8,128)S(1)}, f32[2,64,128]{2,1,0:T(8,128)S(1)}, u32[]{:S(2)}, u32[]{:S(2)}) collective-permute-start(f32[2,64,128]{2,1,0:T(8,128)S(1)} %get-tuple-element.48.refs_0_), channel_id=1, source_target_pairs={{0,16},{8,24},{16,0},{24,8},{1,17},{9,25},{17,1},{25,9},{2,18},{10... | collective-permute-start | bytes 196616 | tf_op jit(solution)/shard_map/ppermute | solution.py:364
  65.9 1.2 %collective-permute-start.10 = (f32[2,64,128]{2,1,0:T(8,128)S(1)}, f32[2,64,128]{2,1,0:T(8,128)S(1)}, u32[]{:S(2)}, u32[]{:S(2)}) collective-permute-start(f32[2,64,128]{2,1,0:T(8,128)S(1)} %get-tuple-element.48.refs_0_), channel_id=1, source_target_pairs={{0,24},{8,0},{16,8},{24,16},{1,25},{9,1},{17,9},{25,17},{2,26},{10... | collective-permute-start | bytes 196616 | tf_op jit(solution)/shard_map/ppermute | solution.py:364
  67.1 1.4 %shard_map.90.refs_6_ = f32[256,128]{1,0:T(8,128)S(1)} custom-call(f32[2,64,128]{2,1,0:T(8,128)S(1)} %get-tuple-element.49.refs_0_, f32[2,64,128]{2,1,0:T(8,128)S(1)} %collective-permute-done.11.refs_1_, f32[2,64,128]{2,1,0:T(8,128)S(1)} %collective-permute-done.12.refs_2_, f32[2,64,128]{2,1,0:T(8,128)S(1)} %collective-permute-done.13.refs_3_, ...), custom_call_target="tpu_custom_call" | custom-call | tf_op jit(solution)/shard_map/pallas_call | solution.py:413
  68.8 1.3 %collective-permute-done.10.refs_3_ = f32[2,64,128]{2,1,0:T(8,128)S(1)} collective-permute-done((f32[2,64,128]{2,1,0:T(8,128)S(1)}, f32[2,64,128]{2,1,0:T(8,128)S(1)}, u32[]{:S(2)}, u32[]{:S(2)}) %collective-permute-start.10) | collective-permute-done | bytes 65568 | tf_op jit(solution)/shard_map/ppermute | solution.py:364
  70.2 2.0 %shard_map.91 = (f32[64,128]{1,0:T(8,128)S(1)}, f32[64,128]{1,0:T(8,128)S(1)}, f32[64,128]{1,0:T(8,128)S(1)}, f32[64,128]{1,0:T(8,128)S(1)}, f32[64,128]{1,0:T(8...) custom-call(s32[8]{0:T(128)S(1)} %and_select_fusion.2.slot_ref, ...), custom_call_target="tpu_custom_call" | custom-call | tf_op jit(solution)/shard_map/pallas_call | solution.py:424
  72.4 2.9 %collective-permute-start.17 = (f32[64,128]{1,0:T(8,128)S(1)}, f32[64,128]{1,0:T(8,128)S(1)}, u32[]{:S(2)}, u32[]{:S(2)}) collective-permute-start(f32[64,128]{1,0:T(8,128)S(1)} %get-tuple-element.54), channel_id=1, source_target_pairs={{0,4},{1,5},{2,6},{3,7},{4,0},{5,1},{6,2},{7,3},{8,12},{9,13},{10,... | collective-permute-start | bytes 98312 | tf_op jit(solution)/shard_map/ppermute | solution.py:432
  75.3 1.7 %collective-permute-start.15 = (f32[64,128]{1,0:T(8,128)S(1)}, f32[64,128]{1,0:T(8,128)S(1)}, u32[]{:S(2)}, u32[]{:S(2)}) collective-permute-start(f32[64,128]{1,0:T(8,128)S(1)} %get-tuple-element.52), channel_id=1, source_target_pairs={{0,2},{1,3},{2,4},{3,5},{4,6},{5,7},{6,0},{7,1},{8,10},{9,11},{10,... | collective-permute-start | bytes 98312 | tf_op jit(solution)/shard_map/ppermute | solution.py:432
  77.1 2.1 %collective-permute-done.17 = f32[64,128]{1,0:T(8,128)S(1)} collective-permute-done((f32[64,128]{1,0:T(8,128)S(1)}, f32[64,128]{1,0:T(8,128)S(1)}, u32[]{:S(2)}, u32[]{:S(2)}) %collective-permute-start.17) | collective-permute-done | bytes 32800 | tf_op jit(solution)/shard_map/ppermute | solution.py:432
  79.5 2.2 %collective-permute-done.15 = f32[64,128]{1,0:T(8,128)S(1)} collective-permute-done((f32[64,128]{1,0:T(8,128)S(1)}, f32[64,128]{1,0:T(8,128)S(1)}, u32[]{:S(2)}, u32[]{:S(2)}) %collective-permute-start.15) | collective-permute-done | bytes 32800 | tf_op jit(solution)/shard_map/ppermute | solution.py:432
  81.7 0.4 collective-permute-done.14
  82.2 0.6 add_add_fusion
  (49 shorter events, 1.5 us)
Async XLA Ops:
  1.3 2.3 %copy-start = (f32[4,36,64,128]{3,2,1,0:T(8,128)S(1)}, f32[4,36,64,128]{3,2,1,0:T(8,128)}, u32[]{:S(2)}) copy-start(f32[4,36,64,128]{3,2,1,0:T(8,128)} %refs_0_.2) | copy-start | bytes 14155780
  3.6 16.3 %copy-start.9 = (s32[32]{0:T(128)S(1)}, s32[32]{0:T(128)}, u32[]{:S(2)}) copy-start(s32[32]{0:T(128)} %param.13) | copy-start | bytes 388
  3.6 16.5 %copy-start.5 = (f32[36,64,128]{2,1,0:T(8,128)S(1)}, f32[36,64,128]{2,1,0:T(8,128)}, u32[]{:S(2)}) copy-start(f32[36,64,128]{2,1,0:T(8,128)} %vd_ref.1) | copy-start | bytes 3538948
  3.6 19.8 %copy-start.2 = (f32[2,36,64,128]{3,2,1,0:T(8,128)S(1)}, f32[2,36,64,128]{3,2,1,0:T(8,128)}, u32[]{:S(2)}) copy-start(f32[2,36,64,128]{3,2,1,0:T(8,128)} %refs_3_.1) | copy-start | bytes 7077892
  6.6 1.4 %copy-start.3 = (f32[2,36,64,128]{3,2,1,0:T(8,128)}, f32[2,36,64,128]{3,2,1,0:T(8,128)S(1)}, u32[]{:S(2)}) copy-start(f32[2,36,64,128]{3,2,1,0:T(8,128)S(1)} %get-tuple-element.30.refs_1_) | copy-start | bytes 7077892
  8.0 15.4 %collective-permute-start = (f32[36,8,128]{2,1,0:T(8,128)}, f32[36,8,128]{2,1,0:T(8,128)}, u32[]{:S(2)}, u32[]{:S(2)}) collective-permute-start(f32[36,8,128]{2,1,0:T(8,128)} %get-tuple-element.37), channel_id=1, source_target_pairs={{0,8},{8,16},{16,24},{1,9},{9,17},{17,25},{2,10},{10,18},{18,26},{... | collective-permute-start | bytes 442376 | tf_op jit(solution)/shard_map/ppermute | solution.py:354
  13.5 9.9 %collective-permute-start.1 = (f32[36,8,128]{2,1,0:T(8,128)}, f32[36,8,128]{2,1,0:T(8,128)}, u32[]{:S(2)}, u32[]{:S(2)}) collective-permute-start(f32[36,8,128]{2,1,0:T(8,128)} %get-tuple-element.38), channel_id=1, source_target_pairs={{8,0},{16,8},{24,16},{9,1},{17,9},{25,17},{10,2},{18,10},{26,18},{... | collective-permute-start | bytes 442376 | tf_op jit(solution)/shard_map/ppermute | solution.py:355
  14.7 7.4 %collective-permute-start.2 = (f32[2,64,128]{2,1,0:T(8,128)}, f32[2,64,128]{2,1,0:T(8,128)}, u32[]{:S(2)}, u32[]{:S(2)}) collective-permute-start(f32[2,64,128]{2,1,0:T(8,128)} %get-tuple-element.39), channel_id=1, source_target_pairs={{1,0},{2,1},{3,2},{4,3},{5,4},{6,5},{7,6},{0,7},{9,8},{10,9},{11,1... | collective-permute-start | bytes 196616 | tf_op jit(solution)/shard_map/ppermute | solution.py:356
  17.6 5.8 %collective-permute-start.3 = (f32[2,64,128]{2,1,0:T(8,128)}, f32[2,64,128]{2,1,0:T(8,128)}, u32[]{:S(2)}, u32[]{:S(2)}) collective-permute-start(f32[2,64,128]{2,1,0:T(8,128)} %get-tuple-element.40), channel_id=1, source_target_pairs={{0,1},{1,2},{2,3},{3,4},{4,5},{5,6},{6,7},{7,0},{8,9},{9,10},{10,1... | collective-permute-start | bytes 196616 | tf_op jit(solution)/shard_map/ppermute | solution.py:357
  20.1 0.8 copy-start.8
  23.4 2.3 %copy-start.1 = (f32[4,36,64,128]{3,2,1,0:T(8,128)S(1)}, f32[4,36,64,128]{3,2,1,0:T(8,128)}, u32[]{:S(2)}) copy-start(f32[4,36,64,128]{3,2,1,0:T(8,128)} %refs_0_.2) | copy-start | bytes 14155780
  25.8 1.7 %copy-start.4 = (f32[2,36,64,128]{3,2,1,0:T(8,128)S(1)}, f32[2,36,64,128]{3,2,1,0:T(8,128)}, u32[]{:S(2)}) copy-start(f32[2,36,64,128]{3,2,1,0:T(8,128)} %copy-done.3) | copy-start | bytes 7077892
  37.6 16.5 %collective-permute-start.4 = (f32[36,8,128]{2,1,0:T(8,128)S(1)}, f32[36,8,128]{2,1,0:T(8,128)S(1)}, u32[]{:S(2)}, u32[]{:S(2)}) collective-permute-start(f32[36,8,128]{2,1,0:T(8,128)S(1)} %get-tuple-element.43), channel_id=1, source_target_pairs={{0,8},{8,16},{16,24},{1,9},{9,17},{17,25},{2,10},{10,18},{18,26},{... | collective-permute-start | bytes 442376 | tf_op jit(solution)/shard_map/ppermute | solution.py:354
  41.9 12.2 %collective-permute-start.5 = (f32[36,8,128]{2,1,0:T(8,128)S(1)}, f32[36,8,128]{2,1,0:T(8,128)S(1)}, u32[]{:S(2)}, u32[]{:S(2)}) collective-permute-start(f32[36,8,128]{2,1,0:T(8,128)S(1)} %get-tuple-element.44), channel_id=1, source_target_pairs={{8,0},{16,8},{24,16},{9,1},{17,9},{25,17},{10,2},{18,10},{26,18},{... | collective-permute-start | bytes 442376 | tf_op jit(solution)/shard_map/ppermute | solution.py:355
  43.2 5.2 %collective-permute-start.6 = (f32[2,64,128]{2,1,0:T(8,128)S(1)}, f32[2,64,128]{2,1,0:T(8,128)S(1)}, u32[]{:S(2)}, u32[]{:S(2)}) collective-permute-start(f32[2,64,128]{2,1,0:T(8,128)S(1)} %get-tuple-element.45), channel_id=1, source_target_pairs={{1,0},{2,1},{3,2},{4,3},{5,4},{6,5},{7,6},{0,7},{9,8},{10,9},{11,1... | collective-permute-start | bytes 196616 | tf_op jit(solution)/shard_map/ppermute | solution.py:356
  45.3 5.5 %collective-permute-start.7 = (f32[2,64,128]{2,1,0:T(8,128)S(1)}, f32[2,64,128]{2,1,0:T(8,128)S(1)}, u32[]{:S(2)}, u32[]{:S(2)}) collective-permute-start(f32[2,64,128]{2,1,0:T(8,128)S(1)} %get-tuple-element.46), channel_id=1, source_target_pairs={{0,1},{1,2},{2,3},{3,4},{4,5},{5,6},{6,7},{7,0},{8,9},{9,10},{10,1... | collective-permute-start | bytes 196616 | tf_op jit(solution)/shard_map/ppermute | solution.py:357
  45.3 20.6 %collective-permute-start.11 = (f32[2,64,128]{2,1,0:T(8,128)S(1)}, f32[2,64,128]{2,1,0:T(8,128)S(1)}, u32[]{:S(2)}, u32[]{:S(2)}) collective-permute-start(f32[2,64,128]{2,1,0:T(8,128)S(1)} %get-tuple-element.49.refs_0_), channel_id=1, source_target_pairs={{0,8},{8,16},{16,24},{24,0},{1,9},{9,17},{17,25},{25,1},{2,10},{10... | collective-permute-start | bytes 196616 | tf_op jit(solution)/shard_map/ppermute | solution.py:364
  48.3 18.8 %collective-permute-start.12 = (f32[2,64,128]{2,1,0:T(8,128)S(1)}, f32[2,64,128]{2,1,0:T(8,128)S(1)}, u32[]{:S(2)}, u32[]{:S(2)}) collective-permute-start(f32[2,64,128]{2,1,0:T(8,128)S(1)} %get-tuple-element.49.refs_0_), channel_id=1, source_target_pairs={{0,16},{8,24},{16,0},{24,8},{1,17},{9,25},{17,1},{25,9},{2,18},{10... | collective-permute-start | bytes 196616 | tf_op jit(solution)/shard_map/ppermute | solution.py:364
  50.8 16.4 %collective-permute-start.13 = (f32[2,64,128]{2,1,0:T(8,128)S(1)}, f32[2,64,128]{2,1,0:T(8,128)S(1)}, u32[]{:S(2)}, u32[]{:S(2)}) collective-permute-start(f32[2,64,128]{2,1,0:T(8,128)S(1)} %get-tuple-element.49.refs_0_), channel_id=1, source_target_pairs={{0,24},{8,0},{16,8},{24,16},{1,25},{9,1},{17,9},{25,17},{2,26},{10... | collective-permute-start | bytes 196616 | tf_op jit(solution)/shard_map/ppermute | solution.py:364
  54.1 13.1 %copy-start.6 = (f32[256,128]{1,0:T(8,128)S(1)}, f32[256,128]{1,0:T(8,128)}, u32[]{:S(2)}) copy-start(f32[256,128]{1,0:T(8,128)} %fusion.3.refs_4_) | copy-start | bytes 393220
  54.1 13.1 %copy-start.7 = (f32[128,128]{1,0:T(8,128)S(1)}, f32[128,128]{1,0:T(8,128)}, u32[]{:S(2)}) copy-start(f32[128,128]{1,0:T(8,128)} %fusion.10.refs_5_) | copy-start | bytes 196612
  63.6 5.2 %collective-permute-start.8 = (f32[2,64,128]{2,1,0:T(8,128)S(1)}, f32[2,64,128]{2,1,0:T(8,128)S(1)}, u32[]{:S(2)}, u32[]{:S(2)}) collective-permute-start(f32[2,64,128]{2,1,0:T(8,128)S(1)} %get-tuple-element.48.refs_0_), channel_id=1, source_target_pairs={{0,8},{8,16},{16,24},{24,0},{1,9},{9,17},{17,25},{25,1},{2,10},{10... | collective-permute-start | bytes 196616 | tf_op jit(solution)/shard_map/ppermute | solution.py:364
  63.6 5.2 %collective-permute-start.9 = (f32[2,64,128]{2,1,0:T(8,128)S(1)}, f32[2,64,128]{2,1,0:T(8,128)S(1)}, u32[]{:S(2)}, u32[]{:S(2)}) collective-permute-start(f32[2,64,128]{2,1,0:T(8,128)S(1)} %get-tuple-element.48.refs_0_), channel_id=1, source_target_pairs={{0,16},{8,24},{16,0},{24,8},{1,17},{9,25},{17,1},{25,9},{2,18},{10... | collective-permute-start | bytes 196616 | tf_op jit(solution)/shard_map/ppermute | solution.py:364
  65.9 4.3 %collective-permute-start.10 = (f32[2,64,128]{2,1,0:T(8,128)S(1)}, f32[2,64,128]{2,1,0:T(8,128)S(1)}, u32[]{:S(2)}, u32[]{:S(2)}) collective-permute-start(f32[2,64,128]{2,1,0:T(8,128)S(1)} %get-tuple-element.48.refs_0_), channel_id=1, source_target_pairs={{0,24},{8,0},{16,8},{24,16},{1,25},{9,1},{17,9},{25,17},{2,26},{10... | collective-permute-start | bytes 196616 | tf_op jit(solution)/shard_map/ppermute | solution.py:364
  72.2 3.1 %collective-permute-start.20 = (f32[64,128]{1,0:T(8,128)S(1)}, f32[64,128]{1,0:T(8,128)S(1)}, u32[]{:S(2)}, u32[]{:S(2)}) collective-permute-start(f32[64,128]{1,0:T(8,128)S(1)} %get-tuple-element.57), channel_id=1, source_target_pairs={{0,7},{1,0},{2,1},{3,2},{4,3},{5,4},{6,5},{7,6},{8,15},{9,8},{10,9... | collective-permute-start | bytes 98312 | tf_op jit(solution)/shard_map/ppermute | solution.py:432
  72.2 4.8 %collective-permute-start.19 = (f32[64,128]{1,0:T(8,128)S(1)}, f32[64,128]{1,0:T(8,128)S(1)}, u32[]{:S(2)}, u32[]{:S(2)}) collective-permute-start(f32[64,128]{1,0:T(8,128)S(1)} %get-tuple-element.56), channel_id=1, source_target_pairs={{0,6},{1,7},{2,0},{3,1},{4,2},{5,3},{6,4},{7,5},{8,14},{9,15},{10,... | collective-permute-start | bytes 98312 | tf_op jit(solution)/shard_map/ppermute | solution.py:432
  72.3 4.8 %collective-permute-start.18 = (f32[64,128]{1,0:T(8,128)S(1)}, f32[64,128]{1,0:T(8,128)S(1)}, u32[]{:S(2)}, u32[]{:S(2)}) collective-permute-start(f32[64,128]{1,0:T(8,128)S(1)} %get-tuple-element.55), channel_id=1, source_target_pairs={{0,5},{1,6},{2,7},{3,0},{4,1},{5,2},{6,3},{7,4},{8,13},{9,14},{10,... | collective-permute-start | bytes 98312 | tf_op jit(solution)/shard_map/ppermute | solution.py:432
  72.4 6.8 %collective-permute-start.17 = (f32[64,128]{1,0:T(8,128)S(1)}, f32[64,128]{1,0:T(8,128)S(1)}, u32[]{:S(2)}, u32[]{:S(2)}) collective-permute-start(f32[64,128]{1,0:T(8,128)S(1)} %get-tuple-element.54), channel_id=1, source_target_pairs={{0,4},{1,5},{2,6},{3,7},{4,0},{5,1},{6,2},{7,3},{8,12},{9,13},{10,... | collective-permute-start | bytes 98312 | tf_op jit(solution)/shard_map/ppermute | solution.py:432
  75.3 4.3 %collective-permute-start.16 = (f32[64,128]{1,0:T(8,128)S(1)}, f32[64,128]{1,0:T(8,128)S(1)}, u32[]{:S(2)}, u32[]{:S(2)}) collective-permute-start(f32[64,128]{1,0:T(8,128)S(1)} %get-tuple-element.53), channel_id=1, source_target_pairs={{0,3},{1,4},{2,5},{3,6},{4,7},{5,0},{6,1},{7,2},{8,11},{9,12},{10,... | collective-permute-start | bytes 98312 | tf_op jit(solution)/shard_map/ppermute | solution.py:432
  75.3 6.5 %collective-permute-start.15 = (f32[64,128]{1,0:T(8,128)S(1)}, f32[64,128]{1,0:T(8,128)S(1)}, u32[]{:S(2)}, u32[]{:S(2)}) collective-permute-start(f32[64,128]{1,0:T(8,128)S(1)} %get-tuple-element.52), channel_id=1, source_target_pairs={{0,2},{1,3},{2,4},{3,5},{4,6},{5,7},{6,0},{7,1},{8,10},{9,11},{10,... | collective-permute-start | bytes 98312 | tf_op jit(solution)/shard_map/ppermute | solution.py:432
  77.0 5.1 %collective-permute-start.14 = (f32[64,128]{1,0:T(8,128)S(1)}, f32[64,128]{1,0:T(8,128)S(1)}, u32[]{:S(2)}, u32[]{:S(2)}) collective-permute-start(f32[64,128]{1,0:T(8,128)S(1)} %get-tuple-element.51), channel_id=1, source_target_pairs={{0,1},{1,2},{2,3},{3,4},{4,5},{5,6},{6,7},{7,0},{8,9},{9,10},{10,1... | collective-permute-start | bytes 98312 | tf_op jit(solution)/shard_map/ppermute | solution.py:432

commit v3 on v2

v3 whole, which is shorter than its diff:
```python
import functools
import math

import jax
import jax.numpy as jnp
import numpy as np
from jax import lax
from jax.experimental import pallas as pl
from jax.experimental.pallas import tpu as pltpu
from jax.sharding import PartitionSpec as P

KY = 128
KX = 128
NFACE = 4

ADVECT_COEF = 0.3
DIFFUSE_COEF = 0.12
VISCOUS_COEF = 0.1
THERMAL_COEF = 0.4
HALINE_COEF = 0.3
PRESSURE_COEF = 0.4
SALINE_WEIGHT = 0.8
CORIOLIS_PEAK = 0.5
MOMENTUM_RATIO = 1.5

TILE = 8
LANES = 128
ANY = pl.BlockSpec(memory_space=pl.ANY)
VMEM = pl.BlockSpec(memory_space=pltpu.VMEM)
SMEM = pl.BlockSpec(memory_space=pltpu.SMEM)
F32 = jnp.float32
PREP_UNROLL = 6
FACTOR_ROWS, FACTOR_UNROLL = 64, 2
STEP_ROWS, UP_UNROLL, DOWN_UNROLL = 64, 4, 6


def shape(*dims):
    return jax.ShapeDtypeStruct(dims, F32)


def lanes_of(rows):
    return lax.broadcasted_iota(jnp.int32, (rows, LANES), 1)


def rows_of(rows):
    return lax.broadcasted_iota(jnp.int32, (rows, LANES), 0)


def loop(count, load, body, init, unroll):
    while count % unroll:
        unroll -= 1

    def several(i, carry):
        steps = [i * unroll + j for j in range(unroll)]
        loaded = [load(step) for step in steps]
        stores = []
        for step, values in zip(steps, loaded):
            carry, store = body(step, values, carry)
            stores.append(store)
        for store in stores:
            store()
        return carry

    return lax.fori_loop(0, count // unroll, several, init)


def turn_scalars(code):
    cosine = jnp.where(code == 0, 1.0, jnp.where(code == 2, -1.0, 0.0)).astype(F32)
    sine = jnp.where(code == 1, 1.0, jnp.where(code == 3, -1.0, 0.0)).astype(F32)
    return cosine, sine


def pack_columns(acc, k, fields, lane):
    at = 3 * k
    first, second, third = lane >= at, lane >= at + 1, lane >= at + 2
    east, west = [], []
    for g in range(2):
        tracer, flow = fields[g], fields[g + 2]
        rolled = pltpu.roll(tracer, at + 2, 1)
        east.append(jnp.where(first, jnp.where(third, pltpu.roll(flow, at + 3, 1), rolled), acc[g]))
        west.append(jnp.where(second, jnp.where(third, rolled, pltpu.roll(flow, at + 1, 1)), acc[g + 2]))
    return tuple(east + west)


def store_edge_rows(k, fields, block, last, south_ref, north_ref):
    size = fields[0].shape[0]
    for c in range(4):
        if block == 0:
            south_ref[k, 2 * c : 2 * c + 2, :] = fields[c][0:2, :]
        if block == last:
            north_ref[k, 2 * c : 2 * c + 2, :] = fields[c][size - 2 : size, :]


def write_messages(refs, south_ref, north_ref, east, west):
    row_a, row_b, col_a, col_b = refs
    even_y, even_x = lax.axis_index("ty") % 2 == 0, lax.axis_index("tx") % 2 == 0
    south, north = south_ref[...], north_ref[...]
    row_a[...] = jnp.where(even_y, north, south)
    row_b[...] = jnp.where(even_y, south, north)
    for rows, e, w in zip(east[0], east[1], west):
        for g in range(2):
            col_a[g, rows, :] = jnp.where(even_x, e[g], w[g])
            col_b[g, rows, :] = jnp.where(even_x, w[g], e[g])


def read_messages(refs, south_ref, north_ref, east_ref, west_ref):
    row_a, row_b, col_a, col_b = (ref[...] for ref in refs)
    here = lax.axis_index("ty")
    even_y, even_x = here % 2 == 0, lax.axis_index("tx") % 2 == 0
    south = jnp.where(even_y, row_b, row_a)
    north = jnp.where(even_y, row_a, row_b)
    south_ref[...] = jnp.where(here == 0, 0.0, south)
    north_ref[...] = jnp.where(here == lax.axis_size("ty") - 1, 0.0, north)
    east_ref[...] = jnp.where(even_x, col_a, col_b)
    west_ref[...] = jnp.where(even_x, col_b, col_a)


def prep_kernel(rot_ref, adj_ref, ts_ref, uv_ref, row_a, row_b, col_a, col_b, raw_ref, south_ref, north_ref, sems):
    levels, height = adj_ref.shape[1], adj_ref.shape[2]
    cosine, sine = turn_scalars(rot_ref[0, 0])
    step = PREP_UNROLL
    chunks = levels // step
    copies = []
    for i in range(chunks):
        part = pl.ds(i * step, step)
        for h, target in enumerate((ts_ref, raw_ref)):
            copy = pltpu.make_async_copy(adj_ref.at[pl.ds(2 * h, 2), part], target.at[:, part], sems.at[2 * i + h])
            copy.start()
            copies.append(copy)
    lane = lanes_of(height)
    zero = jnp.zeros((height, LANES), F32)
    acc = (zero,) * 4
    for i in range(chunks):
        copies[2 * i].wait()
        copies[2 * i + 1].wait()
        levels_here = range(i * step, (i + 1) * step)
        loaded = [(ts_ref[0, k], ts_ref[1, k], raw_ref[0, k], raw_ref[1, k]) for k in levels_here]
        stores = []
        for k, (t, s, a, b) in zip(levels_here, loaded):
            fields = (t, s, cosine * a - sine * b, sine * a + cosine * b)
            acc = pack_columns(acc, k, fields, lane)
            stores.append((k, fields))
        for k, fields in stores:
            uv_ref[0, k] = fields[2]
            uv_ref[1, k] = fields[3]
            store_edge_rows(k, fields, 0, 0, south_ref, north_ref)
    write_messages((row_a, row_b, col_a, col_b), south_ref, north_ref, ([pl.ds(0, height)], [acc[:2]]), [acc[2:]])


def factor_kernel(vd_ref, wet_ref, w1_ref, w2_ref, h1_ref, h2_ref, g1_ref, g2_ref):
    levels, height = vd_ref.shape[0], vd_ref.shape[1]
    out = ((w1_ref, h1_ref, g1_ref, 1.0), (w2_ref, h2_ref, g2_ref, MOMENTUM_RATIO))
    size = FACTOR_ROWS
    for block in range(height // size):
        rows = pl.ds(block * size, size)
        wet = wet_ref[rows, :]
        zero = jnp.zeros((size, LANES), F32)

        def load(i, rows=rows):
            return vd_ref[jnp.maximum(levels - 2 - i, 0), rows, :]

        def level(i, loaded, carry, rows=rows, wet=wet):
            k = levels - 1 - i
            below, inverses = carry
            mask = jnp.where(k < wet, 1.0, 0.0).astype(F32)
            above = jnp.where(k > 0, loaded * mask, 0.0)
            kept, stores = [], []
            for (w_ref, h_ref, g_ref, factor), inverse in zip(out, inverses):
                low, high = factor * below, factor * above
                pivot = 1.0 + high + low - low * (low * inverse)
                inverse = 1.0 / pivot
                masked = inverse * mask
                stores += [(w_ref, masked), (h_ref, low * masked), (g_ref, high * masked)]
                kept.append(inverse)

            def store():
                for ref, value in stores:
                    ref[k, rows, :] = value

            return (above, tuple(kept)), store

        loop(levels, load, level, (zero, (zero, zero)), FACTOR_UNROLL)


def step_kernel(final, *refs):
    ts_ref, uv_ref, flow_ref, w1_ref, w2_ref, h1_ref, h2_ref = refs[:7]
    if final:
        cor_ref, *messages = refs[7:12]
        first_ref, value_ref, surface_ref = refs[12:15]
        surface_ref[0:2] = first_ref[...]
        surface_at = 2
    else:
        g1_ref, g2_ref, cor_ref, *messages = refs[7:14]
        ts_out, uv_out, surface_ref, *sent = refs[14:21]
        value_ref, south_out, north_out = refs[21:24]
        surface_at = 0
    south_ref, north_ref, east_ref, west_ref = refs[-4:]
    read_messages(messages, south_ref, north_ref, east_ref, west_ref)
    levels, height = ts_ref.shape[1], ts_ref.shape[2]
    size = STEP_ROWS
    blocks = height // size
    lane, row = lanes_of(size), rows_of(size)
    low_two, high_two = lane < 2, lane >= LANES - 2
    low_one, high_one = lane < 1, lane >= LANES - 1
    zero = jnp.zeros((size, LANES), F32)
    first_cor = pl.multiple_of(lax.axis_index("ty") * height, TILE)
    packed = []

    def get(c, k, start):
        rows = pl.ds(start, TILE)
        return ts_ref[c, k, rows, :] if c < 2 else uv_ref[c - 2, k, rows, :]

    def line(c, k, start, halos):
        if 0 <= start <= height - TILE:
            return get(c, k, start)
        south, north = halos
        part = rows_of(TILE)
        if start < 0:
            halo = pltpu.roll(south, (-2 * c - 2 - start) % TILE, 0)
            return jnp.where(part < -start, halo, pltpu.roll(get(c, k, 0), -start, 0))
        over = start + TILE - height
        halo = pltpu.roll(north, (TILE - over - 2 * c) % TILE, 0)
        return jnp.where(part >= TILE - over, halo, pltpu.roll(get(c, k, height - TILE), TILE - over, 0))

    for block in range(blocks):
        rows = pl.ds(block * size, size)
        first_row = block * size
        cor = cor_ref[pl.ds(first_cor + block * size, size), :]

        def fetch(c, k, shift, halos, first_row=first_row):
            start = first_row + shift
            if 0 <= start <= height - size:
                part = pl.ds(start, size)
                return ts_ref[c, k, part, :] if c < 2 else uv_ref[c - 2, k, part, :]
            lines = [line(c, k, start + i, halos) for i in range(0, size, TILE)]
            return lines[0] if len(lines) == 1 else jnp.concatenate(lines, axis=0)

        def load_up(i, rows=rows, block=block, fetch=fetch):
            k = levels - 1 - i
            halos = (south_ref[k] if block == 0 else None, north_ref[k] if block == blocks - 1 else None)
            turn = LANES - 2 - 3 * k
            east = [pltpu.roll(east_ref[g, rows, :], turn, 1) for g in range(2)]
            west = [pltpu.roll(west_ref[g, rows, :], turn, 1) for g in range(2)]
            lines = [{s: fetch(c, k, s, halos) for s in ((0, 1, -1, 2, -2) if c < 2 else (0, 1, -1))} for c in range(4)]
            flow = [flow_ref[i, k, rows, :] for i in range(2)]
            factors = [ref[k, rows, :] for ref in (w1_ref, w2_ref, h1_ref, h2_ref)]
            return east, west, lines, flow, factors

        def upward(i, loaded, below, cor=cor, rows=rows):
            k = levels - 1 - i
            east, west, lines, flow, factors = loaded
            flow_x = flow[0] * (ADVECT_COEF / 12.0)
            flow_y = flow[1] * (ADVECT_COEF / 12.0)
            rhs, diff_x, diff_y = [], [], []
            for c in range(2):
                mid = lines[c][0]
                e1 = pltpu.roll(jnp.where(low_one, east[c], mid), LANES - 1, 1)
                w1 = pltpu.roll(jnp.where(high_one, west[c], mid), 1, 1)
                e2 = pltpu.roll(jnp.where(low_two, east[c], mid), LANES - 2, 1)
                w2 = pltpu.roll(jnp.where(high_two, west[c], mid), 2, 1)
                n1, s1, n2, s2 = (lines[c][s] for s in (1, -1, 2, -2))
                dx, dy = e1 - w1, n1 - s1
                grad = flow_x * (8.0 * dx - (e2 - w2)) + flow_y * (8.0 * dy - (n2 - s2))
                near = (e1 + w1) + (n1 + s1)
                rhs.append((1.0 - 4.0 * DIFFUSE_COEF) * mid + DIFFUSE_COEF * near + grad)
                diff_x.append(dx)
                diff_y.append(dy)
            push = [
                (0.5 * PRESSURE_COEF) * (d[0] - SALINE_WEIGHT * d[1]) for d in (diff_x, diff_y)
            ]
            sides = []
            for c in range(2, 4):
                mid = lines[c][0]
                e1 = jnp.where(high_one, east[c - 2], pltpu.roll(mid, LANES - 1, 1))
                w1 = jnp.where(low_one, west[c - 2], pltpu.roll(mid, 1, 1))
                n1, s1 = lines[c][1], lines[c][-1]
                near = (e1 + w1) + (n1 + s1)
                sides.append(e1 - w1 if c == 2 else n1 - s1)
                rhs.append((1.0 - 4.0 * VISCOUS_COEF) * mid + VISCOUS_COEF * near - push[c - 2])
            spread = sides[0] + sides[1]
            rhs[0] = rhs[0] + (0.5 * THERMAL_COEF) * spread
            rhs[1] = rhs[1] - (0.5 * HALINE_COEF) * spread
            rhs[2] = rhs[2] + cor * lines[3][0]
            rhs[3] = rhs[3] - cor * lines[2][0]
            values = tuple(
                factors[c // 2] * rhs[c] + factors[2 + c // 2] * below[c] for c in range(4)
            )

            def store():
                for c in range(4):
                    value_ref[c, k, rows, :] = values[c]

            return values, store

        top = loop(levels, load_up, upward, (zero,) * 4, UP_UNROLL)
        for c in range(2):
            surface_ref[surface_at + c, rows, :] = top[c]
        if final:
            continue

        def load_down(k, rows=rows):
            return [value_ref[c, k, rows, :] for c in range(4)], (g1_ref[k, rows, :], g2_ref[k, rows, :])

        def downward(k, loaded, carry, rows=rows, block=block):
            above, acc = carry
            values, gains = loaded
            fields = tuple(values[c] + gains[c // 2] * above[c] for c in range(4))

            def store():
                for c in range(2):
                    ts_out[c, k, rows, :] = fields[c]
                    uv_out[c, k, rows, :] = fields[c + 2]
                store_edge_rows(k, fields, block, blocks - 1, south_out, north_out)

            return (fields, pack_columns(acc, k, fields, lane)), store

        _, acc = loop(levels, load_down, downward, ((zero,) * 4, (zero,) * 4), DOWN_UNROLL)
        packed.append((rows, acc[:2], acc[2:]))
    if not final:
        parts, east, west = zip(*packed)
        write_messages(sent, south_out, north_out, (parts, east), west)


def last_kernel(rot_ref, value_ref, g1_ref, g2_ref, out_ref, field_ref, sems):
    levels = value_ref.shape[1]
    cosine, sine = turn_scalars(rot_ref[0, 0])
    step = DOWN_UNROLL
    above, copies = None, []
    for i in range(levels // step):
        group = range(i * step, (i + 1) * step)
        loaded = [([value_ref[c, k] for c in range(4)], (g1_ref[k], g2_ref[k])) for k in group]
        done = []
        for values, gains in loaded:
            if above is not None:
                values = [values[c] + gains[c // 2] * above[c] for c in range(4)]
            above = values
            u, v = values[2:]
            done.append((values[0], values[1], cosine * u + sine * v, cosine * v - sine * u))
        for k, fields in zip(group, done):
            for c in range(4):
                field_ref[c, k] = fields[c]
        part = pl.ds(i * step, step)
        copy = pltpu.make_async_copy(field_ref.at[:, part], out_ref.at[:, part], sems.at[i])
        copy.start()
        copies.append(copy)
    for copy in copies:
        copy.wait()


HIGHEST = lax.Precision.HIGHEST


def halving_order(count):
    bits = [1 << i for i in range(1, count.bit_length() - 1)]
    order = [0]
    for bit in reversed(bits):
        order = order + [place | bit for place in order]
    return order


def transform_kernel(count, norm, owner_ref, face_ref, row_table_ref, col_table_ref, *refs):
    parts, (keep_ref, send_ref, cells, table, inverse) = refs[: -5], refs[-5:]
    height, width = parts[0].shape[1:]
    here_y, here_x = lax.axis_index("ty"), lax.axis_index("tx")
    targets = owner_ref.shape[0]
    per_face = targets // NFACE

    def note(i, _):
        inverse[owner_ref[i]] = i
        return 0

    lax.fori_loop(0, targets, note, 0)
    for i, part in enumerate(parts):
        rows = pl.ds(pl.multiple_of((here_y ^ i) * height, TILE), height)
        for c in range(4):
            cells[rows, c * width : (c + 1) * width] = part[c]
    along_rows = jnp.dot(row_table_ref[...], cells[...], precision=HIGHEST, preferred_element_type=F32)
    stacked = jnp.concatenate([along_rows[:, c * width : (c + 1) * width] for c in range(4)], axis=0)
    columns = col_table_ref[pl.ds(pl.multiple_of(here_x * width, TILE), width), :]
    table[...] = norm * jnp.dot(stacked, columns, precision=HIGHEST, preferred_element_type=F32)
    size = table.shape[0] // per_face
    for i, place in enumerate(halving_order(count)):
        for ref, relative in ((keep_ref, place), (send_ref, place ^ 1)):
            tile = inverse[here_y * count + (here_x ^ relative)]
            start = pl.multiple_of(lax.rem(tile, per_face) * size, TILE)
            mine = lax.div(tile, per_face) == face_ref[0, 0]
            ref[i * size : (i + 1) * size, :] = jnp.where(mine, table[pl.ds(start, size), :], 0.0)


def call(kernel, outs, in_specs, scratch=(), out_specs=None, limit=4):
    many = isinstance(outs, (list, tuple))
    return pl.pallas_call(
        kernel,
        out_shape=outs,
        in_specs=in_specs,
        out_specs=out_specs or ([VMEM] * len(outs) if many else VMEM),
        scratch_shapes=list(scratch),
        compiler_params=pltpu.CompilerParams(vmem_limit_bytes=limit << 20),
    )


def swap(block, axis, bit):
    return lax.ppermute(block, axis, [(i, i ^ bit) for i in range(lax.axis_size(axis))])


def exchange(row_a, row_b, col_a, col_b):
    received = []
    for axis, first, second in (("ty", row_a, row_b), ("tx", col_a, col_b)):
        count = lax.axis_size(axis)
        others = [(i, (i + 1 if i % 2 else i - 1) % count) for i in range(count)]
        received += [swap(first, axis, 1), lax.ppermute(second, axis, others)]
    return received


def cosines(total, mode_count):
    phase = (2 * np.arange(total)[:, None] + 1) * np.arange(mode_count)[None, :] % (4 * total)
    return np.cos(phase * (math.pi / (2 * total)))


def body(adjoint, background_flow, vert_diff, wet_levels, rotation, face_map, ctrl_owner):
    _, levels, height, width = adjoint.shape
    ty, tx = lax.axis_size("ty"), lax.axis_size("tx")
    rows_total, cols_total = height * ty, width * tx
    full = shape(levels, height, width)
    pair = shape(2, levels, height, width)
    messages = [shape(levels, TILE, width)] * 2 + [shape(2, height, LANES)] * 2
    rows_scratch = [pltpu.VMEM((levels, TILE, width), F32)] * 2
    halo_scratch = rows_scratch + [pltpu.VMEM((2, height, LANES), F32)] * 2
    whole_scratch = pltpu.VMEM((4, levels, height, width), F32)

    places = np.arange(rows_total)
    coriolis = CORIOLIS_PEAK * np.sin(math.pi * (places + 0.5) / rows_total - 0.5 * math.pi)
    coriolis = jnp.asarray(np.repeat(coriolis[:, None], width, axis=1), F32)
    row_table = jnp.asarray(cosines(rows_total, KY).T, F32)
    col_table = jnp.asarray(cosines(cols_total, KX), F32)
    norm = math.sqrt(2.0 * NFACE / (rows_total * cols_total))

    ts, uv, *sent = call(
        prep_kernel,
        [pair, pair] + messages,
        [SMEM, ANY],
        [pltpu.VMEM((2, levels, height, width), F32)] + rows_scratch + [pltpu.SemaphoreType.DMA((2 * levels // PREP_UNROLL,))],
        limit=6,
    )(rotation, adjoint)
    received = exchange(*sent)
    w1, w2, h1, h2, g1, g2 = call(factor_kernel, [full] * 6, [VMEM] * 2)(vert_diff, wet_levels)
    ts, uv, first, *sent = call(
        functools.partial(step_kernel, False),
        [pair, pair, shape(2, height, width)] + messages,
        [VMEM] * 14,
        [whole_scratch] + rows_scratch + halo_scratch,
        limit=12,
    )(ts, uv, background_flow, w1, w2, h1, h2, g1, g2, coriolis, *received)
    received = exchange(*sent)
    values, surfaces = call(
        functools.partial(step_kernel, True),
        [shape(4, levels, height, width), shape(4, height, width)],
        [VMEM] * 13,
        halo_scratch,
        limit=8,
    )(ts, uv, background_flow, w1, w2, h1, h2, coriolis, *received, first)
    parts = [surfaces] + [swap(surfaces, "ty", bit) for bit in range(1, ty)]
    adjoint_out = call(
        last_kernel,
        shape(*adjoint.shape),
        [SMEM] + [VMEM] * 3,
        [whole_scratch, pltpu.SemaphoreType.DMA((levels // DOWN_UNROLL,))],
        out_specs=ANY,
        limit=8,
    )(rotation, values, g1, g2)
    size = 4 * KY * NFACE // ctrl_owner.shape[0]
    keep, send = call(
        functools.partial(transform_kernel, tx, norm),
        [shape(size * tx // 2, KX)] * 2,
        [SMEM] * 2 + [VMEM] * (ty + 2),
        [pltpu.VMEM((rows_total, 4 * width), F32), pltpu.VMEM((4 * KY, KX), F32), pltpu.SMEM(ctrl_owner.shape, jnp.int32)],
        limit=6,
    )(ctrl_owner, face_map, row_table, col_table, *parts)
    bit = 1
    while True:
        keep = keep + swap(send, "tx", bit)
        bit *= 2
        if bit == tx:
            break
        half = keep.shape[0] // 2
        keep, send = keep[:half], keep[half:]
    return adjoint_out, keep.reshape(1, -1)


def solution(mesh):
    return jax.shard_map(
        body,
        mesh=mesh,
        in_specs=(
            P(None, None, "ty", "tx"),
            P(None, None, "ty", "tx"),
            P(None, "ty", "tx"),
            P("ty", "tx"),
            P("ty", "tx"),
            P("ty", "tx"),
            P(),
        ),
        out_specs=(P(None, None, "ty", "tx"), P(("ty", "tx"), None)),
        check_vma=False,
    )
```

time: 83.2 us -> 64.7 us (0.78)
  starting transfers between devices: 33.7 us -> 23.1 us
  local copies, waits for them, and re-layouts: 8.67 us -> 2.37 us
  waiting for transfers between devices: 7.96 us -> 11.7 us
  Pallas kernels: 27.2 us -> 24.7 us
  other arithmetic: 3.14 us -> 0.64 us
    ppermute x21 -> x14, starting transfers between devices: 33.7 us -> 23.1 us  [the longest x10 13.7 us: swap(): lax.ppermute(block, axis, [(i, i ^ bit) for i in range(lax.axis_size(axis...]
    unnamed x20 -> x16, local copies, waits for them, and re-layouts: 8.52 us -> 2.36 us
    ppermute x21 -> x14, waiting for transfers between devices: 7.96 us -> 11.7 us  [the longest x10 7.54 us: swap(): lax.ppermute(block, axis, [(i, i ^ bit) for i in range(lax.axis_size(axis...]
    pallas_call x6, Pallas kernels: 27.2 us -> 24.7 us  [the longest x1 9.15 us: body(): call(functools.partial(step_kernel, False), [pair, pair, shape(2, height,...]
    cos x2 -> x0, other arithmetic: 2.16 us -> none  [cosine_table(): return jnp.cos(phase_index.astype(F32) * (math.pi / (2 * row_total)))]
  transfers between devices with their start and end apart: 21 -> 14, of which waited for: 7 -> 9; matrix products, arithmetic and copies ran while one was open for 3% -> 0% of each run, Pallas kernels for 15% -> 5%
where the time goes in v3:
time: 64.7 us; the launch traced here: 64.6 us
  Pallas kernels  24.7 us (38%)
  starting transfers between devices  23.1 us (36%)
  waiting for transfers between devices  11.7 us (18%)
  local copies, waits for them, and re-layouts  2.37 us (4%)
  between operations  2.05 us (3%)
    ppermute x10, starting transfers between devices, swap(): lax.ppermute(block, axis, [(i, i ^ bit) for i in range(lax.axis_size(axis...  13.7 us
    ppermute x4, starting transfers between devices, exchange(): received += [swap(first, axis, 1), lax.ppermute(second, axis, others)]  9.39 us
    pallas_call x1, Pallas kernels, body(): call(functools.partial(step_kernel, False), [pair, pair, shape(2, height,...  9.15 us
    ppermute x10, waiting for transfers between devices, swap(): lax.ppermute(block, axis, [(i, i ^ bit) for i in range(lax.axis_size(axis...  7.54 us
    pallas_call x1, Pallas kernels, body(): call(functools.partial(step_kernel, True), [shape(4, levels, height, widt...  6.8 us
    ppermute x4, waiting for transfers between devices, exchange(): received += [swap(first, axis, 1), lax.ppermute(second, axis, others)]  4.12 us
    pallas_call x1, Pallas kernels, body(): call(prep_kernel, [pair, pair] + messages, [SMEM, ANY], [pltpu.VMEM((2, l...  3.61 us
    unnamed x16, local copies, waits for them, and re-layouts  2.36 us
  transfers between devices with their start and end apart: 14, of which 9 were waited for; matrix products, arithmetic and copies ran while one was open for 0% of the time, Pallas kernels for 5%

profile of v3, /device:TPU:0, one launch (start us, length us, event | category | flops | bytes accessed | tf_op | source)
XLA Modules:
  0.0 64.6 jit_solution(5709356125890853432)
XLA Ops:
  1.3 2.3 %copy-done.1 = f32[4,36,64,128]{3,2,1,0:T(8,128)S(1)} copy-done((f32[4,36,64,128]{3,2,1,0:T(8,128)S(1)}, f32[4,36,64,128]{3,2,1,0:T(8,128)}, u32[]{:S(2)}) %copy-start.1) | copy-done | bytes 4718616
  3.6 3.6 %shard_map.113 = (f32[2,36,64,128]{3,2,1,0:T(8,128)S(1)}, f32[2,36,64,128]{3,2,1,0:T(8,128)S(1)}, f32[36,8,128]{2,1,0:T(8,128)S(1)}, f32[36,8,128]{2,1,0:T(8,128...) custom-call(s32[1,1]{1,0:T(1,128)S(6)} %copy.12.rot_ref, f32[4,36,64,128]{3,2,1,0:T(8,128)S(1)} %copy-done.1), custom_call_target="tpu_custom_call" | custom-call | tf_op jit(solution)/shard_map/pallas_call | solution.py:438
  7.2 3.0 %collective-permute-start = (f32[36,8,128]{2,1,0:T(8,128)S(1)}, f32[36,8,128]{2,1,0:T(8,128)S(1)}, u32[]{:S(2)}, u32[]{:S(2)}) collective-permute-start(f32[36,8,128]{2,1,0:T(8,128)S(1)} %get-tuple-element.33), channel_id=1, source_target_pairs={{0,8},{8,0},{16,24},{24,16},{1,9},{9,1},{17,25},{25,17},{2,10},{10... | collective-permute-start | bytes 442376 | tf_op jit(solution)/shard_map/ppermute | solution.py:403
  10.2 1.5 %collective-permute-start.1 = (f32[36,8,128]{2,1,0:T(8,128)S(1)}, f32[36,8,128]{2,1,0:T(8,128)S(1)}, u32[]{:S(2)}, u32[]{:S(2)}) collective-permute-start(f32[36,8,128]{2,1,0:T(8,128)S(1)} %get-tuple-element.34), channel_id=1, source_target_pairs={{0,24},{8,16},{16,8},{24,0},{1,25},{9,17},{17,9},{25,1},{2,26},{10... | collective-permute-start | bytes 442376 | tf_op jit(solution)/shard_map/ppermute | solution.py:411
  11.7 0.0 collective-permute-start.2
  11.7 3.7 %collective-permute-start.3 = (f32[2,64,128]{2,1,0:T(8,128)S(1)}, f32[2,64,128]{2,1,0:T(8,128)S(1)}, u32[]{:S(2)}, u32[]{:S(2)}) collective-permute-start(f32[2,64,128]{2,1,0:T(8,128)S(1)} %get-tuple-element.36), channel_id=1, source_target_pairs={{0,7},{1,2},{2,1},{3,4},{4,3},{5,6},{6,5},{7,0},{8,15},{9,10},{10,... | collective-permute-start | bytes 196616 | tf_op jit(solution)/shard_map/ppermute | solution.py:411
  15.5 1.2 %shard_map.114 = (f32[36,64,128]{2,1,0:T(8,128)S(1)}, f32[36,64,128]{2,1,0:T(8,128)S(1)}, f32[36,64,128]{2,1,0:T(8,128)S(1)}, f32[36,64,128]{2,1,0:T(8,128)S(1)}...) custom-call(f32[36,64,128]{2,1,0:T(8,128)S(1)} %copy-done.2, s32[64,128]{1,0:T(8,128)S(1)} %copy-done.6), custom_call_target="tpu_custom_call" | custom-call | tf_op jit(solution)/shard_map/pallas_call | solution.py:446
  16.7 0.0 collective-permute-done.2.refs_12_
  16.7 0.8 %collective-permute-done.3.refs_13_ = f32[2,64,128]{2,1,0:T(8,128)S(1)} collective-permute-done((f32[2,64,128]{2,1,0:T(8,128)S(1)}, f32[2,64,128]{2,1,0:T(8,128)S(1)}, u32[]{:S(2)}, u32[]{:S(2)}) %collective-permute-start.3) | collective-permute-done | bytes 65568 | tf_op jit(solution)/shard_map/ppermute | solution.py:411
  17.5 0.0 collective-permute-done.refs_10_
  17.5 0.9 %collective-permute-done.1.refs_11_ = f32[36,8,128]{2,1,0:T(8,128)S(1)} collective-permute-done((f32[36,8,128]{2,1,0:T(8,128)S(1)}, f32[36,8,128]{2,1,0:T(8,128)S(1)}, u32[]{:S(2)}, u32[]{:S(2)}) %collective-permute-start.1) | collective-permute-done | bytes 147488 | tf_op jit(solution)/shard_map/ppermute | solution.py:411
  18.5 9.1 %shard_map.115 = (f32[2,36,64,128]{3,2,1,0:T(8,128)S(1)}, f32[2,36,64,128]{3,2,1,0:T(8,128)S(1)}, f32[2,64,128]{2,1,0:T(8,128)S(1)}, f32[36,8,128]{2,1,0:T(8,128...) custom-call(f32[2,36,64,128]{3,2,1,0:T(8,128)S(1)} %get-tuple-element.25.refs_0_, ...), custom_call_target="tpu_custom_call" | custom-call | tf_op jit(solution)/shard_map/pallas_call | solution.py:447
  27.6 1.6 %collective-permute-start.4 = (f32[36,8,128]{2,1,0:T(8,128)S(1)}, f32[36,8,128]{2,1,0:T(8,128)S(1)}, u32[]{:S(2)}, u32[]{:S(2)}) collective-permute-start(f32[36,8,128]{2,1,0:T(8,128)S(1)} %get-tuple-element.39), channel_id=1, source_target_pairs={{0,8},{8,0},{16,24},{24,16},{1,9},{9,1},{17,25},{25,17},{2,10},{10... | collective-permute-start | bytes 442376 | tf_op jit(solution)/shard_map/ppermute | solution.py:403
  29.2 0.2 collective-permute-start.5
  29.4 4.0 %collective-permute-start.7 = (f32[2,64,128]{2,1,0:T(8,128)S(1)}, f32[2,64,128]{2,1,0:T(8,128)S(1)}, u32[]{:S(2)}, u32[]{:S(2)}) collective-permute-start(f32[2,64,128]{2,1,0:T(8,128)S(1)} %get-tuple-element.42), channel_id=1, source_target_pairs={{0,7},{1,2},{2,1},{3,4},{4,3},{5,6},{6,5},{7,0},{8,15},{9,10},{10,... | collective-permute-start | bytes 196616 | tf_op jit(solution)/shard_map/ppermute | solution.py:411
  33.4 2.1 %collective-permute-done.7.refs_11_ = f32[2,64,128]{2,1,0:T(8,128)S(1)} collective-permute-done((f32[2,64,128]{2,1,0:T(8,128)S(1)}, f32[2,64,128]{2,1,0:T(8,128)S(1)}, u32[]{:S(2)}, u32[]{:S(2)}) %collective-permute-start.7) | collective-permute-done | bytes 65568 | tf_op jit(solution)/shard_map/ppermute | solution.py:411
  35.4 0.3 collective-permute-done.5.refs_9_
  35.7 6.8 %shard_map.116 = (f32[4,36,64,128]{3,2,1,0:T(8,128)S(1)}, f32[4,64,128]{2,1,0:T(8,128)S(1)}) custom-call(f32[2,36,64,128]{3,2,1,0:T(8,128)S(1)} %get-tuple-element.37.refs_0_, f32[2,36,64,128]{3,2,1,0:T(8,128)S(1)} %get-tuple-element.38.refs_1_, f32[2,36,64,128]{3,2,1,0:T(8,128)S(1)} %copy-done, f32[36,64,128]{2,1,0:T(8,128)S(1)} %get-tuple-element.27.refs_3_, ...), custom_call_target="tpu_custom_call" | custom-call | tf_op jit(solution)/shard_map/pallas_call | solution.py:455
  42.5 2.3 %collective-permute-start.10 = (f32[4,64,128]{2,1,0:T(8,128)S(1)}, f32[4,64,128]{2,1,0:T(8,128)S(1)}, u32[]{:S(2)}, u32[]{:S(2)}) collective-permute-start(f32[4,64,128]{2,1,0:T(8,128)S(1)} %get-tuple-element.45.refs_0_), channel_id=1, source_target_pairs={{0,24},{8,16},{16,8},{24,0},{1,25},{9,17},{17,9},{25,1},{2,26},{10... | collective-permute-start | bytes 393224 | tf_op jit(solution)/shard_map/ppermute | solution.py:403
  44.8 0.5 collective-permute-start.8
  45.4 0.7 %collective-permute-start.9 = (f32[4,64,128]{2,1,0:T(8,128)S(1)}, f32[4,64,128]{2,1,0:T(8,128)S(1)}, u32[]{:S(2)}, u32[]{:S(2)}) collective-permute-start(f32[4,64,128]{2,1,0:T(8,128)S(1)} %get-tuple-element.45.refs_0_), channel_id=1, source_target_pairs={{0,16},{8,24},{16,0},{24,8},{1,17},{9,25},{17,1},{25,9},{2,18},{10... | collective-permute-start | bytes 393224 | tf_op jit(solution)/shard_map/ppermute | solution.py:403
  46.8 2.4 %collective-permute-done.10.refs_3_ = f32[4,64,128]{2,1,0:T(8,128)S(1)} collective-permute-done((f32[4,64,128]{2,1,0:T(8,128)S(1)}, f32[4,64,128]{2,1,0:T(8,128)S(1)}, u32[]{:S(2)}, u32[]{:S(2)}) %collective-permute-start.10) | collective-permute-done | bytes 131104 | tf_op jit(solution)/shard_map/ppermute | solution.py:403
  49.1 1.1 %collective-permute-done.8.refs_1_ = f32[4,64,128]{2,1,0:T(8,128)S(1)} collective-permute-done((f32[4,64,128]{2,1,0:T(8,128)S(1)}, f32[4,64,128]{2,1,0:T(8,128)S(1)}, u32[]{:S(2)}, u32[]{:S(2)}) %collective-permute-start.8) | collective-permute-done | bytes 131104 | tf_op jit(solution)/shard_map/ppermute | solution.py:403
  50.2 0.3 collective-permute-done.9.refs_2_
  50.5 1.6 %shard_map.118 = (f32[256,128]{1,0:T(8,128)S(1)}, f32[256,128]{1,0:T(8,128)S(1)}) custom-call(s32[32]{0:T(128)S(1)} %copy-done.7, s32[1,1]{1,0:T(1,128)S(6)} %copy.13.face_ref, f32[128,256]{1,0:T(8,128)S(1)} %copy-done.5, f32[1024,128]{1,0:T(8,128)S(1)} %copy-done.4, f32[4,64,128]{2,1,0:T(8,128)S(1)} %get-tuple-element.45.refs_0_, ...), custom_call_target="tpu_custom_call" | custom-call | tf_op jit(solution)/shard_map/pallas_call | solution.py:472
  52.2 0.1 collective-permute-start.11
  52.3 1.3 %collective-permute-done.11 = f32[256,128]{1,0:T(8,128)S(1)} collective-permute-done((f32[256,128]{1,0:T(8,128)S(1)}, f32[256,128]{1,0:T(8,128)S(1)}, u32[]{:S(2)}, u32[]{:S(2)}) %collective-permute-start.11) | collective-permute-done | bytes 131104 | tf_op jit(solution)/shard_map/ppermute | solution.py:403
  53.7 2.1 %collective-permute-start.12 = (f32[128,128]{1,0:T(8,128)S(1)}, f32[128,128]{1,0:T(8,128)S(1)}, u32[]{:S(2)}, u32[]{:S(2)}) collective-permute-start(f32[128,128]{1,0:T(8,128)S(1)} %slice.17), channel_id=1, source_target_pairs={{0,2},{1,3},{2,0},{3,1},{4,6},{5,7},{6,4},{7,5},{8,10},{9,11},{10,... | collective-permute-start | bytes 196616 | tf_op jit(solution)/shard_map/ppermute | solution.py:403
  55.8 2.4 %collective-permute-done.12 = f32[128,128]{1,0:T(8,128)S(1)} collective-permute-done((f32[128,128]{1,0:T(8,128)S(1)}, f32[128,128]{1,0:T(8,128)S(1)}, u32[]{:S(2)}, u32[]{:S(2)}) %collective-permute-start.12) | collective-permute-done | bytes 65568 | tf_op jit(solution)/shard_map/ppermute | solution.py:403
  58.2 3.4 %collective-permute-start.13 = (f32[64,128]{1,0:T(8,128)S(1)}, f32[64,128]{1,0:T(8,128)S(1)}, u32[]{:S(2)}, u32[]{:S(2)}) collective-permute-start(f32[64,128]{1,0:T(8,128)S(1)} %slice.19), channel_id=1, source_target_pairs={{0,4},{1,5},{2,6},{3,7},{4,0},{5,1},{6,2},{7,3},{8,12},{9,13},{10,... | collective-permute-start | bytes 98312 | tf_op jit(solution)/shard_map/ppermute | solution.py:403
  61.6 2.3 %shard_map.117 = f32[4,36,64,128]{3,2,1,0:T(8,128)} custom-call(s32[1,1]{1,0:T(1,128)S(6)} %copy.12.rot_ref, f32[4,36,64,128]{3,2,1,0:T(8,128)S(1)} %get-tuple-element.44.value_ref, f32[36,64,128]{2,1,0:T(8,128)S(1)} %get-tuple-element.31.refs_7_.g1_ref, f32[36,64,128]{2,1,0:T(8,128)S(1)} %get-tuple-element.32.refs_8_.g2_ref), custom_call_target="tpu_custom_call" | custom-call | tf_op jit(solution)/shard_map/pallas_call | solution.py:463
  63.9 0.6 slice_add_fusion.1
  (23 shorter events, 0.1 us)
Async XLA Ops:
  1.3 2.3 %copy-start.1 = (f32[4,36,64,128]{3,2,1,0:T(8,128)S(1)}, f32[4,36,64,128]{3,2,1,0:T(8,128)}, u32[]{:S(2)}) copy-start(f32[4,36,64,128]{3,2,1,0:T(8,128)} %adj_ref.1) | copy-start | bytes 14155780
  3.6 11.8 %copy-start.2 = (f32[36,64,128]{2,1,0:T(8,128)S(1)}, f32[36,64,128]{2,1,0:T(8,128)}, u32[]{:S(2)}) copy-start(f32[36,64,128]{2,1,0:T(8,128)} %vd_ref.1) | copy-start | bytes 3538948
  3.6 11.8 %copy-start.6 = (s32[64,128]{1,0:T(8,128)S(1)}, s32[64,128]{1,0:T(8,128)}, u32[]{:S(2)}) copy-start(s32[64,128]{1,0:T(8,128)} %wet_ref.1) | copy-start | bytes 98308
  3.6 14.8 %copy-start = (f32[2,36,64,128]{3,2,1,0:T(8,128)S(1)}, f32[2,36,64,128]{3,2,1,0:T(8,128)}, u32[]{:S(2)}) copy-start(f32[2,36,64,128]{3,2,1,0:T(8,128)} %refs_2_.3) | copy-start | bytes 7077892
  3.6 14.8 %copy-start.3 = (f32[256,128]{1,0:T(8,128)S(1)}, f32[256,128]{1,0:T(8,128)}, u32[]{:S(2)}) copy-start(f32[256,128]{1,0:T(8,128)} %constant.6.clone.refs_9_.refs_7_) | copy-start | bytes 393220
  7.2 10.3 %collective-permute-start = (f32[36,8,128]{2,1,0:T(8,128)S(1)}, f32[36,8,128]{2,1,0:T(8,128)S(1)}, u32[]{:S(2)}, u32[]{:S(2)}) collective-permute-start(f32[36,8,128]{2,1,0:T(8,128)S(1)} %get-tuple-element.33), channel_id=1, source_target_pairs={{0,8},{8,0},{16,24},{24,16},{1,9},{9,1},{17,25},{25,17},{2,10},{10... | collective-permute-start | bytes 442376 | tf_op jit(solution)/shard_map/ppermute | solution.py:403
  10.2 8.2 %collective-permute-start.1 = (f32[36,8,128]{2,1,0:T(8,128)S(1)}, f32[36,8,128]{2,1,0:T(8,128)S(1)}, u32[]{:S(2)}, u32[]{:S(2)}) collective-permute-start(f32[36,8,128]{2,1,0:T(8,128)S(1)} %get-tuple-element.34), channel_id=1, source_target_pairs={{0,24},{8,16},{16,8},{24,0},{1,25},{9,17},{17,9},{25,1},{2,26},{10... | collective-permute-start | bytes 442376 | tf_op jit(solution)/shard_map/ppermute | solution.py:411
  11.7 4.9 %collective-permute-start.2 = (f32[2,64,128]{2,1,0:T(8,128)S(1)}, f32[2,64,128]{2,1,0:T(8,128)S(1)}, u32[]{:S(2)}, u32[]{:S(2)}) collective-permute-start(f32[2,64,128]{2,1,0:T(8,128)S(1)} %get-tuple-element.35), channel_id=1, source_target_pairs={{0,1},{1,0},{2,3},{3,2},{4,5},{5,4},{6,7},{7,6},{8,9},{9,8},{10,11... | collective-permute-start | bytes 196616 | tf_op jit(solution)/shard_map/ppermute | solution.py:403
  11.7 5.8 %collective-permute-start.3 = (f32[2,64,128]{2,1,0:T(8,128)S(1)}, f32[2,64,128]{2,1,0:T(8,128)S(1)}, u32[]{:S(2)}, u32[]{:S(2)}) collective-permute-start(f32[2,64,128]{2,1,0:T(8,128)S(1)} %get-tuple-element.36), channel_id=1, source_target_pairs={{0,7},{1,2},{2,1},{3,4},{4,3},{5,6},{6,5},{7,0},{8,15},{9,10},{10,... | collective-permute-start | bytes 196616 | tf_op jit(solution)/shard_map/ppermute | solution.py:411
  27.6 7.8 %collective-permute-start.4 = (f32[36,8,128]{2,1,0:T(8,128)S(1)}, f32[36,8,128]{2,1,0:T(8,128)S(1)}, u32[]{:S(2)}, u32[]{:S(2)}) collective-permute-start(f32[36,8,128]{2,1,0:T(8,128)S(1)} %get-tuple-element.39), channel_id=1, source_target_pairs={{0,8},{8,0},{16,24},{24,16},{1,9},{9,1},{17,25},{25,17},{2,10},{10... | collective-permute-start | bytes 442376 | tf_op jit(solution)/shard_map/ppermute | solution.py:403
  29.2 6.5 %collective-permute-start.5 = (f32[36,8,128]{2,1,0:T(8,128)S(1)}, f32[36,8,128]{2,1,0:T(8,128)S(1)}, u32[]{:S(2)}, u32[]{:S(2)}) collective-permute-start(f32[36,8,128]{2,1,0:T(8,128)S(1)} %get-tuple-element.40), channel_id=1, source_target_pairs={{0,24},{8,16},{16,8},{24,0},{1,25},{9,17},{17,9},{25,1},{2,26},{10... | collective-permute-start | bytes 442376 | tf_op jit(solution)/shard_map/ppermute | solution.py:411
  29.4 4.0 %collective-permute-start.6 = (f32[2,64,128]{2,1,0:T(8,128)S(1)}, f32[2,64,128]{2,1,0:T(8,128)S(1)}, u32[]{:S(2)}, u32[]{:S(2)}) collective-permute-start(f32[2,64,128]{2,1,0:T(8,128)S(1)} %get-tuple-element.41), channel_id=1, source_target_pairs={{0,1},{1,0},{2,3},{3,2},{4,5},{5,4},{6,7},{7,6},{8,9},{9,8},{10,11... | collective-permute-start | bytes 196616 | tf_op jit(solution)/shard_map/ppermute | solution.py:403
  29.4 6.0 %collective-permute-start.7 = (f32[2,64,128]{2,1,0:T(8,128)S(1)}, f32[2,64,128]{2,1,0:T(8,128)S(1)}, u32[]{:S(2)}, u32[]{:S(2)}) collective-permute-start(f32[2,64,128]{2,1,0:T(8,128)S(1)} %get-tuple-element.42), channel_id=1, source_target_pairs={{0,7},{1,2},{2,1},{3,4},{4,3},{5,6},{6,5},{7,0},{8,15},{9,10},{10,... | collective-permute-start | bytes 196616 | tf_op jit(solution)/shard_map/ppermute | solution.py:411
  35.7 14.8 %copy-start.4 = (f32[1024,128]{1,0:T(8,128)S(1)}, f32[1024,128]{1,0:T(8,128)}, u32[]{:S(2)}) copy-start(f32[1024,128]{1,0:T(8,128)} %constant.8.clone.col_table_ref) | copy-start | bytes 1572868
  35.7 14.8 %copy-start.5 = (f32[128,256]{1,0:T(8,128)S(1)}, f32[128,256]{1,0:T(8,128)}, u32[]{:S(2)}) copy-start(f32[128,256]{1,0:T(8,128)} %constant.7.clone.row_table_ref) | copy-start | bytes 393220
  35.7 14.8 %copy-start.7 = (s32[32]{0:T(128)S(1)}, s32[32]{0:T(128)}, u32[]{:S(2)}) copy-start(s32[32]{0:T(128)} %owner_ref.1) | copy-start | bytes 388
  42.5 6.6 %collective-permute-start.10 = (f32[4,64,128]{2,1,0:T(8,128)S(1)}, f32[4,64,128]{2,1,0:T(8,128)S(1)}, u32[]{:S(2)}, u32[]{:S(2)}) collective-permute-start(f32[4,64,128]{2,1,0:T(8,128)S(1)} %get-tuple-element.45.refs_0_), channel_id=1, source_target_pairs={{0,24},{8,16},{16,8},{24,0},{1,25},{9,17},{17,9},{25,1},{2,26},{10... | collective-permute-start | bytes 393224 | tf_op jit(solution)/shard_map/ppermute | solution.py:403
  44.8 5.4 %collective-permute-start.8 = (f32[4,64,128]{2,1,0:T(8,128)S(1)}, f32[4,64,128]{2,1,0:T(8,128)S(1)}, u32[]{:S(2)}, u32[]{:S(2)}) collective-permute-start(f32[4,64,128]{2,1,0:T(8,128)S(1)} %get-tuple-element.45.refs_0_), channel_id=1, source_target_pairs={{0,8},{8,0},{16,24},{24,16},{1,9},{9,1},{17,25},{25,17},{2,10},{10... | collective-permute-start | bytes 393224 | tf_op jit(solution)/shard_map/ppermute | solution.py:403
  45.4 5.2 %collective-permute-start.9 = (f32[4,64,128]{2,1,0:T(8,128)S(1)}, f32[4,64,128]{2,1,0:T(8,128)S(1)}, u32[]{:S(2)}, u32[]{:S(2)}) collective-permute-start(f32[4,64,128]{2,1,0:T(8,128)S(1)} %get-tuple-element.45.refs_0_), channel_id=1, source_target_pairs={{0,16},{8,24},{16,0},{24,8},{1,17},{9,25},{17,1},{25,9},{2,18},{10... | collective-permute-start | bytes 393224 | tf_op jit(solution)/shard_map/ppermute | solution.py:403
  52.2 1.4 %collective-permute-start.11 = (f32[256,128]{1,0:T(8,128)S(1)}, f32[256,128]{1,0:T(8,128)S(1)}, u32[]{:S(2)}, u32[]{:S(2)}) collective-permute-start(f32[256,128]{1,0:T(8,128)S(1)} %get-tuple-element.47), channel_id=1, source_target_pairs={{0,1},{1,0},{2,3},{3,2},{4,5},{5,4},{6,7},{7,6},{8,9},{9,8},{10,11... | collective-permute-start | bytes 393224 | tf_op jit(solution)/shard_map/ppermute | solution.py:403
  53.7 4.5 %collective-permute-start.12 = (f32[128,128]{1,0:T(8,128)S(1)}, f32[128,128]{1,0:T(8,128)S(1)}, u32[]{:S(2)}, u32[]{:S(2)}) collective-permute-start(f32[128,128]{1,0:T(8,128)S(1)} %slice.17), channel_id=1, source_target_pairs={{0,2},{1,3},{2,0},{3,1},{4,6},{5,7},{6,4},{7,5},{8,10},{9,11},{10,... | collective-permute-start | bytes 196616 | tf_op jit(solution)/shard_map/ppermute | solution.py:403
  58.2 5.7 %collective-permute-start.13 = (f32[64,128]{1,0:T(8,128)S(1)}, f32[64,128]{1,0:T(8,128)S(1)}, u32[]{:S(2)}, u32[]{:S(2)}) collective-permute-start(f32[64,128]{1,0:T(8,128)S(1)} %slice.19), channel_id=1, source_target_pairs={{0,4},{1,5},{2,6},{3,7},{4,0},{5,1},{6,2},{7,3},{8,12},{9,13},{10,... | collective-permute-start | bytes 98312 | tf_op jit(solution)/shard_map/ppermute | solution.py:403

commit v4 on v3

--- a/solution.py
+++ b/solution.py
@@ -31,7 +31,9 @@
 F32 = jnp.float32
 PREP_UNROLL = 6
 FACTOR_ROWS, FACTOR_UNROLL = 64, 2
-STEP_ROWS, UP_UNROLL, DOWN_UNROLL = 64, 4, 6
+UNROLLS = {16: (6, 9), 32: (4, 6)}
+DOWN_UNROLL = 6
+EDGE = 16
 
 
 def shape(*dims):
@@ -87,35 +89,65 @@
     for c in range(4):
         if block == 0:
             south_ref[k, 2 * c : 2 * c + 2, :] = fields[c][0:2, :]
-        if block == last:
+        if block == last or block is last:
             north_ref[k, 2 * c : 2 * c + 2, :] = fields[c][size - 2 : size, :]
 
 
-def write_messages(refs, south_ref, north_ref, east, west):
-    row_a, row_b, col_a, col_b = refs
-    even_y, even_x = lax.axis_index("ty") % 2 == 0, lax.axis_index("tx") % 2 == 0
+def write_rows(row_a, row_b, south_ref, north_ref):
+    even = lax.axis_index("ty") % 2 == 0
     south, north = south_ref[...], north_ref[...]
-    row_a[...] = jnp.where(even_y, north, south)
-    row_b[...] = jnp.where(even_y, south, north)
-    for rows, e, w in zip(east[0], east[1], west):
-        for g in range(2):
-            col_a[g, rows, :] = jnp.where(even_x, e[g], w[g])
-            col_b[g, rows, :] = jnp.where(even_x, w[g], e[g])
-
-
-def read_messages(refs, south_ref, north_ref, east_ref, west_ref):
-    row_a, row_b, col_a, col_b = (ref[...] for ref in refs)
+    row_a[...] = jnp.where(even, north, south)
+    row_b[...] = jnp.where(even, south, north)
+
+
+def write_columns(col_a, col_b, east, west):
+    even = lax.axis_index("tx") % 2 == 0
+    col_a[...] = jnp.where(even, east, west)
+    col_b[...] = jnp.where(even, west, east)
+
+
+def read_rows(row_a, row_b, south_ref, north_ref):
     here = lax.axis_index("ty")
-    even_y, even_x = here % 2 == 0, lax.axis_index("tx") % 2 == 0
-    south = jnp.where(even_y, row_b, row_a)
-    north = jnp.where(even_y, row_a, row_b)
-    south_ref[...] = jnp.where(here == 0, 0.0, south)
-    north_ref[...] = jnp.where(here == lax.axis_size("ty") - 1, 0.0, north)
-    east_ref[...] = jnp.where(even_x, col_a, col_b)
-    west_ref[...] = jnp.where(even_x, col_b, col_a)
-
-
-def prep_kernel(rot_ref, adj_ref, ts_ref, uv_ref, row_a, row_b, col_a, col_b, raw_ref, south_ref, north_ref, sems):
+    even = here % 2 == 0
+    first, second = row_a[...], row_b[...]
+    south_ref[...] = jnp.where(here == 0, 0.0, jnp.where(even, second, first))
+    north_ref[...] = jnp.where(here == lax.axis_size("ty") - 1, 0.0, jnp.where(even, first, second))
+
+
+def read_columns(col_a, col_b, east_ref, west_ref):
+    even = lax.axis_index("tx") % 2 == 0
+    first, second = col_a[...], col_b[...]
+    east_ref[...] = jnp.where(even, first, second)
+    west_ref[...] = jnp.where(even, second, first)
+
+
+def prep_rows_kernel(rot_ref, adj_ref, row_a, row_b, raw_ref, south_ref, north_ref, sems):
+    levels, height = adj_ref.shape[1], adj_ref.shape[2]
+    cosine, sine = turn_scalars(rot_ref[0, 0])
+    copies = []
+    for i, start in enumerate((0, height - TILE)):
+        copies.append(pltpu.make_async_copy(adj_ref.at[:, :, pl.ds(start, TILE)], raw_ref.at[i], sems.at[i]))
+        copies[-1].start()
+    for copy in copies:
+        copy.wait()
+
+    def load(k):
+        return [[raw_ref[i, c, k] for c in range(4)] for i in range(2)]
+
+    def level(k, loaded, carry):
+        rotated = [(t, s, cosine * a - sine * b, sine * a + cosine * b) for t, s, a, b in loaded]
+
+        def store():
+            store_edge_rows(k, rotated[0], 0, None, south_ref, north_ref)
+            store_edge_rows(k, rotated[1], None, None, south_ref, north_ref)
+
+        return carry, store
+
+    loop(levels, load, level, 0, 6)
+    write_rows(row_a, row_b, south_ref, north_ref)
+
+
+def prep_columns_kernel(rot_ref, adj_ref, ts_ref, uv_ref, col_a, col_b, raw_ref, sems):
     levels, height = adj_ref.shape[1], adj_ref.shape[2]
     cosine, sine = turn_scalars(rot_ref[0, 0])
     step = PREP_UNROLL
@@ -133,18 +165,17 @@
     for i in range(chunks):
         copies[2 * i].wait()
         copies[2 * i + 1].wait()
-        levels_here = range(i * step, (i + 1) * step)
-        loaded = [(ts_ref[0, k], ts_ref[1, k], raw_ref[0, k], raw_ref[1, k]) for k in levels_here]
+        group = range(i * step, (i + 1) * step)
+        loaded = [(ts_ref[0, k], ts_ref[1, k], raw_ref[0, k], raw_ref[1, k]) for k in group]
         stores = []
-        for k, (t, s, a, b) in zip(levels_here, loaded):
+        for k, (t, s, a, b) in zip(group, loaded):
             fields = (t, s, cosine * a - sine * b, sine * a + cosine * b)
             acc = pack_columns(acc, k, fields, lane)
             stores.append((k, fields))
         for k, fields in stores:
             uv_ref[0, k] = fields[2]
             uv_ref[1, k] = fields[3]
-            store_edge_rows(k, fields, 0, 0, south_ref, north_ref)
-    write_messages((row_a, row_b, col_a, col_b), south_ref, north_ref, ([pl.ds(0, height)], [acc[:2]]), [acc[2:]])
+    write_columns(col_a, col_b, jnp.stack(acc[:2]), jnp.stack(acc[2:]))
 
 
 def factor_kernel(vd_ref, wet_ref, w1_ref, w2_ref, h1_ref, h2_ref, g1_ref, g2_ref):
@@ -182,29 +213,43 @@
         loop(levels, load, level, (zero, (zero, zero)), FACTOR_UNROLL)
 
 
-def step_kernel(final, *refs):
-    ts_ref, uv_ref, flow_ref, w1_ref, w2_ref, h1_ref, h2_ref = refs[:7]
-    if final:
-        cor_ref, *messages = refs[7:12]
-        first_ref, value_ref, surface_ref = refs[12:15]
+def step_kernel(stage, blocks, *refs):
+    refs = list(refs)
+
+    def take(count):
+        taken, refs[:] = refs[:count], refs[count:]
+        return taken
+
+    ts_ref, uv_ref, flow_ref, w1_ref, w2_ref, h1_ref, h2_ref, cor_ref, col_a, col_b = take(10)
+    south_ref = north_ref = None
+    if stage != "middle":
+        row_a, row_b = take(2)
+    if stage == "up":
+        (first_ref,) = take(1)
+        value_ref, surface_ref = take(2)
         surface_ref[0:2] = first_ref[...]
-        surface_at = 2
     else:
-        g1_ref, g2_ref, cor_ref, *messages = refs[7:14]
-        ts_out, uv_out, surface_ref, *sent = refs[14:21]
-        value_ref, south_out, north_out = refs[21:24]
-        surface_at = 0
-    south_ref, north_ref, east_ref, west_ref = refs[-4:]
-    read_messages(messages, south_ref, north_ref, east_ref, west_ref)
+        g1_ref, g2_ref = take(2)
+        if stage == "middle":
+            ts_in, uv_in, surface_in, east_in, west_in = take(5)
+            ts_out, uv_out, surface_ref, east_out, west_out = take(5)
+        else:
+            ts_out, uv_out, surface_ref, east_out, west_out, sent_a, sent_b = take(7)
+            south_out, north_out = take(2)
+        (value_ref,) = take(1)
+    east_ref, west_ref = take(2)
+    read_columns(col_a, col_b, east_ref, west_ref)
+    if stage != "middle":
+        south_ref, north_ref = take(2)
+        read_rows(row_a, row_b, south_ref, north_ref)
     levels, height = ts_ref.shape[1], ts_ref.shape[2]
-    size = STEP_ROWS
-    blocks = height // size
-    lane, row = lanes_of(size), rows_of(size)
-    low_two, high_two = lane < 2, lane >= LANES - 2
-    low_one, high_one = lane < 1, lane >= LANES - 1
-    zero = jnp.zeros((size, LANES), F32)
     first_cor = pl.multiple_of(lax.axis_index("ty") * height, TILE)
-    packed = []
+    packed = {}
+    done, others = (), ()
+    if stage == "middle":
+        ((first_row, size),) = blocks
+        done = ((ts_in, ts_out), (uv_in, uv_out))
+        others = (pl.ds(0, first_row), pl.ds(first_row + size, height - first_row - size))
 
     def get(c, k, start):
         rows = pl.ds(start, TILE)
@@ -222,12 +267,18 @@
         halo = pltpu.roll(north, (TILE - over - 2 * c) % TILE, 0)
         return jnp.where(part >= TILE - over, halo, pltpu.roll(get(c, k, height - TILE), TILE - over, 0))
 
-    for block in range(blocks):
-        rows = pl.ds(block * size, size)
-        first_row = block * size
-        cor = cor_ref[pl.ds(first_cor + block * size, size), :]
-
-        def fetch(c, k, shift, halos, first_row=first_row):
+    for block, (first_row, size) in enumerate(blocks):
+        lane = lanes_of(size)
+        low_two, high_two = lane < 2, lane >= LANES - 2
+        low_one, high_one = lane < 1, lane >= LANES - 1
+        zero = jnp.zeros((size, LANES), F32)
+        rows = pl.ds(first_row, size)
+        kept_rows = rows if stage == "up" else pl.ds(0, size)
+        south_end, north_end = first_row == 0, first_row + size == height
+        cor = cor_ref[pl.ds(first_cor + first_row, size), :]
+        up_unroll, down_unroll = UNROLLS[min(size, 32)]
+
+        def fetch(c, k, shift, halos, first_row=first_row, size=size):
             start = first_row + shift
             if 0 <= start <= height - size:
                 part = pl.ds(start, size)
@@ -235,9 +286,9 @@
             lines = [line(c, k, start + i, halos) for i in range(0, size, TILE)]
             return lines[0] if len(lines) == 1 else jnp.concatenate(lines, axis=0)
 
-        def load_up(i, rows=rows, block=block, fetch=fetch):
+        def load_up(i, rows=rows, ends=(south_end, north_end), fetch=fetch):
             k = levels - 1 - i
-            halos = (south_ref[k] if block == 0 else None, north_ref[k] if block == blocks - 1 else None)
+            halos = (south_ref[k] if ends[0] else None, north_ref[k] if ends[1] else None)
             turn = LANES - 2 - 3 * k
             east = [pltpu.roll(east_ref[g, rows, :], turn, 1) for g in range(2)]
             west = [pltpu.roll(west_ref[g, rows, :], turn, 1) for g in range(2)]
@@ -246,7 +297,7 @@
             factors = [ref[k, rows, :] for ref in (w1_ref, w2_ref, h1_ref, h2_ref)]
             return east, west, lines, flow, factors
 
-        def upward(i, loaded, below, cor=cor, rows=rows):
+        def upward(i, loaded, below, cor=cor, rows=kept_rows):
             k = levels - 1 - i
             east, west, lines, flow, factors = loaded
             flow_x = flow[0] * (ADVECT_COEF / 12.0)
@@ -292,36 +343,61 @@
 
             return values, store
 
-        top = loop(levels, load_up, upward, (zero,) * 4, UP_UNROLL)
+        top = loop(levels, load_up, upward, (zero,) * 4, up_unroll)
         for c in range(2):
-            surface_ref[surface_at + c, rows, :] = top[c]
-        if final:
+            surface_ref[(2 if stage == "up" else 0) + c, rows, :] = top[c]
+        if stage == "up":
             continue
 
-        def load_down(k, rows=rows):
-            return [value_ref[c, k, rows, :] for c in range(4)], (g1_ref[k, rows, :], g2_ref[k, rows, :])
-
-        def downward(k, loaded, carry, rows=rows, block=block):
+        def load_down(k, rows=rows, kept_rows=kept_rows):
+            passed = [
+                (source, target, c, part, source[c, k, part, :])
+                for source, target in done
+                for c in range(2)
+                for part in others
+            ]
+            values = [value_ref[c, k, kept_rows, :] for c in range(4)]
+            return values, (g1_ref[k, rows, :], g2_ref[k, rows, :]), passed
+
+        def downward(k, loaded, carry, rows=rows, ends=(south_end, north_end), lane=lane):
             above, acc = carry
-            values, gains = loaded
+            values, gains, passed = loaded
             fields = tuple(values[c] + gains[c // 2] * above[c] for c in range(4))
 
             def store():
                 for c in range(2):
                     ts_out[c, k, rows, :] = fields[c]
                     uv_out[c, k, rows, :] = fields[c + 2]
-                store_edge_rows(k, fields, block, blocks - 1, south_out, north_out)
+                for _, target, c, part, value in passed:
+                    target[c, k, part, :] = value
+                if ends[0] or ends[1]:
+                    store_edge_rows(k, fields, 0 if ends[0] else 1, 1 if ends[1] else 2, south_out, north_out)
 
             return (fields, pack_columns(acc, k, fields, lane)), store
 
-        _, acc = loop(levels, load_down, downward, ((zero,) * 4, (zero,) * 4), DOWN_UNROLL)
-        packed.append((rows, acc[:2], acc[2:]))
-    if not final:
-        parts, east, west = zip(*packed)
-        write_messages(sent, south_out, north_out, (parts, east), west)
-
-
-def last_kernel(rot_ref, value_ref, g1_ref, g2_ref, out_ref, field_ref, sems):
+        _, acc = loop(levels, load_down, downward, ((zero,) * 4, (zero,) * 4), down_unroll)
+        packed[first_row] = acc
+    if stage == "edge":
+        for (first_row, size), acc in zip(blocks, packed.values()):
+            for g in range(2):
+                east_out[g, pl.ds(first_row, size), :] = acc[g]
+                west_out[g, pl.ds(first_row, size), :] = acc[g + 2]
+        write_rows(sent_a, sent_b, south_out, north_out)
+    if stage == "middle":
+        for c in range(2):
+            for part in others:
+                surface_ref[c, part, :] = surface_in[c, part, :]
+        acc = packed[first_row]
+        spans = (slice(0, first_row), slice(first_row + size, height))
+        east, west = (
+            jnp.stack([jnp.concatenate([ref[g, spans[0], :], acc[g + at], ref[g, spans[1], :]], axis=0) for g in range(2)])
+            for ref, at in ((east_in, 0), (west_in, 2))
+        )
+        write_columns(east_out, west_out, east, west)
+
+
+def last_kernel(rot_ref, value_ref, g1_ref, g2_ref, out_ref, token_ref, field_ref, sems):
+    token_ref[...] = jnp.zeros_like(token_ref)
     levels = value_ref.shape[1]
     cosine, sine = turn_scalars(rot_ref[0, 0])
     step = DOWN_UNROLL
@@ -358,7 +434,7 @@
     return order
 
 
-def transform_kernel(count, norm, owner_ref, face_ref, row_table_ref, col_table_ref, *refs):
+def transform_kernel(count, norm, owner_ref, face_ref, row_table_ref, col_table_ref, _, *refs):
     parts, (keep_ref, send_ref, cells, table, inverse) = refs[: -5], refs[-5:]
     height, width = parts[0].shape[1:]
     here_y, here_x = lax.axis_index("ty"), lax.axis_index("tx")
@@ -387,14 +463,15 @@
             ref[i * size : (i + 1) * size, :] = jnp.where(mine, table[pl.ds(start, size), :], 0.0)
 
 
-def call(kernel, outs, in_specs, scratch=(), out_specs=None, limit=4):
-    many = isinstance(outs, (list, tuple))
+def call(kernel, outs, in_specs, scratch=(), out_specs=None, limit=4, aliases=None, work=0):
     return pl.pallas_call(
         kernel,
         out_shape=outs,
         in_specs=in_specs,
-        out_specs=out_specs or ([VMEM] * len(outs) if many else VMEM),
+        out_specs=out_specs or [VMEM] * len(outs),
         scratch_shapes=list(scratch),
+        input_output_aliases=aliases or {},
+        cost_estimate=pl.CostEstimate(flops=work, transcendentals=0, bytes_accessed=work) if work else None,
         compiler_params=pltpu.CompilerParams(vmem_limit_bytes=limit << 20),
     )
 
@@ -403,13 +480,10 @@
     return lax.ppermute(block, axis, [(i, i ^ bit) for i in range(lax.axis_size(axis))])
 
 
-def exchange(row_a, row_b, col_a, col_b):
-    received = []
-    for axis, first, second in (("ty", row_a, row_b), ("tx", col_a, col_b)):
-        count = lax.axis_size(axis)
-        others = [(i, (i + 1 if i % 2 else i - 1) % count) for i in range(count)]
-        received += [swap(first, axis, 1), lax.ppermute(second, axis, others)]
-    return received
+def exchange(axis, first, second):
+    count = lax.axis_size(axis)
+    others = [(i, (i + 1 if i % 2 else i - 1) % count) for i in range(count)]
+    return lax.ppermute(second, axis, others), swap(first, axis, 1)
 
 
 def cosines(total, mode_count):
@@ -423,10 +497,13 @@
     rows_total, cols_total = height * ty, width * tx
     full = shape(levels, height, width)
     pair = shape(2, levels, height, width)
-    messages = [shape(levels, TILE, width)] * 2 + [shape(2, height, LANES)] * 2
+    row_pair, col_pair = [shape(levels, TILE, width)] * 2, [shape(2, height, LANES)] * 2
     rows_scratch = [pltpu.VMEM((levels, TILE, width), F32)] * 2
-    halo_scratch = rows_scratch + [pltpu.VMEM((2, height, LANES), F32)] * 2
-    whole_scratch = pltpu.VMEM((4, levels, height, width), F32)
+    cols_scratch = [pltpu.VMEM((2, height, LANES), F32)] * 2
+    state = [pair, pair, shape(2, height, width)]
+
+    def kept(rows):
+        return pltpu.VMEM((4, levels, rows, width), F32)
 
     places = np.arange(rows_total)
     coriolis = CORIOLIS_PEAK * np.sin(math.pi * (places + 0.5) / rows_total - 0.5 * math.pi)
@@ -435,47 +512,66 @@
     col_table = jnp.asarray(cosines(cols_total, KX), F32)
     norm = math.sqrt(2.0 * NFACE / (rows_total * cols_total))
 
-    ts, uv, *sent = call(
-        prep_kernel,
-        [pair, pair] + messages,
+    dma = pltpu.SemaphoreType.DMA
+    adjoint = pltpu.with_memory_space_constraint(adjoint, pltpu.HBM)
+    edge_raw = pltpu.VMEM((2, 4, levels, TILE, width), F32)
+    rows = call(prep_rows_kernel, row_pair, [SMEM, ANY], [edge_raw] + rows_scratch + [dma((2,))])(rotation, adjoint)
+    row_b, row_a = exchange("ty", *rows)
+    ts, uv, *cols = call(
+        prep_columns_kernel,
+        [pair, pair] + col_pair,
         [SMEM, ANY],
-        [pltpu.VMEM((2, levels, height, width), F32)] + rows_scratch + [pltpu.SemaphoreType.DMA((2 * levels // PREP_UNROLL,))],
+        [pltpu.VMEM((2, levels, height, width), F32), dma((2 * levels // PREP_UNROLL,))],
         limit=6,
+        work=1 << 23,
     )(rotation, adjoint)
-    received = exchange(*sent)
-    w1, w2, h1, h2, g1, g2 = call(factor_kernel, [full] * 6, [VMEM] * 2)(vert_diff, wet_levels)
-    ts, uv, first, *sent = call(
-        functools.partial(step_kernel, False),
-        [pair, pair, shape(2, height, width)] + messages,
+    col_b, col_a = exchange("tx", *cols)
+    w1, w2, h1, h2, g1, g2 = call(factor_kernel, [full] * 6, [VMEM] * 2, work=1 << 22)(vert_diff, wet_levels)
+    edge_blocks = ((0, EDGE), (height - EDGE, EDGE))
+    middle = height - 2 * EDGE
+    ts1, uv1, first, east, west, *rows = call(
+        functools.partial(step_kernel, "edge", edge_blocks),
+        state + col_pair + row_pair,
         [VMEM] * 14,
-        [whole_scratch] + rows_scratch + halo_scratch,
-        limit=12,
-    )(ts, uv, background_flow, w1, w2, h1, h2, g1, g2, coriolis, *received)
-    received = exchange(*sent)
+        rows_scratch + [kept(EDGE)] + cols_scratch + rows_scratch,
+        limit=8,
+    )(ts, uv, background_flow, w1, w2, h1, h2, coriolis, col_a, col_b, row_a, row_b, g1, g2)
+    row_b, row_a = exchange("ty", *rows)
+    ts, uv, first, *cols = call(
+        functools.partial(step_kernel, "middle", ((EDGE, middle),)),
+        state + col_pair,
+        [VMEM] * 17,
+        [kept(middle)] + cols_scratch,
+        limit=8,
+        aliases={12: 0, 13: 1, 14: 2},
+        work=1 << 24,
+    )(ts, uv, background_flow, w1, w2, h1, h2, coriolis, col_a, col_b, g1, g2, ts1, uv1, first, east, west)
+    col_b, col_a = exchange("tx", *cols)
     values, surfaces = call(
-        functools.partial(step_kernel, True),
+        functools.partial(step_kernel, "up", ((0, height),)),
         [shape(4, levels, height, width), shape(4, height, width)],
         [VMEM] * 13,
-        halo_scratch,
+        cols_scratch + rows_scratch,
         limit=8,
-    )(ts, uv, background_flow, w1, w2, h1, h2, coriolis, *received, first)
+    )(ts, uv, background_flow, w1, w2, h1, h2, coriolis, col_a, col_b, row_a, row_b, first)
     parts = [surfaces] + [swap(surfaces, "ty", bit) for bit in range(1, ty)]
-    adjoint_out = call(
+    adjoint_out, token = call(
         last_kernel,
-        shape(*adjoint.shape),
+        [shape(*adjoint.shape), shape(TILE, LANES)],
         [SMEM] + [VMEM] * 3,
-        [whole_scratch, pltpu.SemaphoreType.DMA((levels // DOWN_UNROLL,))],
-        out_specs=ANY,
+        [kept(height), dma((levels // DOWN_UNROLL,))],
+        out_specs=[ANY, VMEM],
         limit=8,
+        work=1 << 23,
     )(rotation, values, g1, g2)
     size = 4 * KY * NFACE // ctrl_owner.shape[0]
     keep, send = call(
         functools.partial(transform_kernel, tx, norm),
         [shape(size * tx // 2, KX)] * 2,
-        [SMEM] * 2 + [VMEM] * (ty + 2),
+        [SMEM] * 2 + [VMEM] * (ty + 3),
         [pltpu.VMEM((rows_total, 4 * width), F32), pltpu.VMEM((4 * KY, KX), F32), pltpu.SMEM(ctrl_owner.shape, jnp.int32)],
         limit=6,
-    )(ctrl_owner, face_map, row_table, col_table, *parts)
+    )(ctrl_owner, face_map, row_table, col_table, token, *parts)
     bit = 1
     while True:
         keep = keep + swap(send, "tx", bit)

time: 64.7 us -> 63.5 us (0.981)
  starting transfers between devices: 23.1 us -> 19.1 us
  waiting for transfers between devices: 11.7 us -> 14.3 us
  Pallas kernels: 24.7 us -> 27.1 us
  local copies, waits for them, and re-layouts: 2.37 us -> 0.05 us
    ppermute x10, starting transfers between devices: 13.7 us -> 10.2 us  [swap(): lax.ppermute(block, axis, [(i, i ^ bit) for i in range(lax.axis_size(axis...]
    ppermute x10, waiting for transfers between devices: 7.54 us -> 10.2 us  [swap(): lax.ppermute(block, axis, [(i, i ^ bit) for i in range(lax.axis_size(axis...]
    pallas_call x5 -> x7, Pallas kernels: 23.1 us -> 25.5 us  [the longest x1 6.8 us: body(): call(functools.partial(step_kernel, 'up', ((0, height),)), [shape(4, leve...]
    unnamed x16 -> x14, local copies, waits for them, and re-layouts: 2.36 us -> 0.03 us
  transfers between devices with their start and end apart: 14 -> 14, of which waited for: 9 -> 7; matrix products, arithmetic and copies ran while one was open for 0% -> 0% of each run, Pallas kernels for 5% -> 19%
where the time goes in v4:
time: 63.5 us; the launch traced here: 63.3 us
  Pallas kernels  27.1 us (43%)
  starting transfers between devices  19.1 us (30%)
  waiting for transfers between devices  14.3 us (23%)
  between operations  2.11 us (3%)
  other arithmetic  0.64 us (1%)
    ppermute x10, starting transfers between devices, swap(): lax.ppermute(block, axis, [(i, i ^ bit) for i in range(lax.axis_size(axis...  10.2 us
    ppermute x10, waiting for transfers between devices, swap(): lax.ppermute(block, axis, [(i, i ^ bit) for i in range(lax.axis_size(axis...  10.2 us
    ppermute x4, starting transfers between devices, exchange(): return (lax.ppermute(second, axis, others), swap(first, axis, 1))  8.95 us
    pallas_call x1, Pallas kernels, body(): call(functools.partial(step_kernel, 'up', ((0, height),)), [shape(4, leve...  6.8 us
    pallas_call x1, Pallas kernels, body(): call(functools.partial(step_kernel, 'edge', edge_blocks), state + col_pai...  5.2 us
    pallas_call x1, Pallas kernels, body(): call(functools.partial(step_kernel, 'middle', ((EDGE, middle),)), state +...  5.06 us
    ppermute x4, waiting for transfers between devices, exchange(): return (lax.ppermute(second, axis, others), swap(first, axis, 1))  4.09 us
    pallas_call x1, Pallas kernels, body(): call(prep_columns_kernel, [pair, pair] + col_pair, [SMEM, ANY], [pltpu.VM...  3.46 us
  transfers between devices with their start and end apart: 14, of which 7 were waited for; matrix products, arithmetic and copies ran while one was open for 0% of the time, Pallas kernels for 19%

profile of v4, /device:TPU:0, one launch (start us, length us, event | category | flops | bytes accessed | tf_op | source)
XLA Modules:
  0.0 63.3 jit_solution(997864512789088278)
XLA Ops:
  1.3 1.4 %shard_map.115 = (f32[36,8,128]{2,1,0:T(8,128)S(1)}, f32[36,8,128]{2,1,0:T(8,128)S(1)}) custom-call(s32[1,1]{1,0:T(1,128)S(6)} %copy.18.rot_ref, f32[4,36,64,128]{3,2,1,0:T(8,128)} %adj_ref.3), custom_call_target="tpu_custom_call" | custom-call | tf_op jit(solution)/shard_map/pallas_call | solution.py:518
  2.7 3.0 %collective-permute-start.2 = (f32[36,8,128]{2,1,0:T(8,128)S(1)}, f32[36,8,128]{2,1,0:T(8,128)S(1)}, u32[]{:S(2)}, u32[]{:S(2)}) collective-permute-start(f32[36,8,128]{2,1,0:T(8,128)S(1)} %get-tuple-element.42), channel_id=1, source_target_pairs={{0,8},{8,0},{16,24},{24,16},{1,9},{9,1},{17,25},{25,17},{2,10},{10... | collective-permute-start | bytes 442376 | tf_op jit(solution)/shard_map/ppermute | solution.py:480
  5.7 1.6 %collective-permute-start.3 = (f32[36,8,128]{2,1,0:T(8,128)S(1)}, f32[36,8,128]{2,1,0:T(8,128)S(1)}, u32[]{:S(2)}, u32[]{:S(2)}) collective-permute-start(f32[36,8,128]{2,1,0:T(8,128)S(1)} %get-tuple-element.43), channel_id=1, source_target_pairs={{0,24},{8,16},{16,8},{24,0},{1,25},{9,17},{17,9},{25,1},{2,26},{10... | collective-permute-start | bytes 442376 | tf_op jit(solution)/shard_map/ppermute | solution.py:486
  7.3 3.5 %shard_map.113 = (f32[2,36,64,128]{3,2,1,0:T(8,128)S(1)}, f32[2,36,64,128]{3,2,1,0:T(8,128)S(1)}, f32[2,64,128]{2,1,0:T(8,128)S(1)}, f32[2,64,128]{2,1,0:T(8,128)S(1)}) custom-call(s32[1,1]{1,0:T(1,128)S(6)} %copy.18.rot_ref, f32[4,36,64,128]{3,2,1,0:T(8,128)} %adj_ref.3), custom_call_target="tpu_custom_call" | custom-call | flops 8388608 | bytes 8388608 | tf_op jit(solution)/shard_map/pallas_call | solution.py:520
  10.7 0.1 collective-permute-start
  10.8 3.7 %collective-permute-start.1 = (f32[2,64,128]{2,1,0:T(8,128)S(1)}, f32[2,64,128]{2,1,0:T(8,128)S(1)}, u32[]{:S(2)}, u32[]{:S(2)}) collective-permute-start(f32[2,64,128]{2,1,0:T(8,128)S(1)} %get-tuple-element.39), channel_id=1, source_target_pairs={{0,7},{1,2},{2,1},{3,4},{4,3},{5,6},{6,5},{7,0},{8,15},{9,10},{10,... | collective-permute-start | bytes 196616 | tf_op jit(solution)/shard_map/ppermute | solution.py:486
  14.5 1.2 %shard_map.114 = (f32[36,64,128]{2,1,0:T(8,128)S(1)}, f32[36,64,128]{2,1,0:T(8,128)S(1)}, f32[36,64,128]{2,1,0:T(8,128)S(1)}, f32[36,64,128]{2,1,0:T(8,128)S(1)}...) custom-call(f32[36,64,128]{2,1,0:T(8,128)S(1)} %copy-done.2, s32[64,128]{1,0:T(8,128)S(1)} %copy-done.5), custom_call_target="tpu_custom_call" | custom-call | flops 4194304 | bytes 4194304 | tf_op jit(solution)/shard_map/pallas_call | solution.py:529
  15.7 0.8 %collective-permute-done.1.refs_9_ = f32[2,64,128]{2,1,0:T(8,128)S(1)} collective-permute-done((f32[2,64,128]{2,1,0:T(8,128)S(1)}, f32[2,64,128]{2,1,0:T(8,128)S(1)}, u32[]{:S(2)}, u32[]{:S(2)}) %collective-permute-start.1) | collective-permute-done | bytes 65568 | tf_op jit(solution)/shard_map/ppermute | solution.py:486
  16.6 5.2 %shard_map.116 = (f32[2,36,64,128]{3,2,1,0:T(8,128)S(1)}, f32[2,36,64,128]{3,2,1,0:T(8,128)S(1)}, f32[2,64,128]{2,1,0:T(8,128)S(1)}, f32[2,64,128]{2,1,0:T(8,128...) custom-call(f32[2,36,64,128]{3,2,1,0:T(8,128)S(1)} %get-tuple-element.32.refs_0_, ...), custom_call_target="tpu_custom_call" | custom-call | tf_op jit(solution)/shard_map/pallas_call | solution.py:532
  21.8 1.6 %collective-permute-start.6 = (f32[36,8,128]{2,1,0:T(8,128)S(1)}, f32[36,8,128]{2,1,0:T(8,128)S(1)}, u32[]{:S(2)}, u32[]{:S(2)}) collective-permute-start(f32[36,8,128]{2,1,0:T(8,128)S(1)} %get-tuple-element.53), channel_id=1, source_target_pairs={{0,8},{8,0},{16,24},{24,16},{1,9},{9,1},{17,25},{25,17},{2,10},{10... | collective-permute-start | bytes 442376 | tf_op jit(solution)/shard_map/ppermute | solution.py:480
  23.4 0.8 %collective-permute-start.7 = (f32[36,8,128]{2,1,0:T(8,128)S(1)}, f32[36,8,128]{2,1,0:T(8,128)S(1)}, u32[]{:S(2)}, u32[]{:S(2)}) collective-permute-start(f32[36,8,128]{2,1,0:T(8,128)S(1)} %get-tuple-element.54), channel_id=1, source_target_pairs={{0,24},{8,16},{16,8},{24,0},{1,25},{9,17},{17,9},{25,1},{2,26},{10... | collective-permute-start | bytes 442376 | tf_op jit(solution)/shard_map/ppermute | solution.py:486
  24.1 5.1 %shard_map.117 = (f32[2,36,64,128]{3,2,1,0:T(8,128)S(1)}, f32[2,36,64,128]{3,2,1,0:T(8,128)S(1)}, f32[2,64,128]{2,1,0:T(8,128)S(1)}, f32[2,64,128]{2,1,0:T(8,128)S(1)}, f32[2,64,128]{2,1,0:T(8,128)S(1)}) custom-call(f32[2,36,64,128]{3,2,1,0:T(8,128)S(1)} %get-tuple-element.32.refs_0_, ...), custom_call_target="tpu_custom_call", output_to_operand_aliasing={{0}: (12, {}), {1}: (13, {}), {2}: (14, {})} | custom-call | flops 16777216 | bytes 16777216 | tf_op jit(solution)/shard_map/pallas_call | solution.py:540
  29.2 0.1 collective-permute-start.4
  29.3 2.9 %collective-permute-start.5 = (f32[2,64,128]{2,1,0:T(8,128)S(1)}, f32[2,64,128]{2,1,0:T(8,128)S(1)}, u32[]{:S(2)}, u32[]{:S(2)}) collective-permute-start(f32[2,64,128]{2,1,0:T(8,128)S(1)} %get-tuple-element.52), channel_id=1, source_target_pairs={{0,7},{1,2},{2,1},{3,4},{4,3},{5,6},{6,5},{7,0},{8,15},{9,10},{10,... | collective-permute-start | bytes 196616 | tf_op jit(solution)/shard_map/ppermute | solution.py:486
  32.2 3.3 %collective-permute-done.5.refs_9_ = f32[2,64,128]{2,1,0:T(8,128)S(1)} collective-permute-done((f32[2,64,128]{2,1,0:T(8,128)S(1)}, f32[2,64,128]{2,1,0:T(8,128)S(1)}, u32[]{:S(2)}, u32[]{:S(2)}) %collective-permute-start.5) | collective-permute-done | bytes 65568 | tf_op jit(solution)/shard_map/ppermute | solution.py:486
  35.5 6.8 %shard_map.118 = (f32[4,36,64,128]{3,2,1,0:T(8,128)S(1)}, f32[4,64,128]{2,1,0:T(8,128)S(1)}) custom-call(f32[2,36,64,128]{3,2,1,0:T(8,128)S(1)} %get-tuple-element.49.refs_0_, f32[2,36,64,128]{3,2,1,0:T(8,128)S(1)} %get-tuple-element.50.refs_1_, f32[2,36,64,128]{3,2,1,0:T(8,128)S(1)} %copy-done, f32[36,64,128]{2,1,0:T(8,128)S(1)} %get-tuple-element.34.refs_3_, ...), custom_call_target="tpu_custom_call" | custom-call | tf_op jit(solution)/shard_map/pallas_call | solution.py:550
  42.3 2.2 %collective-permute-start.10 = (f32[4,64,128]{2,1,0:T(8,128)S(1)}, f32[4,64,128]{2,1,0:T(8,128)S(1)}, u32[]{:S(2)}, u32[]{:S(2)}) collective-permute-start(f32[4,64,128]{2,1,0:T(8,128)S(1)} %get-tuple-element.59.refs_0_), channel_id=1, source_target_pairs={{0,24},{8,16},{16,8},{24,0},{1,25},{9,17},{17,9},{25,1},{2,26},{10... | collective-permute-start | bytes 393224 | tf_op jit(solution)/shard_map/ppermute | solution.py:480
  44.5 0.5 collective-permute-start.8
  45.0 0.8 %collective-permute-start.9 = (f32[4,64,128]{2,1,0:T(8,128)S(1)}, f32[4,64,128]{2,1,0:T(8,128)S(1)}, u32[]{:S(2)}, u32[]{:S(2)}) collective-permute-start(f32[4,64,128]{2,1,0:T(8,128)S(1)} %get-tuple-element.59.refs_0_), channel_id=1, source_target_pairs={{0,16},{8,24},{16,0},{24,8},{1,17},{9,25},{17,1},{25,9},{2,18},{10... | collective-permute-start | bytes 393224 | tf_op jit(solution)/shard_map/ppermute | solution.py:480
  46.5 0.0 copy-start.3
  46.5 0.0 copy-start.4
  46.5 2.3 %shard_map.119 = (f32[4,36,64,128]{3,2,1,0:T(8,128)}, f32[8,128]{1,0:T(8,128)S(1)}) custom-call(s32[1,1]{1,0:T(1,128)S(6)} %copy.18.rot_ref, f32[4,36,64,128]{3,2,1,0:T(8,128)S(1)} %get-tuple-element.56.value_ref, f32[36,64,128]{2,1,0:T(8,128)S(1)} %get-tuple-element.40.refs_12_.refs_10_.g1_ref, f32[36,64,128]{2,1,0:T(8,128)S(1)} %get-tuple-element.41.refs_13_.refs_11_.g2_ref), custom_call_target="tpu_custom_call" | custom-call | flops 8388608 | bytes 8388608 | tf_op jit(solution)/shard_map/pallas_call | solution.py:558
  48.9 0.6 collective-permute-done.8.refs_1_
  49.5 0.5 collective-permute-done.9.refs_2_
  50.0 1.7 %shard_map.120 = (f32[256,128]{1,0:T(8,128)S(1)}, f32[256,128]{1,0:T(8,128)S(1)}) custom-call(s32[32]{0:T(128)S(1)} %copy-done.6, s32[1,1]{1,0:T(1,128)S(6)} %copy.19.face_ref, f32[128,256]{1,0:T(8,128)S(1)} %copy-done.4, f32[1024,128]{1,0:T(8,128)S(1)} %copy-done.3, f32[8,128]{1,0:T(8,128)S(1)} %get-tuple-element.58._, ...), custom_call_target="tpu_custom_call" | custom-call | tf_op jit(solution)/shard_map/pallas_call | solution.py:568
  51.7 0.1 collective-permute-start.11
  51.8 1.3 %collective-permute-done.11 = f32[256,128]{1,0:T(8,128)S(1)} collective-permute-done((f32[256,128]{1,0:T(8,128)S(1)}, f32[256,128]{1,0:T(8,128)S(1)}, u32[]{:S(2)}, u32[]{:S(2)}) %collective-permute-start.11) | collective-permute-done | bytes 131104 | tf_op jit(solution)/shard_map/ppermute | solution.py:480
  53.1 0.1 collective-permute-start.12
  53.2 4.3 %collective-permute-done.12 = f32[128,128]{1,0:T(8,128)S(1)} collective-permute-done((f32[128,128]{1,0:T(8,128)S(1)}, f32[128,128]{1,0:T(8,128)S(1)}, u32[]{:S(2)}, u32[]{:S(2)}) %collective-permute-start.12) | collective-permute-done | bytes 65568 | tf_op jit(solution)/shard_map/ppermute | solution.py:480
  57.5 1.8 %collective-permute-start.13 = (f32[64,128]{1,0:T(8,128)S(1)}, f32[64,128]{1,0:T(8,128)S(1)}, u32[]{:S(2)}, u32[]{:S(2)}) collective-permute-start(f32[64,128]{1,0:T(8,128)S(1)} %slice.19), channel_id=1, source_target_pairs={{0,4},{1,5},{2,6},{3,7},{4,0},{5,1},{6,2},{7,3},{8,12},{9,13},{10,... | collective-permute-start | bytes 98312 | tf_op jit(solution)/shard_map/ppermute | solution.py:480
  59.3 3.4 %collective-permute-done.13 = f32[64,128]{1,0:T(8,128)S(1)} collective-permute-done((f32[64,128]{1,0:T(8,128)S(1)}, f32[64,128]{1,0:T(8,128)S(1)}, u32[]{:S(2)}, u32[]{:S(2)}) %collective-permute-start.13) | collective-permute-done | bytes 32800 | tf_op jit(solution)/shard_map/ppermute | solution.py:480
  62.7 0.6 slice_add_fusion.1
  (23 shorter events, 0.1 us)
Async XLA Ops:
  2.7 13.9 %collective-permute-start.2 = (f32[36,8,128]{2,1,0:T(8,128)S(1)}, f32[36,8,128]{2,1,0:T(8,128)S(1)}, u32[]{:S(2)}, u32[]{:S(2)}) collective-permute-start(f32[36,8,128]{2,1,0:T(8,128)S(1)} %get-tuple-element.42), channel_id=1, source_target_pairs={{0,8},{8,0},{16,24},{24,16},{1,9},{9,1},{17,25},{25,17},{2,10},{10... | collective-permute-start | bytes 442376 | tf_op jit(solution)/shard_map/ppermute | solution.py:480
  5.7 8.8 %copy-start.2 = (f32[36,64,128]{2,1,0:T(8,128)S(1)}, f32[36,64,128]{2,1,0:T(8,128)}, u32[]{:S(2)}) copy-start(f32[36,64,128]{2,1,0:T(8,128)} %vd_ref.1) | copy-start | bytes 3538948
  5.7 8.8 %copy-start.5 = (s32[64,128]{1,0:T(8,128)S(1)}, s32[64,128]{1,0:T(8,128)}, u32[]{:S(2)}) copy-start(s32[64,128]{1,0:T(8,128)} %wet_ref.1) | copy-start | bytes 98308
  5.7 10.9 %copy-start = (f32[2,36,64,128]{3,2,1,0:T(8,128)S(1)}, f32[2,36,64,128]{3,2,1,0:T(8,128)}, u32[]{:S(2)}) copy-start(f32[2,36,64,128]{3,2,1,0:T(8,128)} %refs_2_.5) | copy-start | bytes 7077892
  5.7 10.9 %copy-start.1 = (f32[256,128]{1,0:T(8,128)S(1)}, f32[256,128]{1,0:T(8,128)}, u32[]{:S(2)}) copy-start(f32[256,128]{1,0:T(8,128)} %constant.6.clone.refs_7_) | copy-start | bytes 393220
  5.7 10.9 %collective-permute-start.3 = (f32[36,8,128]{2,1,0:T(8,128)S(1)}, f32[36,8,128]{2,1,0:T(8,128)S(1)}, u32[]{:S(2)}, u32[]{:S(2)}) collective-permute-start(f32[36,8,128]{2,1,0:T(8,128)S(1)} %get-tuple-element.43), channel_id=1, source_target_pairs={{0,24},{8,16},{16,8},{24,0},{1,25},{9,17},{17,9},{25,1},{2,26},{10... | collective-permute-start | bytes 442376 | tf_op jit(solution)/shard_map/ppermute | solution.py:486
  10.7 5.0 %collective-permute-start = (f32[2,64,128]{2,1,0:T(8,128)S(1)}, f32[2,64,128]{2,1,0:T(8,128)S(1)}, u32[]{:S(2)}, u32[]{:S(2)}) collective-permute-start(f32[2,64,128]{2,1,0:T(8,128)S(1)} %get-tuple-element.38), channel_id=1, source_target_pairs={{0,1},{1,0},{2,3},{3,2},{4,5},{5,4},{6,7},{7,6},{8,9},{9,8},{10,11... | collective-permute-start | bytes 196616 | tf_op jit(solution)/shard_map/ppermute | solution.py:480
  10.8 5.8 %collective-permute-start.1 = (f32[2,64,128]{2,1,0:T(8,128)S(1)}, f32[2,64,128]{2,1,0:T(8,128)S(1)}, u32[]{:S(2)}, u32[]{:S(2)}) collective-permute-start(f32[2,64,128]{2,1,0:T(8,128)S(1)} %get-tuple-element.39), channel_id=1, source_target_pairs={{0,7},{1,2},{2,1},{3,4},{4,3},{5,6},{6,5},{7,0},{8,15},{9,10},{10,... | collective-permute-start | bytes 196616 | tf_op jit(solution)/shard_map/ppermute | solution.py:486
  21.8 13.7 %collective-permute-start.6 = (f32[36,8,128]{2,1,0:T(8,128)S(1)}, f32[36,8,128]{2,1,0:T(8,128)S(1)}, u32[]{:S(2)}, u32[]{:S(2)}) collective-permute-start(f32[36,8,128]{2,1,0:T(8,128)S(1)} %get-tuple-element.53), channel_id=1, source_target_pairs={{0,8},{8,0},{16,24},{24,16},{1,9},{9,1},{17,25},{25,17},{2,10},{10... | collective-permute-start | bytes 442376 | tf_op jit(solution)/shard_map/ppermute | solution.py:480
  23.4 12.1 %collective-permute-start.7 = (f32[36,8,128]{2,1,0:T(8,128)S(1)}, f32[36,8,128]{2,1,0:T(8,128)S(1)}, u32[]{:S(2)}, u32[]{:S(2)}) collective-permute-start(f32[36,8,128]{2,1,0:T(8,128)S(1)} %get-tuple-element.54), channel_id=1, source_target_pairs={{0,24},{8,16},{16,8},{24,0},{1,25},{9,17},{17,9},{25,1},{2,26},{10... | collective-permute-start | bytes 442376 | tf_op jit(solution)/shard_map/ppermute | solution.py:486
  29.2 3.0 %collective-permute-start.4 = (f32[2,64,128]{2,1,0:T(8,128)S(1)}, f32[2,64,128]{2,1,0:T(8,128)S(1)}, u32[]{:S(2)}, u32[]{:S(2)}) collective-permute-start(f32[2,64,128]{2,1,0:T(8,128)S(1)} %get-tuple-element.51), channel_id=1, source_target_pairs={{0,1},{1,0},{2,3},{3,2},{4,5},{5,4},{6,7},{7,6},{8,9},{9,8},{10,11... | collective-permute-start | bytes 196616 | tf_op jit(solution)/shard_map/ppermute | solution.py:480
  29.3 6.2 %collective-permute-start.5 = (f32[2,64,128]{2,1,0:T(8,128)S(1)}, f32[2,64,128]{2,1,0:T(8,128)S(1)}, u32[]{:S(2)}, u32[]{:S(2)}) collective-permute-start(f32[2,64,128]{2,1,0:T(8,128)S(1)} %get-tuple-element.52), channel_id=1, source_target_pairs={{0,7},{1,2},{2,1},{3,4},{4,3},{5,6},{6,5},{7,0},{8,15},{9,10},{10,... | collective-permute-start | bytes 196616 | tf_op jit(solution)/shard_map/ppermute | solution.py:486
  42.3 6.6 %collective-permute-start.10 = (f32[4,64,128]{2,1,0:T(8,128)S(1)}, f32[4,64,128]{2,1,0:T(8,128)S(1)}, u32[]{:S(2)}, u32[]{:S(2)}) collective-permute-start(f32[4,64,128]{2,1,0:T(8,128)S(1)} %get-tuple-element.59.refs_0_), channel_id=1, source_target_pairs={{0,24},{8,16},{16,8},{24,0},{1,25},{9,17},{17,9},{25,1},{2,26},{10... | collective-permute-start | bytes 393224 | tf_op jit(solution)/shard_map/ppermute | solution.py:480
  44.5 5.0 %collective-permute-start.8 = (f32[4,64,128]{2,1,0:T(8,128)S(1)}, f32[4,64,128]{2,1,0:T(8,128)S(1)}, u32[]{:S(2)}, u32[]{:S(2)}) collective-permute-start(f32[4,64,128]{2,1,0:T(8,128)S(1)} %get-tuple-element.59.refs_0_), channel_id=1, source_target_pairs={{0,8},{8,0},{16,24},{24,16},{1,9},{9,1},{17,25},{25,17},{2,10},{10... | collective-permute-start | bytes 393224 | tf_op jit(solution)/shard_map/ppermute | solution.py:480
  45.0 5.0 %collective-permute-start.9 = (f32[4,64,128]{2,1,0:T(8,128)S(1)}, f32[4,64,128]{2,1,0:T(8,128)S(1)}, u32[]{:S(2)}, u32[]{:S(2)}) collective-permute-start(f32[4,64,128]{2,1,0:T(8,128)S(1)} %get-tuple-element.59.refs_0_), channel_id=1, source_target_pairs={{0,16},{8,24},{16,0},{24,8},{1,17},{9,25},{17,1},{25,9},{2,18},{10... | collective-permute-start | bytes 393224 | tf_op jit(solution)/shard_map/ppermute | solution.py:480
  46.5 3.5 %copy-start.3 = (f32[1024,128]{1,0:T(8,128)S(1)}, f32[1024,128]{1,0:T(8,128)}, u32[]{:S(2)}) copy-start(f32[1024,128]{1,0:T(8,128)} %constant.8.clone.col_table_ref) | copy-start | bytes 1572868
  46.5 3.5 %copy-start.4 = (f32[128,256]{1,0:T(8,128)S(1)}, f32[128,256]{1,0:T(8,128)}, u32[]{:S(2)}) copy-start(f32[128,256]{1,0:T(8,128)} %constant.7.clone.row_table_ref) | copy-start | bytes 393220
  46.5 3.5 %copy-start.6 = (s32[32]{0:T(128)S(1)}, s32[32]{0:T(128)}, u32[]{:S(2)}) copy-start(s32[32]{0:T(128)} %owner_ref.1) | copy-start | bytes 388
  51.7 1.4 %collective-permute-start.11 = (f32[256,128]{1,0:T(8,128)S(1)}, f32[256,128]{1,0:T(8,128)S(1)}, u32[]{:S(2)}, u32[]{:S(2)}) collective-permute-start(f32[256,128]{1,0:T(8,128)S(1)} %get-tuple-element.61), channel_id=1, source_target_pairs={{0,1},{1,0},{2,3},{3,2},{4,5},{5,4},{6,7},{7,6},{8,9},{9,8},{10,11... | collective-permute-start | bytes 393224 | tf_op jit(solution)/shard_map/ppermute | solution.py:480
  53.1 4.3 %collective-permute-start.12 = (f32[128,128]{1,0:T(8,128)S(1)}, f32[128,128]{1,0:T(8,128)S(1)}, u32[]{:S(2)}, u32[]{:S(2)}) collective-permute-start(f32[128,128]{1,0:T(8,128)S(1)} %slice.17), channel_id=1, source_target_pairs={{0,2},{1,3},{2,0},{3,1},{4,6},{5,7},{6,4},{7,5},{8,10},{9,11},{10,... | collective-permute-start | bytes 196616 | tf_op jit(solution)/shard_map/ppermute | solution.py:480
  57.5 5.2 %collective-permute-start.13 = (f32[64,128]{1,0:T(8,128)S(1)}, f32[64,128]{1,0:T(8,128)S(1)}, u32[]{:S(2)}, u32[]{:S(2)}) collective-permute-start(f32[64,128]{1,0:T(8,128)S(1)} %slice.19), channel_id=1, source_target_pairs={{0,4},{1,5},{2,6},{3,7},{4,0},{5,1},{6,2},{7,3},{8,12},{9,13},{10,... | collective-permute-start | bytes 98312 | tf_op jit(solution)/shard_map/ppermute | solution.py:480

commit v5 on v4

--- a/solution.py
+++ b/solution.py
@@ -31,7 +31,7 @@
 F32 = jnp.float32
 PREP_UNROLL = 6
 FACTOR_ROWS, FACTOR_UNROLL = 64, 2
-UNROLLS = {16: (6, 9), 32: (4, 6)}
+UNROLLS = {16: (6, 9), 32: (4, 6), 64: (4, 6)}
 DOWN_UNROLL = 6
 EDGE = 16
 
@@ -84,12 +84,12 @@
     return tuple(east + west)
 
 
-def store_edge_rows(k, fields, block, last, south_ref, north_ref):
+def store_edge_rows(k, fields, ends, south_ref, north_ref):
     size = fields[0].shape[0]
     for c in range(4):
-        if block == 0:
+        if ends[0]:
             south_ref[k, 2 * c : 2 * c + 2, :] = fields[c][0:2, :]
-        if block == last or block is last:
+        if ends[1]:
             north_ref[k, 2 * c : 2 * c + 2, :] = fields[c][size - 2 : size, :]
 
 
@@ -121,33 +121,7 @@
     west_ref[...] = jnp.where(even, second, first)
 
 
-def prep_rows_kernel(rot_ref, adj_ref, row_a, row_b, raw_ref, south_ref, north_ref, sems):
-    levels, height = adj_ref.shape[1], adj_ref.shape[2]
-    cosine, sine = turn_scalars(rot_ref[0, 0])
-    copies = []
-    for i, start in enumerate((0, height - TILE)):
-        copies.append(pltpu.make_async_copy(adj_ref.at[:, :, pl.ds(start, TILE)], raw_ref.at[i], sems.at[i]))
-        copies[-1].start()
-    for copy in copies:
-        copy.wait()
-
-    def load(k):
-        return [[raw_ref[i, c, k] for c in range(4)] for i in range(2)]
-
-    def level(k, loaded, carry):
-        rotated = [(t, s, cosine * a - sine * b, sine * a + cosine * b) for t, s, a, b in loaded]
-
-        def store():
-            store_edge_rows(k, rotated[0], 0, None, south_ref, north_ref)
-            store_edge_rows(k, rotated[1], None, None, south_ref, north_ref)
-
-        return carry, store
-
-    loop(levels, load, level, 0, 6)
-    write_rows(row_a, row_b, south_ref, north_ref)
-
-
-def prep_columns_kernel(rot_ref, adj_ref, ts_ref, uv_ref, col_a, col_b, raw_ref, sems):
+def prep_kernel(rot_ref, adj_ref, ts_ref, uv_ref, col_a, col_b, row_a, row_b, raw_ref, south_ref, north_ref, sems):
     levels, height = adj_ref.shape[1], adj_ref.shape[2]
     cosine, sine = turn_scalars(rot_ref[0, 0])
     step = PREP_UNROLL
@@ -175,6 +149,8 @@
         for k, fields in stores:
             uv_ref[0, k] = fields[2]
             uv_ref[1, k] = fields[3]
+            store_edge_rows(k, fields, (True, True), south_ref, north_ref)
+    write_rows(row_a, row_b, south_ref, north_ref)
     write_columns(col_a, col_b, jnp.stack(acc[:2]), jnp.stack(acc[2:]))
 
 
@@ -220,37 +196,25 @@
         taken, refs[:] = refs[:count], refs[count:]
         return taken
 
-    ts_ref, uv_ref, flow_ref, w1_ref, w2_ref, h1_ref, h2_ref, cor_ref, col_a, col_b = take(10)
+    ts_ref, uv_ref, flow_ref, w1_ref, w2_ref, h1_ref, h2_ref, cor_ref, col_b, col_a = take(10)
     south_ref = north_ref = None
-    if stage != "middle":
-        row_a, row_b = take(2)
-    if stage == "up":
-        (first_ref,) = take(1)
+    if stage != "inner":
+        row_b, row_a = take(2)
+    if stage == "outer":
+        first_ref, inner_ref = take(2)
+    if stage == "whole":
+        g1_ref, g2_ref = take(2)
+        ts_out, uv_out, surface_ref, *sent = take(7)
+        south_out, north_out, value_ref = take(3)
+    else:
         value_ref, surface_ref = take(2)
-        surface_ref[0:2] = first_ref[...]
-    else:
-        g1_ref, g2_ref = take(2)
-        if stage == "middle":
-            ts_in, uv_in, surface_in, east_in, west_in = take(5)
-            ts_out, uv_out, surface_ref, east_out, west_out = take(5)
-        else:
-            ts_out, uv_out, surface_ref, east_out, west_out, sent_a, sent_b = take(7)
-            south_out, north_out = take(2)
-        (value_ref,) = take(1)
     east_ref, west_ref = take(2)
     read_columns(col_a, col_b, east_ref, west_ref)
-    if stage != "middle":
+    if stage != "inner":
         south_ref, north_ref = take(2)
         read_rows(row_a, row_b, south_ref, north_ref)
     levels, height = ts_ref.shape[1], ts_ref.shape[2]
     first_cor = pl.multiple_of(lax.axis_index("ty") * height, TILE)
-    packed = {}
-    done, others = (), ()
-    if stage == "middle":
-        ((first_row, size),) = blocks
-        done = ((ts_in, ts_out), (uv_in, uv_out))
-        others = (pl.ds(0, first_row), pl.ds(first_row + size, height - first_row - size))
-
     def get(c, k, start):
         rows = pl.ds(start, TILE)
         return ts_ref[c, k, rows, :] if c < 2 else uv_ref[c - 2, k, rows, :]
@@ -273,10 +237,10 @@
         low_one, high_one = lane < 1, lane >= LANES - 1
         zero = jnp.zeros((size, LANES), F32)
         rows = pl.ds(first_row, size)
-        kept_rows = rows if stage == "up" else pl.ds(0, size)
+        kept_rows = pl.ds(block * size, size)
         south_end, north_end = first_row == 0, first_row + size == height
         cor = cor_ref[pl.ds(first_cor + first_row, size), :]
-        up_unroll, down_unroll = UNROLLS[min(size, 32)]
+        up_unroll, down_unroll = UNROLLS[size]
 
         def fetch(c, k, shift, halos, first_row=first_row, size=size):
             start = first_row + shift
@@ -345,66 +309,52 @@
 
         top = loop(levels, load_up, upward, (zero,) * 4, up_unroll)
         for c in range(2):
-            surface_ref[(2 if stage == "up" else 0) + c, rows, :] = top[c]
-        if stage == "up":
+            if stage == "outer":
+                surface_ref[2 + c, rows, :] = top[c]
+            else:
+                surface_ref[c, kept_rows, :] = top[c]
+        if stage != "whole":
             continue
 
         def load_down(k, rows=rows, kept_rows=kept_rows):
-            passed = [
-                (source, target, c, part, source[c, k, part, :])
-                for source, target in done
-                for c in range(2)
-                for part in others
-            ]
             values = [value_ref[c, k, kept_rows, :] for c in range(4)]
-            return values, (g1_ref[k, rows, :], g2_ref[k, rows, :]), passed
+            return values, (g1_ref[k, rows, :], g2_ref[k, rows, :])
 
         def downward(k, loaded, carry, rows=rows, ends=(south_end, north_end), lane=lane):
             above, acc = carry
-            values, gains, passed = loaded
+            values, gains = loaded
             fields = tuple(values[c] + gains[c // 2] * above[c] for c in range(4))
 
             def store():
                 for c in range(2):
                     ts_out[c, k, rows, :] = fields[c]
                     uv_out[c, k, rows, :] = fields[c + 2]
-                for _, target, c, part, value in passed:
-                    target[c, k, part, :] = value
-                if ends[0] or ends[1]:
-                    store_edge_rows(k, fields, 0 if ends[0] else 1, 1 if ends[1] else 2, south_out, north_out)
+                store_edge_rows(k, fields, ends, south_out, north_out)
 
             return (fields, pack_columns(acc, k, fields, lane)), store
 
         _, acc = loop(levels, load_down, downward, ((zero,) * 4, (zero,) * 4), down_unroll)
-        packed[first_row] = acc
-    if stage == "edge":
-        for (first_row, size), acc in zip(blocks, packed.values()):
-            for g in range(2):
-                east_out[g, pl.ds(first_row, size), :] = acc[g]
-                west_out[g, pl.ds(first_row, size), :] = acc[g + 2]
-        write_rows(sent_a, sent_b, south_out, north_out)
-    if stage == "middle":
+        write_rows(sent[2], sent[3], south_out, north_out)
+        write_columns(sent[0], sent[1], jnp.stack(acc[:2]), jnp.stack(acc[2:]))
+    if stage == "outer":
+        surface_ref[0:2] = first_ref[...]
         for c in range(2):
-            for part in others:
-                surface_ref[c, part, :] = surface_in[c, part, :]
-        acc = packed[first_row]
-        spans = (slice(0, first_row), slice(first_row + size, height))
-        east, west = (
-            jnp.stack([jnp.concatenate([ref[g, spans[0], :], acc[g + at], ref[g, spans[1], :]], axis=0) for g in range(2)])
-            for ref, at in ((east_in, 0), (west_in, 2))
-        )
-        write_columns(east_out, west_out, east, west)
-
-
-def last_kernel(rot_ref, value_ref, g1_ref, g2_ref, out_ref, token_ref, field_ref, sems):
+            surface_ref[2 + c, blocks[0][1] : blocks[1][0], :] = inner_ref[c]
+
+
+def last_kernel(rot_ref, inner_ref, outer_ref, g1_ref, g2_ref, out_ref, token_ref, field_ref, sems):
     token_ref[...] = jnp.zeros_like(token_ref)
-    levels = value_ref.shape[1]
+    levels = inner_ref.shape[1]
     cosine, sine = turn_scalars(rot_ref[0, 0])
     step = DOWN_UNROLL
+
+    def column(c, k):
+        return jnp.concatenate([outer_ref[c, k, 0:EDGE, :], inner_ref[c, k], outer_ref[c, k, EDGE:, :]], axis=0)
+
     above, copies = None, []
     for i in range(levels // step):
         group = range(i * step, (i + 1) * step)
-        loaded = [([value_ref[c, k] for c in range(4)], (g1_ref[k], g2_ref[k])) for k in group]
+        loaded = [([column(c, k) for c in range(4)], (g1_ref[k], g2_ref[k])) for k in group]
         done = []
         for values, gains in loaded:
             if above is not None:
@@ -500,7 +450,7 @@
     row_pair, col_pair = [shape(levels, TILE, width)] * 2, [shape(2, height, LANES)] * 2
     rows_scratch = [pltpu.VMEM((levels, TILE, width), F32)] * 2
     cols_scratch = [pltpu.VMEM((2, height, LANES), F32)] * 2
-    state = [pair, pair, shape(2, height, width)]
+    surface = shape(2, height, width)
 
     def kept(rows):
         return pltpu.VMEM((4, levels, rows, width), F32)
@@ -514,56 +464,49 @@
 
     dma = pltpu.SemaphoreType.DMA
     adjoint = pltpu.with_memory_space_constraint(adjoint, pltpu.HBM)
-    edge_raw = pltpu.VMEM((2, 4, levels, TILE, width), F32)
-    rows = call(prep_rows_kernel, row_pair, [SMEM, ANY], [edge_raw] + rows_scratch + [dma((2,))])(rotation, adjoint)
-    row_b, row_a = exchange("ty", *rows)
-    ts, uv, *cols = call(
-        prep_columns_kernel,
-        [pair, pair] + col_pair,
+    ts, uv, *sent = call(
+        prep_kernel,
+        [pair, pair] + col_pair + row_pair,
         [SMEM, ANY],
-        [pltpu.VMEM((2, levels, height, width), F32), dma((2 * levels // PREP_UNROLL,))],
+        [pltpu.VMEM((2, levels, height, width), F32)] + rows_scratch + [dma((2 * levels // PREP_UNROLL,))],
         limit=6,
         work=1 << 23,
     )(rotation, adjoint)
-    col_b, col_a = exchange("tx", *cols)
+    cols, rows = exchange("tx", *sent[:2]), exchange("ty", *sent[2:])
     w1, w2, h1, h2, g1, g2 = call(factor_kernel, [full] * 6, [VMEM] * 2, work=1 << 22)(vert_diff, wet_levels)
-    edge_blocks = ((0, EDGE), (height - EDGE, EDGE))
+    coefficients = (background_flow, w1, w2, h1, h2, coriolis)
+    ts, uv, first, *sent = call(
+        functools.partial(step_kernel, "whole", ((0, height),)),
+        [pair, pair, surface] + col_pair + row_pair,
+        [VMEM] * 14,
+        rows_scratch + [kept(height)] + cols_scratch + rows_scratch,
+        limit=12,
+    )(ts, uv, *coefficients, *cols, *rows, g1, g2)
+    cols, rows = exchange("tx", *sent[:2]), exchange("ty", *sent[2:])
     middle = height - 2 * EDGE
-    ts1, uv1, first, east, west, *rows = call(
-        functools.partial(step_kernel, "edge", edge_blocks),
-        state + col_pair + row_pair,
+    inner, inner_surface = call(
+        functools.partial(step_kernel, "inner", ((EDGE, middle),)),
+        [shape(4, levels, middle, width), shape(2, middle, width)],
+        [VMEM] * 10,
+        cols_scratch,
+        work=1 << 24,
+    )(ts, uv, *coefficients, *cols)
+    outer, surfaces = call(
+        functools.partial(step_kernel, "outer", ((0, EDGE), (height - EDGE, EDGE))),
+        [shape(4, levels, 2 * EDGE, width), shape(4, height, width)],
         [VMEM] * 14,
-        rows_scratch + [kept(EDGE)] + cols_scratch + rows_scratch,
-        limit=8,
-    )(ts, uv, background_flow, w1, w2, h1, h2, coriolis, col_a, col_b, row_a, row_b, g1, g2)
-    row_b, row_a = exchange("ty", *rows)
-    ts, uv, first, *cols = call(
-        functools.partial(step_kernel, "middle", ((EDGE, middle),)),
-        state + col_pair,
-        [VMEM] * 17,
-        [kept(middle)] + cols_scratch,
-        limit=8,
-        aliases={12: 0, 13: 1, 14: 2},
-        work=1 << 24,
-    )(ts, uv, background_flow, w1, w2, h1, h2, coriolis, col_a, col_b, g1, g2, ts1, uv1, first, east, west)
-    col_b, col_a = exchange("tx", *cols)
-    values, surfaces = call(
-        functools.partial(step_kernel, "up", ((0, height),)),
-        [shape(4, levels, height, width), shape(4, height, width)],
-        [VMEM] * 13,
         cols_scratch + rows_scratch,
-        limit=8,
-    )(ts, uv, background_flow, w1, w2, h1, h2, coriolis, col_a, col_b, row_a, row_b, first)
+    )(ts, uv, *coefficients, *cols, *rows, first, inner_surface)
     parts = [surfaces] + [swap(surfaces, "ty", bit) for bit in range(1, ty)]
     adjoint_out, token = call(
         last_kernel,
         [shape(*adjoint.shape), shape(TILE, LANES)],
-        [SMEM] + [VMEM] * 3,
+        [SMEM] + [VMEM] * 4,
         [kept(height), dma((levels // DOWN_UNROLL,))],
         out_specs=[ANY, VMEM],
         limit=8,
         work=1 << 23,
-    )(rotation, values, g1, g2)
+    )(rotation, inner, outer, g1, g2)
     size = 4 * KY * NFACE // ctrl_owner.shape[0]
     keep, send = call(
         functools.partial(transform_kernel, tx, norm),

time: 63.5 us -> 61.6 us (0.970)
  Pallas kernels: 27.1 us -> 25.1 us
  waiting for transfers between devices: 14.3 us -> 15.5 us
  starting transfers between devices: 19.1 us -> 18.1 us
    pallas_call x5 -> x4, Pallas kernels: 21.9 us -> 19.9 us  [the longest x1 9.17 us: body(): call(functools.partial(step_kernel, 'whole', ((0, height),)), [pair, pair...]
    ppermute x4, waiting for transfers between devices: 4.09 us -> 6.05 us  [exchange(): return (lax.ppermute(second, axis, others), swap(first, axis, 1))]
    ppermute x10, starting transfers between devices: 10.2 us -> 8.34 us  [swap(): lax.ppermute(block, axis, [(i, i ^ bit) for i in range(lax.axis_size(axis...]
    ppermute x4, starting transfers between devices: 8.95 us -> 9.74 us  [exchange(): return (lax.ppermute(second, axis, others), swap(first, axis, 1))]
    ppermute x10, waiting for transfers between devices: 10.2 us -> 9.43 us  [swap(): lax.ppermute(block, axis, [(i, i ^ bit) for i in range(lax.axis_size(axis...]
  transfers between devices with their start and end apart: 14 -> 14, of which waited for: 7 -> 8; matrix products, arithmetic and copies ran while one was open for 0% -> 0% of each run, Pallas kernels for 19% -> 11%
where the time goes in v5:
time: 61.6 us; the launch traced here: 61.5 us
  Pallas kernels  25.1 us (41%)
  starting transfers between devices  18.1 us (29%)
  waiting for transfers between devices  15.5 us (25%)
  between operations  2.11 us (3%)
  other arithmetic  0.64 us (1%)
    ppermute x4, starting transfers between devices, exchange(): return (lax.ppermute(second, axis, others), swap(first, axis, 1))  9.74 us
    ppermute x10, waiting for transfers between devices, swap(): lax.ppermute(block, axis, [(i, i ^ bit) for i in range(lax.axis_size(axis...  9.43 us
    pallas_call x1, Pallas kernels, body(): call(functools.partial(step_kernel, 'whole', ((0, height),)), [pair, pair...  9.17 us
    ppermute x10, starting transfers between devices, swap(): lax.ppermute(block, axis, [(i, i ^ bit) for i in range(lax.axis_size(axis...  8.34 us
    ppermute x4, waiting for transfers between devices, exchange(): return (lax.ppermute(second, axis, others), swap(first, axis, 1))  6.05 us
    pallas_call x1, Pallas kernels, body(): call(functools.partial(step_kernel, 'outer', ((0, EDGE), (height - EDGE,...  3.65 us
    pallas_call x1, Pallas kernels, body(): call(prep_kernel, [pair, pair] + col_pair + row_pair, [SMEM, ANY], [pltpu...  3.64 us
    pallas_call x1, Pallas kernels, body(): call(functools.partial(step_kernel, 'inner', ((EDGE, middle),)), [shape(4...  3.45 us
  transfers between devices with their start and end apart: 14, of which 8 were waited for; matrix products, arithmetic and copies ran while one was open for 0% of the time, Pallas kernels for 11%

profile of v5, /device:TPU:0, one launch (start us, length us, event | category | flops | bytes accessed | tf_op | source)
XLA Modules:
  0.0 61.5 jit_solution(14284664152207810254)
XLA Ops:
  1.3 0.0 copy-start.1
  1.3 3.6 %shard_map.113 = (f32[2,36,64,128]{3,2,1,0:T(8,128)S(1)}, f32[2,36,64,128]{3,2,1,0:T(8,128)S(1)}, f32[2,64,128]{2,1,0:T(8,128)S(1)}, f32[2,64,128]{2,1,0:T(8,128...) custom-call(s32[1,1]{1,0:T(1,128)S(6)} %copy.12.rot_ref, f32[4,36,64,128]{3,2,1,0:T(8,128)} %adj_ref.1), custom_call_target="tpu_custom_call" | custom-call | flops 8388608 | bytes 8388608 | tf_op jit(solution)/shard_map/pallas_call | solution.py:467
  5.0 4.0 %collective-permute-start.2 = (f32[36,8,128]{2,1,0:T(8,128)S(1)}, f32[36,8,128]{2,1,0:T(8,128)S(1)}, u32[]{:S(2)}, u32[]{:S(2)}) collective-permute-start(f32[36,8,128]{2,1,0:T(8,128)S(1)} %get-tuple-element.37), channel_id=1, source_target_pairs={{0,24},{8,16},{16,8},{24,0},{1,25},{9,17},{17,9},{25,1},{2,26},{10... | collective-permute-start | bytes 442376 | tf_op jit(solution)/shard_map/ppermute | solution.py:436
  8.9 0.5 collective-permute-start.3
  9.5 2.5 %collective-permute-start = (f32[2,64,128]{2,1,0:T(8,128)S(1)}, f32[2,64,128]{2,1,0:T(8,128)S(1)}, u32[]{:S(2)}, u32[]{:S(2)}) collective-permute-start(f32[2,64,128]{2,1,0:T(8,128)S(1)} %get-tuple-element.35), channel_id=1, source_target_pairs={{0,7},{1,2},{2,1},{3,4},{4,3},{5,6},{6,5},{7,0},{8,15},{9,10},{10,... | collective-permute-start | bytes 196616 | tf_op jit(solution)/shard_map/ppermute | solution.py:436
  12.0 1.2 %shard_map.114 = (f32[36,64,128]{2,1,0:T(8,128)S(1)}, f32[36,64,128]{2,1,0:T(8,128)S(1)}, f32[36,64,128]{2,1,0:T(8,128)S(1)}, f32[36,64,128]{2,1,0:T(8,128)S(1)}...) custom-call(f32[36,64,128]{2,1,0:T(8,128)S(1)} %copy-done.2, s32[64,128]{1,0:T(8,128)S(1)} %copy-done.5), custom_call_target="tpu_custom_call" | custom-call | flops 4194304 | bytes 4194304 | tf_op jit(solution)/shard_map/pallas_call | solution.py:476
  13.2 2.2 %collective-permute-done.refs_8_ = f32[2,64,128]{2,1,0:T(8,128)S(1)} collective-permute-done((f32[2,64,128]{2,1,0:T(8,128)S(1)}, f32[2,64,128]{2,1,0:T(8,128)S(1)}, u32[]{:S(2)}, u32[]{:S(2)}) %collective-permute-start) | collective-permute-done | bytes 65568 | tf_op jit(solution)/shard_map/ppermute | solution.py:436
  15.4 0.8 %collective-permute-done.3.refs_11_ = f32[36,8,128]{2,1,0:T(8,128)S(1)} collective-permute-done((f32[36,8,128]{2,1,0:T(8,128)S(1)}, f32[36,8,128]{2,1,0:T(8,128)S(1)}, u32[]{:S(2)}, u32[]{:S(2)}) %collective-permute-start.3) | collective-permute-done | bytes 147488 | tf_op jit(solution)/shard_map/ppermute | solution.py:430
  16.2 9.2 %shard_map.115 = (f32[2,36,64,128]{3,2,1,0:T(8,128)S(1)}, f32[2,36,64,128]{3,2,1,0:T(8,128)S(1)}, f32[2,64,128]{2,1,0:T(8,128)S(1)}, f32[2,64,128]{2,1,0:T(8,128...) custom-call(f32[2,36,64,128]{3,2,1,0:T(8,128)S(1)} %get-tuple-element.29.refs_0_, ...), custom_call_target="tpu_custom_call" | custom-call | tf_op jit(solution)/shard_map/pallas_call | solution.py:478
  25.4 1.5 %collective-permute-start.6 = (f32[36,8,128]{2,1,0:T(8,128)S(1)}, f32[36,8,128]{2,1,0:T(8,128)S(1)}, u32[]{:S(2)}, u32[]{:S(2)}) collective-permute-start(f32[36,8,128]{2,1,0:T(8,128)S(1)} %get-tuple-element.46), channel_id=1, source_target_pairs={{0,24},{8,16},{16,8},{24,0},{1,25},{9,17},{17,9},{25,1},{2,26},{10... | collective-permute-start | bytes 442376 | tf_op jit(solution)/shard_map/ppermute | solution.py:436
  26.9 0.3 collective-permute-start.7
  27.2 1.8 %collective-permute-start.4 = (f32[2,64,128]{2,1,0:T(8,128)S(1)}, f32[2,64,128]{2,1,0:T(8,128)S(1)}, u32[]{:S(2)}, u32[]{:S(2)}) collective-permute-start(f32[2,64,128]{2,1,0:T(8,128)S(1)} %get-tuple-element.43), channel_id=1, source_target_pairs={{0,7},{1,2},{2,1},{3,4},{4,3},{5,6},{6,5},{7,0},{8,15},{9,10},{10,... | collective-permute-start | bytes 196616 | tf_op jit(solution)/shard_map/ppermute | solution.py:436
  29.0 0.1 collective-permute-start.5
  29.1 3.8 %collective-permute-done.4.refs_8_ = f32[2,64,128]{2,1,0:T(8,128)S(1)} collective-permute-done((f32[2,64,128]{2,1,0:T(8,128)S(1)}, f32[2,64,128]{2,1,0:T(8,128)S(1)}, u32[]{:S(2)}, u32[]{:S(2)}) %collective-permute-start.4) | collective-permute-done | bytes 65568 | tf_op jit(solution)/shard_map/ppermute | solution.py:436
  32.9 3.4 %shard_map.116 = (f32[4,36,32,128]{3,2,1,0:T(8,128)S(1)}, f32[2,32,128]{2,1,0:T(8,128)S(1)}) custom-call(f32[2,36,64,128]{3,2,1,0:T(8,128)S(1)} %get-tuple-element.41.refs_0_, f32[2,36,64,128]{3,2,1,0:T(8,128)S(1)} %get-tuple-element.42.refs_1_, f32[2,36,64,128]{3,2,1,0:T(8,128)S(1)} %copy-done, f32[36,64,128]{2,1,0:T(8,128)S(1)} %get-tuple-element.31.refs_3_, ...), custom_call_target="tpu_custom_call" | custom-call | flops 16777216 | bytes 16777216 | tf_op jit(solution)/shard_map/pallas_call | solution.py:487
  36.4 3.7 %shard_map.117 = (f32[4,36,32,128]{3,2,1,0:T(8,128)S(1)}, f32[4,64,128]{2,1,0:T(8,128)S(1)}) custom-call(f32[2,36,64,128]{3,2,1,0:T(8,128)S(1)} %get-tuple-element.41.refs_0_, f32[2,36,64,128]{3,2,1,0:T(8,128)S(1)} %get-tuple-element.42.refs_1_, f32[2,36,64,128]{3,2,1,0:T(8,128)S(1)} %copy-done, f32[36,64,128]{2,1,0:T(8,128)S(1)} %get-tuple-element.31.refs_3_, ...), custom_call_target="tpu_custom_call" | custom-call | tf_op jit(solution)/shard_map/pallas_call | solution.py:494
  40.1 2.9 %collective-permute-start.10 = (f32[4,64,128]{2,1,0:T(8,128)S(1)}, f32[4,64,128]{2,1,0:T(8,128)S(1)}, u32[]{:S(2)}, u32[]{:S(2)}) collective-permute-start(f32[4,64,128]{2,1,0:T(8,128)S(1)} %get-tuple-element.53.refs_0_), channel_id=1, source_target_pairs={{0,24},{8,16},{16,8},{24,0},{1,25},{9,17},{17,9},{25,1},{2,26},{10... | collective-permute-start | bytes 393224 | tf_op jit(solution)/shard_map/ppermute | solution.py:430
  43.0 0.5 collective-permute-start.8
  43.5 0.1 collective-permute-start.9
  44.3 0.0 copy-start.3
  44.3 0.0 copy-start.4
  44.3 2.3 %shard_map.118 = (f32[4,36,64,128]{3,2,1,0:T(8,128)}, f32[8,128]{1,0:T(8,128)S(1)}) custom-call(s32[1,1]{1,0:T(1,128)S(6)} %copy.12.rot_ref, f32[4,36,32,128]{3,2,1,0:T(8,128)S(1)} %get-tuple-element.45.inner_ref, f32[4,36,32,128]{3,2,1,0:T(8,128)S(1)} %get-tuple-element.50.outer_ref, f32[36,64,128]{2,1,0:T(8,128)S(1)} %get-tuple-element.39.refs_12_.g1_ref, ...), custom_call_target="tpu_custom_call" | custom-call | flops 8388608 | bytes 8388608 | tf_op jit(solution)/shard_map/pallas_call | solution.py:501
  46.7 1.3 %collective-permute-done.8.refs_1_ = f32[4,64,128]{2,1,0:T(8,128)S(1)} collective-permute-done((f32[4,64,128]{2,1,0:T(8,128)S(1)}, f32[4,64,128]{2,1,0:T(8,128)S(1)}, u32[]{:S(2)}, u32[]{:S(2)}) %collective-permute-start.8) | collective-permute-done | bytes 131104 | tf_op jit(solution)/shard_map/ppermute | solution.py:430
  48.0 0.5 collective-permute-done.9.refs_2_
  48.5 1.7 %shard_map.119 = (f32[256,128]{1,0:T(8,128)S(1)}, f32[256,128]{1,0:T(8,128)S(1)}) custom-call(s32[32]{0:T(128)S(1)} %copy-done.6, s32[1,1]{1,0:T(1,128)S(6)} %copy.13.face_ref, f32[128,256]{1,0:T(8,128)S(1)} %copy-done.4, f32[1024,128]{1,0:T(8,128)S(1)} %copy-done.3, f32[8,128]{1,0:T(8,128)S(1)} %get-tuple-element.52._, ...), custom_call_target="tpu_custom_call" | custom-call | tf_op jit(solution)/shard_map/pallas_call | solution.py:511
  50.2 0.1 collective-permute-start.11
  50.2 1.3 %collective-permute-done.11 = f32[256,128]{1,0:T(8,128)S(1)} collective-permute-done((f32[256,128]{1,0:T(8,128)S(1)}, f32[256,128]{1,0:T(8,128)S(1)}, u32[]{:S(2)}, u32[]{:S(2)}) %collective-permute-start.11) | collective-permute-done | bytes 131104 | tf_op jit(solution)/shard_map/ppermute | solution.py:430
  51.6 1.5 %collective-permute-start.12 = (f32[128,128]{1,0:T(8,128)S(1)}, f32[128,128]{1,0:T(8,128)S(1)}, u32[]{:S(2)}, u32[]{:S(2)}) collective-permute-start(f32[128,128]{1,0:T(8,128)S(1)} %slice.17), channel_id=1, source_target_pairs={{0,2},{1,3},{2,0},{3,1},{4,6},{5,7},{6,4},{7,5},{8,10},{9,11},{10,... | collective-permute-start | bytes 196616 | tf_op jit(solution)/shard_map/ppermute | solution.py:430
  53.1 2.8 %collective-permute-done.12 = f32[128,128]{1,0:T(8,128)S(1)} collective-permute-done((f32[128,128]{1,0:T(8,128)S(1)}, f32[128,128]{1,0:T(8,128)S(1)}, u32[]{:S(2)}, u32[]{:S(2)}) %collective-permute-start.12) | collective-permute-done | bytes 65568 | tf_op jit(solution)/shard_map/ppermute | solution.py:430
  56.0 2.2 %collective-permute-start.13 = (f32[64,128]{1,0:T(8,128)S(1)}, f32[64,128]{1,0:T(8,128)S(1)}, u32[]{:S(2)}, u32[]{:S(2)}) collective-permute-start(f32[64,128]{1,0:T(8,128)S(1)} %slice.19), channel_id=1, source_target_pairs={{0,4},{1,5},{2,6},{3,7},{4,0},{5,1},{6,2},{7,3},{8,12},{9,13},{10,... | collective-permute-start | bytes 98312 | tf_op jit(solution)/shard_map/ppermute | solution.py:430
  58.2 2.6 %collective-permute-done.13 = f32[64,128]{1,0:T(8,128)S(1)} collective-permute-done((f32[64,128]{1,0:T(8,128)S(1)}, f32[64,128]{1,0:T(8,128)S(1)}, u32[]{:S(2)}, u32[]{:S(2)}) %collective-permute-start.13) | collective-permute-done | bytes 32800 | tf_op jit(solution)/shard_map/ppermute | solution.py:430
  60.8 0.6 %slice_add_fusion.1 = f32[64,128]{1,0:T(8,128)} fusion(f32[64,128]{1,0:T(8,128)S(1)} %collective-permute-done.13, f32[128,128]{1,0:T(8,128)S(1)} %slice_add_fusion), kind=kLoop, calls=%fused_computation.1 | loop fusion | flops 8192 | bytes 98304 | tf_op jit(solution)/shard_map/add | solution.py:520
  (22 shorter events, 0.1 us)
Async XLA Ops:
  1.3 10.7 %copy-start.2 = (f32[36,64,128]{2,1,0:T(8,128)S(1)}, f32[36,64,128]{2,1,0:T(8,128)}, u32[]{:S(2)}) copy-start(f32[36,64,128]{2,1,0:T(8,128)} %vd_ref.1) | copy-start | bytes 3538948
  1.3 10.7 %copy-start.5 = (s32[64,128]{1,0:T(8,128)S(1)}, s32[64,128]{1,0:T(8,128)}, u32[]{:S(2)}) copy-start(s32[64,128]{1,0:T(8,128)} %wet_ref.1) | copy-start | bytes 98308
  1.3 14.9 %copy-start = (f32[2,36,64,128]{3,2,1,0:T(8,128)S(1)}, f32[2,36,64,128]{3,2,1,0:T(8,128)}, u32[]{:S(2)}) copy-start(f32[2,36,64,128]{3,2,1,0:T(8,128)} %refs_2_.5) | copy-start | bytes 7077892
  1.3 14.9 %copy-start.1 = (f32[256,128]{1,0:T(8,128)S(1)}, f32[256,128]{1,0:T(8,128)}, u32[]{:S(2)}) copy-start(f32[256,128]{1,0:T(8,128)} %constant.6.clone.refs_7_) | copy-start | bytes 393220
  5.0 10.4 %collective-permute-start.2 = (f32[36,8,128]{2,1,0:T(8,128)S(1)}, f32[36,8,128]{2,1,0:T(8,128)S(1)}, u32[]{:S(2)}, u32[]{:S(2)}) collective-permute-start(f32[36,8,128]{2,1,0:T(8,128)S(1)} %get-tuple-element.37), channel_id=1, source_target_pairs={{0,24},{8,16},{16,8},{24,0},{1,25},{9,17},{17,9},{25,1},{2,26},{10... | collective-permute-start | bytes 442376 | tf_op jit(solution)/shard_map/ppermute | solution.py:436
  8.9 7.3 %collective-permute-start.3 = (f32[36,8,128]{2,1,0:T(8,128)S(1)}, f32[36,8,128]{2,1,0:T(8,128)S(1)}, u32[]{:S(2)}, u32[]{:S(2)}) collective-permute-start(f32[36,8,128]{2,1,0:T(8,128)S(1)} %get-tuple-element.38), channel_id=1, source_target_pairs={{0,8},{8,0},{16,24},{24,16},{1,9},{9,1},{17,25},{25,17},{2,10},{10... | collective-permute-start | bytes 442376 | tf_op jit(solution)/shard_map/ppermute | solution.py:430
  9.5 5.9 %collective-permute-start = (f32[2,64,128]{2,1,0:T(8,128)S(1)}, f32[2,64,128]{2,1,0:T(8,128)S(1)}, u32[]{:S(2)}, u32[]{:S(2)}) collective-permute-start(f32[2,64,128]{2,1,0:T(8,128)S(1)} %get-tuple-element.35), channel_id=1, source_target_pairs={{0,7},{1,2},{2,1},{3,4},{4,3},{5,6},{6,5},{7,0},{8,15},{9,10},{10,... | collective-permute-start | bytes 196616 | tf_op jit(solution)/shard_map/ppermute | solution.py:436
  11.9 3.4 %collective-permute-start.1 = (f32[2,64,128]{2,1,0:T(8,128)S(1)}, f32[2,64,128]{2,1,0:T(8,128)S(1)}, u32[]{:S(2)}, u32[]{:S(2)}) collective-permute-start(f32[2,64,128]{2,1,0:T(8,128)S(1)} %get-tuple-element.36), channel_id=1, source_target_pairs={{0,1},{1,0},{2,3},{3,2},{4,5},{5,4},{6,7},{7,6},{8,9},{9,8},{10,11... | collective-permute-start | bytes 196616 | tf_op jit(solution)/shard_map/ppermute | solution.py:430
  25.4 11.0 %collective-permute-start.6 = (f32[36,8,128]{2,1,0:T(8,128)S(1)}, f32[36,8,128]{2,1,0:T(8,128)S(1)}, u32[]{:S(2)}, u32[]{:S(2)}) collective-permute-start(f32[36,8,128]{2,1,0:T(8,128)S(1)} %get-tuple-element.46), channel_id=1, source_target_pairs={{0,24},{8,16},{16,8},{24,0},{1,25},{9,17},{17,9},{25,1},{2,26},{10... | collective-permute-start | bytes 442376 | tf_op jit(solution)/shard_map/ppermute | solution.py:436
  26.9 9.5 %collective-permute-start.7 = (f32[36,8,128]{2,1,0:T(8,128)S(1)}, f32[36,8,128]{2,1,0:T(8,128)S(1)}, u32[]{:S(2)}, u32[]{:S(2)}) collective-permute-start(f32[36,8,128]{2,1,0:T(8,128)S(1)} %get-tuple-element.47), channel_id=1, source_target_pairs={{0,8},{8,0},{16,24},{24,16},{1,9},{9,1},{17,25},{25,17},{2,10},{10... | collective-permute-start | bytes 442376 | tf_op jit(solution)/shard_map/ppermute | solution.py:430
  27.2 5.7 %collective-permute-start.4 = (f32[2,64,128]{2,1,0:T(8,128)S(1)}, f32[2,64,128]{2,1,0:T(8,128)S(1)}, u32[]{:S(2)}, u32[]{:S(2)}) collective-permute-start(f32[2,64,128]{2,1,0:T(8,128)S(1)} %get-tuple-element.43), channel_id=1, source_target_pairs={{0,7},{1,2},{2,1},{3,4},{4,3},{5,6},{6,5},{7,0},{8,15},{9,10},{10,... | collective-permute-start | bytes 196616 | tf_op jit(solution)/shard_map/ppermute | solution.py:436
  29.0 3.9 %collective-permute-start.5 = (f32[2,64,128]{2,1,0:T(8,128)S(1)}, f32[2,64,128]{2,1,0:T(8,128)S(1)}, u32[]{:S(2)}, u32[]{:S(2)}) collective-permute-start(f32[2,64,128]{2,1,0:T(8,128)S(1)} %get-tuple-element.44), channel_id=1, source_target_pairs={{0,1},{1,0},{2,3},{3,2},{4,5},{5,4},{6,7},{7,6},{8,9},{9,8},{10,11... | collective-permute-start | bytes 196616 | tf_op jit(solution)/shard_map/ppermute | solution.py:430
  40.1 6.6 %collective-permute-start.10 = (f32[4,64,128]{2,1,0:T(8,128)S(1)}, f32[4,64,128]{2,1,0:T(8,128)S(1)}, u32[]{:S(2)}, u32[]{:S(2)}) collective-permute-start(f32[4,64,128]{2,1,0:T(8,128)S(1)} %get-tuple-element.53.refs_0_), channel_id=1, source_target_pairs={{0,24},{8,16},{16,8},{24,0},{1,25},{9,17},{17,9},{25,1},{2,26},{10... | collective-permute-start | bytes 393224 | tf_op jit(solution)/shard_map/ppermute | solution.py:430
  43.0 5.0 %collective-permute-start.8 = (f32[4,64,128]{2,1,0:T(8,128)S(1)}, f32[4,64,128]{2,1,0:T(8,128)S(1)}, u32[]{:S(2)}, u32[]{:S(2)}) collective-permute-start(f32[4,64,128]{2,1,0:T(8,128)S(1)} %get-tuple-element.53.refs_0_), channel_id=1, source_target_pairs={{0,8},{8,0},{16,24},{24,16},{1,9},{9,1},{17,25},{25,17},{2,10},{10... | collective-permute-start | bytes 393224 | tf_op jit(solution)/shard_map/ppermute | solution.py:430
  43.5 5.0 %collective-permute-start.9 = (f32[4,64,128]{2,1,0:T(8,128)S(1)}, f32[4,64,128]{2,1,0:T(8,128)S(1)}, u32[]{:S(2)}, u32[]{:S(2)}) collective-permute-start(f32[4,64,128]{2,1,0:T(8,128)S(1)} %get-tuple-element.53.refs_0_), channel_id=1, source_target_pairs={{0,16},{8,24},{16,0},{24,8},{1,17},{9,25},{17,1},{25,9},{2,18},{10... | collective-permute-start | bytes 393224 | tf_op jit(solution)/shard_map/ppermute | solution.py:430
  44.3 4.2 %copy-start.3 = (f32[1024,128]{1,0:T(8,128)S(1)}, f32[1024,128]{1,0:T(8,128)}, u32[]{:S(2)}) copy-start(f32[1024,128]{1,0:T(8,128)} %constant.8.clone.col_table_ref) | copy-start | bytes 1572868
  44.3 4.2 %copy-start.4 = (f32[128,256]{1,0:T(8,128)S(1)}, f32[128,256]{1,0:T(8,128)}, u32[]{:S(2)}) copy-start(f32[128,256]{1,0:T(8,128)} %constant.7.clone.row_table_ref) | copy-start | bytes 393220
  44.3 4.2 %copy-start.6 = (s32[32]{0:T(128)S(1)}, s32[32]{0:T(128)}, u32[]{:S(2)}) copy-start(s32[32]{0:T(128)} %owner_ref.1) | copy-start | bytes 388
  50.2 1.4 %collective-permute-start.11 = (f32[256,128]{1,0:T(8,128)S(1)}, f32[256,128]{1,0:T(8,128)S(1)}, u32[]{:S(2)}, u32[]{:S(2)}) collective-permute-start(f32[256,128]{1,0:T(8,128)S(1)} %get-tuple-element.55), channel_id=1, source_target_pairs={{0,1},{1,0},{2,3},{3,2},{4,5},{5,4},{6,7},{7,6},{8,9},{9,8},{10,11... | collective-permute-start | bytes 393224 | tf_op jit(solution)/shard_map/ppermute | solution.py:430
  51.6 4.3 %collective-permute-start.12 = (f32[128,128]{1,0:T(8,128)S(1)}, f32[128,128]{1,0:T(8,128)S(1)}, u32[]{:S(2)}, u32[]{:S(2)}) collective-permute-start(f32[128,128]{1,0:T(8,128)S(1)} %slice.17), channel_id=1, source_target_pairs={{0,2},{1,3},{2,0},{3,1},{4,6},{5,7},{6,4},{7,5},{8,10},{9,11},{10,... | collective-permute-start | bytes 196616 | tf_op jit(solution)/shard_map/ppermute | solution.py:430
  56.0 4.9 %collective-permute-start.13 = (f32[64,128]{1,0:T(8,128)S(1)}, f32[64,128]{1,0:T(8,128)S(1)}, u32[]{:S(2)}, u32[]{:S(2)}) collective-permute-start(f32[64,128]{1,0:T(8,128)S(1)} %slice.19), channel_id=1, source_target_pairs={{0,4},{1,5},{2,6},{3,7},{4,0},{5,1},{6,2},{7,3},{8,12},{9,13},{10,... | collective-permute-start | bytes 98312 | tf_op jit(solution)/shard_map/ppermute | solution.py:430

commit v6 on v5

--- a/solution.py
+++ b/solution.py
@@ -31,7 +31,7 @@
 F32 = jnp.float32
 PREP_UNROLL = 6
 FACTOR_ROWS, FACTOR_UNROLL = 64, 2
-UNROLLS = {16: (6, 9), 32: (4, 6), 64: (4, 6)}
+UNROLLS = {16: (12, 9), 32: (6, 6), 64: (6, 9)}
 DOWN_UNROLL = 6
 EDGE = 16
 
@@ -48,13 +48,13 @@
     return lax.broadcasted_iota(jnp.int32, (rows, LANES), 0)
 
 
-def loop(count, load, body, init, unroll):
+def loop(count, load, body, init, unroll, prepare=lambda loaded: loaded):
     while count % unroll:
         unroll -= 1
 
     def several(i, carry):
         steps = [i * unroll + j for j in range(unroll)]
-        loaded = [load(step) for step in steps]
+        loaded = prepare([load(step) for step in steps])
         stores = []
         for step, values in zip(steps, loaded):
             carry, store = body(step, values, carry)
@@ -196,7 +196,7 @@
         taken, refs[:] = refs[:count], refs[count:]
         return taken
 
-    ts_ref, uv_ref, flow_ref, w1_ref, w2_ref, h1_ref, h2_ref, cor_ref, col_b, col_a = take(10)
+    ts_ref, uv_ref, flow_ref, w1_ref, w2_ref, h1_ref, h2_ref, cor_ref, band_ref, col_b, col_a = take(11)
     south_ref = north_ref = None
     if stage != "inner":
         row_b, row_a = take(2)
@@ -233,7 +233,6 @@
 
     for block, (first_row, size) in enumerate(blocks):
         lane = lanes_of(size)
-        low_two, high_two = lane < 2, lane >= LANES - 2
         low_one, high_one = lane < 1, lane >= LANES - 1
         zero = jnp.zeros((size, LANES), F32)
         rows = pl.ds(first_row, size)
@@ -261,28 +260,44 @@
             factors = [ref[k, rows, :] for ref in (w1_ref, w2_ref, h1_ref, h2_ref)]
             return east, west, lines, flow, factors
 
+        def along_x(loaded, lane=lane, size=size):
+            fields = [
+                jnp.concatenate([item[2][c][0], jnp.where(lane < LANES // 2, item[0][c], item[1][c])], axis=1)
+                for item in loaded
+                for c in range(2)
+            ]
+            fields = jnp.concatenate(fields, axis=0)
+            high = fields.astype(jnp.bfloat16)
+            low = (fields - high.astype(F32)).astype(jnp.bfloat16)
+            mixed = sum(jnp.dot(part, band_ref[...], preferred_element_type=F32) for part in (high, low))
+            parts = [mixed[i * size : (i + 1) * size] for i in range(2 * len(loaded))]
+            return [
+                (*item, [(part[:, :LANES], part[:, LANES:]) for part in parts[2 * i : 2 * i + 2]])
+                for i, item in enumerate(loaded)
+            ]
+
         def upward(i, loaded, below, cor=cor, rows=kept_rows):
             k = levels - 1 - i
-            east, west, lines, flow, factors = loaded
+            east, west, lines, flow, factors, mixed = loaded
             flow_x = flow[0] * (ADVECT_COEF / 12.0)
             flow_y = flow[1] * (ADVECT_COEF / 12.0)
-            rhs, diff_x, diff_y = [], [], []
+            rhs, diff_y = [], []
             for c in range(2):
                 mid = lines[c][0]
-                e1 = pltpu.roll(jnp.where(low_one, east[c], mid), LANES - 1, 1)
-                w1 = pltpu.roll(jnp.where(high_one, west[c], mid), 1, 1)
-                e2 = pltpu.roll(jnp.where(low_two, east[c], mid), LANES - 2, 1)
-                w2 = pltpu.roll(jnp.where(high_two, west[c], mid), 2, 1)
                 n1, s1, n2, s2 = (lines[c][s] for s in (1, -1, 2, -2))
-                dx, dy = e1 - w1, n1 - s1
-                grad = flow_x * (8.0 * dx - (e2 - w2)) + flow_y * (8.0 * dy - (n2 - s2))
-                near = (e1 + w1) + (n1 + s1)
+                grad_x, near_x = mixed[c]
+                dy = n1 - s1
+                grad = flow_x * grad_x + flow_y * (8.0 * dy - (n2 - s2))
+                near = near_x + (n1 + s1)
                 rhs.append((1.0 - 4.0 * DIFFUSE_COEF) * mid + DIFFUSE_COEF * near + grad)
-                diff_x.append(dx)
                 diff_y.append(dy)
-            push = [
-                (0.5 * PRESSURE_COEF) * (d[0] - SALINE_WEIGHT * d[1]) for d in (diff_x, diff_y)
-            ]
+            buoyant, at_east, at_west = (
+                pair[0] - SALINE_WEIGHT * pair[1] for pair in ((lines[0][0], lines[1][0]), east, west)
+            )
+            diff_x = pltpu.roll(jnp.where(low_one, at_east, buoyant), LANES - 1, 1) - pltpu.roll(
+                jnp.where(high_one, at_west, buoyant), 1, 1
+            )
+            push = [(0.5 * PRESSURE_COEF) * d for d in (diff_x, diff_y[0] - SALINE_WEIGHT * diff_y[1])]
             sides = []
             for c in range(2, 4):
                 mid = lines[c][0]
@@ -307,7 +322,7 @@
 
             return values, store
 
-        top = loop(levels, load_up, upward, (zero,) * 4, up_unroll)
+        top = loop(levels, load_up, upward, (zero,) * 4, up_unroll, along_x)
         for c in range(2):
             if stage == "outer":
                 surface_ref[2 + c, rows, :] = top[c]
@@ -436,6 +451,17 @@
     return lax.ppermute(second, axis, others), swap(first, axis, 1)
 
 
+def band_matrix():
+    band = np.zeros((2 * LANES, 2 * LANES))
+    for out in range(LANES):
+        for shift, gradient, near in ((1, 8, 1), (-1, -8, 1), (2, -1, 0), (-2, 1, 0)):
+            source = out + shift
+            row = source if 0 <= source < LANES else LANES + source % LANES
+            band[row, out] = gradient
+            band[row, LANES + out] = near
+    return band
+
+
 def cosines(total, mode_count):
     phase = (2 * np.arange(total)[:, None] + 1) * np.arange(mode_count)[None, :] % (4 * total)
     return np.cos(phase * (math.pi / (2 * total)))
@@ -474,11 +500,11 @@
     )(rotation, adjoint)
     cols, rows = exchange("tx", *sent[:2]), exchange("ty", *sent[2:])
     w1, w2, h1, h2, g1, g2 = call(factor_kernel, [full] * 6, [VMEM] * 2, work=1 << 22)(vert_diff, wet_levels)
-    coefficients = (background_flow, w1, w2, h1, h2, coriolis)
+    coefficients = (background_flow, w1, w2, h1, h2, coriolis, jnp.asarray(band_matrix(), jnp.bfloat16))
     ts, uv, first, *sent = call(
         functools.partial(step_kernel, "whole", ((0, height),)),
         [pair, pair, surface] + col_pair + row_pair,
-        [VMEM] * 14,
+        [VMEM] * 15,
         rows_scratch + [kept(height)] + cols_scratch + rows_scratch,
         limit=12,
     )(ts, uv, *coefficients, *cols, *rows, g1, g2)
@@ -487,14 +513,14 @@
     inner, inner_surface = call(
         functools.partial(step_kernel, "inner", ((EDGE, middle),)),
         [shape(4, levels, middle, width), shape(2, middle, width)],
-        [VMEM] * 10,
+        [VMEM] * 11,
         cols_scratch,
         work=1 << 24,
     )(ts, uv, *coefficients, *cols)
     outer, surfaces = call(
         functools.partial(step_kernel, "outer", ((0, EDGE), (height - EDGE, EDGE))),
         [shape(4, levels, 2 * EDGE, width), shape(4, height, width)],
-        [VMEM] * 14,
+        [VMEM] * 15,
         cols_scratch + rows_scratch,
     )(ts, uv, *coefficients, *cols, *rows, first, inner_surface)
     parts = [surfaces] + [swap(surfaces, "ty", bit) for bit in range(1, ty)]

time: 61.6 us -> 59.2 us (0.961)
  Pallas kernels: 25.1 us -> 22.6 us
    pallas_call x1, Pallas kernels: 9.17 us -> 7.9 us  [body(): call(functools.partial(step_kernel, 'whole', ((0, height),)), [pair, pair...]
    pallas_call x1, Pallas kernels: 3.65 us -> 2.97 us  [body(): call(functools.partial(step_kernel, 'outer', ((0, EDGE), (height - EDGE,...]
where the time goes in v6:
time: 59.2 us; the launch traced here: 59 us
  Pallas kernels  22.6 us (38%)
  starting transfers between devices  18.1 us (31%)
  waiting for transfers between devices  15.5 us (26%)
  between operations  2.12 us (4%)
  other arithmetic  0.64 us (1%)
    ppermute x4, starting transfers between devices, exchange(): return (lax.ppermute(second, axis, others), swap(first, axis, 1))  9.74 us
    ppermute x10, waiting for transfers between devices, swap(): lax.ppermute(block, axis, [(i, i ^ bit) for i in range(lax.axis_size(axis...  9.42 us
    ppermute x10, starting transfers between devices, swap(): lax.ppermute(block, axis, [(i, i ^ bit) for i in range(lax.axis_size(axis...  8.35 us
    pallas_call x1, Pallas kernels, body(): call(functools.partial(step_kernel, 'whole', ((0, height),)), [pair, pair...  7.9 us
    ppermute x4, waiting for transfers between devices, exchange(): return (lax.ppermute(second, axis, others), swap(first, axis, 1))  6.04 us
    pallas_call x1, Pallas kernels, body(): call(prep_kernel, [pair, pair] + col_pair + row_pair, [SMEM, ANY], [pltpu...  3.64 us
    pallas_call x1, Pallas kernels, body(): call(functools.partial(step_kernel, 'outer', ((0, EDGE), (height - EDGE,...  2.97 us
    pallas_call x1, Pallas kernels, body(): call(functools.partial(step_kernel, 'inner', ((EDGE, middle),)), [shape(4...  2.92 us
  transfers between devices with their start and end apart: 14, of which 8 were waited for; matrix products, arithmetic and copies ran while one was open for 0% of the time, Pallas kernels for 11%

profile of v6, /device:TPU:0, one launch (start us, length us, event | category | flops | bytes accessed | tf_op | source)
XLA Modules:
  0.0 59.0 jit_solution(12507883452086877987)
XLA Ops:
  1.3 0.0 copy-start.1
  1.3 0.0 copy-start.2
  1.3 3.6 %shard_map.122 = (f32[2,36,64,128]{3,2,1,0:T(8,128)S(1)}, f32[2,36,64,128]{3,2,1,0:T(8,128)S(1)}, f32[2,64,128]{2,1,0:T(8,128)S(1)}, f32[2,64,128]{2,1,0:T(8,128...) custom-call(s32[1,1]{1,0:T(1,128)S(6)} %copy.13.rot_ref, f32[4,36,64,128]{3,2,1,0:T(8,128)} %adj_ref.1), custom_call_target="tpu_custom_call" | custom-call | flops 8388608 | bytes 8388608 | tf_op jit(solution)/shard_map/pallas_call | solution.py:493
  5.0 4.0 %collective-permute-start.2 = (f32[36,8,128]{2,1,0:T(8,128)S(1)}, f32[36,8,128]{2,1,0:T(8,128)S(1)}, u32[]{:S(2)}, u32[]{:S(2)}) collective-permute-start(f32[36,8,128]{2,1,0:T(8,128)S(1)} %get-tuple-element.37), channel_id=1, source_target_pairs={{0,24},{8,16},{16,8},{24,0},{1,25},{9,17},{17,9},{25,1},{2,26},{10... | collective-permute-start | bytes 442376 | tf_op jit(solution)/shard_map/ppermute | solution.py:451
  8.9 0.5 collective-permute-start.3
  9.5 2.5 %collective-permute-start = (f32[2,64,128]{2,1,0:T(8,128)S(1)}, f32[2,64,128]{2,1,0:T(8,128)S(1)}, u32[]{:S(2)}, u32[]{:S(2)}) collective-permute-start(f32[2,64,128]{2,1,0:T(8,128)S(1)} %get-tuple-element.35), channel_id=1, source_target_pairs={{0,7},{1,2},{2,1},{3,4},{4,3},{5,6},{6,5},{7,0},{8,15},{9,10},{10,... | collective-permute-start | bytes 196616 | tf_op jit(solution)/shard_map/ppermute | solution.py:451
  12.0 1.2 %shard_map.123 = (f32[36,64,128]{2,1,0:T(8,128)S(1)}, f32[36,64,128]{2,1,0:T(8,128)S(1)}, f32[36,64,128]{2,1,0:T(8,128)S(1)}, f32[36,64,128]{2,1,0:T(8,128)S(1)}...) custom-call(f32[36,64,128]{2,1,0:T(8,128)S(1)} %copy-done.3, s32[64,128]{1,0:T(8,128)S(1)} %copy-done.6), custom_call_target="tpu_custom_call" | custom-call | flops 4194304 | bytes 4194304 | tf_op jit(solution)/shard_map/pallas_call | solution.py:502
  13.2 2.2 %collective-permute-done.refs_9_ = f32[2,64,128]{2,1,0:T(8,128)S(1)} collective-permute-done((f32[2,64,128]{2,1,0:T(8,128)S(1)}, f32[2,64,128]{2,1,0:T(8,128)S(1)}, u32[]{:S(2)}, u32[]{:S(2)}) %collective-permute-start) | collective-permute-done | bytes 65568 | tf_op jit(solution)/shard_map/ppermute | solution.py:451
  15.4 0.8 %collective-permute-done.3.refs_12_ = f32[36,8,128]{2,1,0:T(8,128)S(1)} collective-permute-done((f32[36,8,128]{2,1,0:T(8,128)S(1)}, f32[36,8,128]{2,1,0:T(8,128)S(1)}, u32[]{:S(2)}, u32[]{:S(2)}) %collective-permute-start.3) | collective-permute-done | bytes 147488 | tf_op jit(solution)/shard_map/ppermute | solution.py:445
  16.2 7.9 %shard_map.124 = (f32[2,36,64,128]{3,2,1,0:T(8,128)S(1)}, f32[2,36,64,128]{3,2,1,0:T(8,128)S(1)}, f32[2,64,128]{2,1,0:T(8,128)S(1)}, f32[2,64,128]{2,1,0:T(8,128...) custom-call(f32[2,36,64,128]{3,2,1,0:T(8,128)S(1)} %get-tuple-element.29.refs_0_, ...), custom_call_target="tpu_custom_call" | custom-call | tf_op jit(solution)/shard_map/pallas_call | solution.py:504
  24.1 1.5 %collective-permute-start.6 = (f32[36,8,128]{2,1,0:T(8,128)S(1)}, f32[36,8,128]{2,1,0:T(8,128)S(1)}, u32[]{:S(2)}, u32[]{:S(2)}) collective-permute-start(f32[36,8,128]{2,1,0:T(8,128)S(1)} %get-tuple-element.46), channel_id=1, source_target_pairs={{0,24},{8,16},{16,8},{24,0},{1,25},{9,17},{17,9},{25,1},{2,26},{10... | collective-permute-start | bytes 442376 | tf_op jit(solution)/shard_map/ppermute | solution.py:451
  25.6 0.3 collective-permute-start.7
  26.0 1.8 %collective-permute-start.4 = (f32[2,64,128]{2,1,0:T(8,128)S(1)}, f32[2,64,128]{2,1,0:T(8,128)S(1)}, u32[]{:S(2)}, u32[]{:S(2)}) collective-permute-start(f32[2,64,128]{2,1,0:T(8,128)S(1)} %get-tuple-element.43), channel_id=1, source_target_pairs={{0,7},{1,2},{2,1},{3,4},{4,3},{5,6},{6,5},{7,0},{8,15},{9,10},{10,... | collective-permute-start | bytes 196616 | tf_op jit(solution)/shard_map/ppermute | solution.py:451
  27.8 0.1 collective-permute-start.5
  27.8 3.8 %collective-permute-done.4.refs_9_ = f32[2,64,128]{2,1,0:T(8,128)S(1)} collective-permute-done((f32[2,64,128]{2,1,0:T(8,128)S(1)}, f32[2,64,128]{2,1,0:T(8,128)S(1)}, u32[]{:S(2)}, u32[]{:S(2)}) %collective-permute-start.4) | collective-permute-done | bytes 65568 | tf_op jit(solution)/shard_map/ppermute | solution.py:451
  31.7 2.9 %shard_map.125 = (f32[4,36,32,128]{3,2,1,0:T(8,128)S(1)}, f32[2,32,128]{2,1,0:T(8,128)S(1)}) custom-call(f32[2,36,64,128]{3,2,1,0:T(8,128)S(1)} %get-tuple-element.41.refs_0_, f32[2,36,64,128]{3,2,1,0:T(8,128)S(1)} %get-tuple-element.42.refs_1_, f32[2,36,64,128]{3,2,1,0:T(8,128)S(1)} %copy-done, f32[36,64,128]{2,1,0:T(8,128)S(1)} %get-tuple-element.31.refs_3_, ...), custom_call_target="tpu_custom_call" | custom-call | flops 16777216 | bytes 16777216 | tf_op jit(solution)/shard_map/pallas_call | solution.py:513
  34.6 3.0 %shard_map.126 = (f32[4,36,32,128]{3,2,1,0:T(8,128)S(1)}, f32[4,64,128]{2,1,0:T(8,128)S(1)}) custom-call(f32[2,36,64,128]{3,2,1,0:T(8,128)S(1)} %get-tuple-element.41.refs_0_, f32[2,36,64,128]{3,2,1,0:T(8,128)S(1)} %get-tuple-element.42.refs_1_, f32[2,36,64,128]{3,2,1,0:T(8,128)S(1)} %copy-done, f32[36,64,128]{2,1,0:T(8,128)S(1)} %get-tuple-element.31.refs_3_, ...), custom_call_target="tpu_custom_call" | custom-call | tf_op jit(solution)/shard_map/pallas_call | solution.py:520
  37.6 2.9 %collective-permute-start.10 = (f32[4,64,128]{2,1,0:T(8,128)S(1)}, f32[4,64,128]{2,1,0:T(8,128)S(1)}, u32[]{:S(2)}, u32[]{:S(2)}) collective-permute-start(f32[4,64,128]{2,1,0:T(8,128)S(1)} %get-tuple-element.53.refs_0_), channel_id=1, source_target_pairs={{0,24},{8,16},{16,8},{24,0},{1,25},{9,17},{17,9},{25,1},{2,26},{10... | collective-permute-start | bytes 393224 | tf_op jit(solution)/shard_map/ppermute | solution.py:445
  40.5 0.5 collective-permute-start.8
  41.1 0.1 collective-permute-start.9
  41.8 0.0 copy-start.4
  41.9 2.3 %shard_map.127 = (f32[4,36,64,128]{3,2,1,0:T(8,128)}, f32[8,128]{1,0:T(8,128)S(1)}) custom-call(s32[1,1]{1,0:T(1,128)S(6)} %copy.13.rot_ref, f32[4,36,32,128]{3,2,1,0:T(8,128)S(1)} %get-tuple-element.45.inner_ref, f32[4,36,32,128]{3,2,1,0:T(8,128)S(1)} %get-tuple-element.50.outer_ref, f32[36,64,128]{2,1,0:T(8,128)S(1)} %get-tuple-element.39.refs_13_.g1_ref, ...), custom_call_target="tpu_custom_call" | custom-call | flops 8388608 | bytes 8388608 | tf_op jit(solution)/shard_map/pallas_call | solution.py:527
  44.2 1.3 %collective-permute-done.8.refs_1_ = f32[4,64,128]{2,1,0:T(8,128)S(1)} collective-permute-done((f32[4,64,128]{2,1,0:T(8,128)S(1)}, f32[4,64,128]{2,1,0:T(8,128)S(1)}, u32[]{:S(2)}, u32[]{:S(2)}) %collective-permute-start.8) | collective-permute-done | bytes 131104 | tf_op jit(solution)/shard_map/ppermute | solution.py:445
  45.5 0.5 collective-permute-done.9.refs_2_
  46.0 1.7 %shard_map.128 = (f32[256,128]{1,0:T(8,128)S(1)}, f32[256,128]{1,0:T(8,128)S(1)}) custom-call(s32[32]{0:T(128)S(1)} %copy-done.7, s32[1,1]{1,0:T(1,128)S(6)} %copy.14.face_ref, f32[128,256]{1,0:T(8,128)S(1)} %copy-done.5, f32[1024,128]{1,0:T(8,128)S(1)} %copy-done.4, f32[8,128]{1,0:T(8,128)S(1)} %get-tuple-element.52._, ...), custom_call_target="tpu_custom_call" | custom-call | tf_op jit(solution)/shard_map/pallas_call | solution.py:537
  47.7 0.1 collective-permute-start.11
  47.8 1.3 %collective-permute-done.11 = f32[256,128]{1,0:T(8,128)S(1)} collective-permute-done((f32[256,128]{1,0:T(8,128)S(1)}, f32[256,128]{1,0:T(8,128)S(1)}, u32[]{:S(2)}, u32[]{:S(2)}) %collective-permute-start.11) | collective-permute-done | bytes 131104 | tf_op jit(solution)/shard_map/ppermute | solution.py:445
  49.1 1.5 %collective-permute-start.12 = (f32[128,128]{1,0:T(8,128)S(1)}, f32[128,128]{1,0:T(8,128)S(1)}, u32[]{:S(2)}, u32[]{:S(2)}) collective-permute-start(f32[128,128]{1,0:T(8,128)S(1)} %slice.17), channel_id=1, source_target_pairs={{0,2},{1,3},{2,0},{3,1},{4,6},{5,7},{6,4},{7,5},{8,10},{9,11},{10,... | collective-permute-start | bytes 196616 | tf_op jit(solution)/shard_map/ppermute | solution.py:445
  50.7 2.8 %collective-permute-done.12 = f32[128,128]{1,0:T(8,128)S(1)} collective-permute-done((f32[128,128]{1,0:T(8,128)S(1)}, f32[128,128]{1,0:T(8,128)S(1)}, u32[]{:S(2)}, u32[]{:S(2)}) %collective-permute-start.12) | collective-permute-done | bytes 65568 | tf_op jit(solution)/shard_map/ppermute | solution.py:445
  53.5 2.2 %collective-permute-start.13 = (f32[64,128]{1,0:T(8,128)S(1)}, f32[64,128]{1,0:T(8,128)S(1)}, u32[]{:S(2)}, u32[]{:S(2)}) collective-permute-start(f32[64,128]{1,0:T(8,128)S(1)} %slice.19), channel_id=1, source_target_pairs={{0,4},{1,5},{2,6},{3,7},{4,0},{5,1},{6,2},{7,3},{8,12},{9,13},{10,... | collective-permute-start | bytes 98312 | tf_op jit(solution)/shard_map/ppermute | solution.py:445
  55.7 2.6 %collective-permute-done.13 = f32[64,128]{1,0:T(8,128)S(1)} collective-permute-done((f32[64,128]{1,0:T(8,128)S(1)}, f32[64,128]{1,0:T(8,128)S(1)}, u32[]{:S(2)}, u32[]{:S(2)}) %collective-permute-start.13) | collective-permute-done | bytes 32800 | tf_op jit(solution)/shard_map/ppermute | solution.py:445
  58.4 0.6 %slice_add_fusion.1 = f32[64,128]{1,0:T(8,128)} fusion(f32[64,128]{1,0:T(8,128)S(1)} %collective-permute-done.13, f32[128,128]{1,0:T(8,128)S(1)} %slice_add_fusion), kind=kLoop, calls=%fused_computation.1 | loop fusion | flops 8192 | bytes 98304 | tf_op jit(solution)/shard_map/add | solution.py:546
  (24 shorter events, 0.1 us)
Async XLA Ops:
  1.3 10.7 %copy-start.3 = (f32[36,64,128]{2,1,0:T(8,128)S(1)}, f32[36,64,128]{2,1,0:T(8,128)}, u32[]{:S(2)}) copy-start(f32[36,64,128]{2,1,0:T(8,128)} %vd_ref.1) | copy-start | bytes 3538948
  1.3 10.7 %copy-start.6 = (s32[64,128]{1,0:T(8,128)S(1)}, s32[64,128]{1,0:T(8,128)}, u32[]{:S(2)}) copy-start(s32[64,128]{1,0:T(8,128)} %wet_ref.1) | copy-start | bytes 98308
  1.3 14.9 %copy-start = (f32[2,36,64,128]{3,2,1,0:T(8,128)S(1)}, f32[2,36,64,128]{3,2,1,0:T(8,128)}, u32[]{:S(2)}) copy-start(f32[2,36,64,128]{3,2,1,0:T(8,128)} %refs_2_.5) | copy-start | bytes 7077892
  1.3 14.9 %copy-start.1 = (bf16[256,256]{1,0:T(8,128)(2,1)S(1)}, bf16[256,256]{1,0:T(8,128)(2,1)}, u32[]{:S(2)}) copy-start(bf16[256,256]{1,0:T(8,128)(2,1)} %constant.11.clone.refs_8_) | copy-start | bytes 393220
  1.3 14.9 %copy-start.2 = (f32[256,128]{1,0:T(8,128)S(1)}, f32[256,128]{1,0:T(8,128)}, u32[]{:S(2)}) copy-start(f32[256,128]{1,0:T(8,128)} %constant.8.clone.refs_7_) | copy-start | bytes 393220
  5.0 10.4 %collective-permute-start.2 = (f32[36,8,128]{2,1,0:T(8,128)S(1)}, f32[36,8,128]{2,1,0:T(8,128)S(1)}, u32[]{:S(2)}, u32[]{:S(2)}) collective-permute-start(f32[36,8,128]{2,1,0:T(8,128)S(1)} %get-tuple-element.37), channel_id=1, source_target_pairs={{0,24},{8,16},{16,8},{24,0},{1,25},{9,17},{17,9},{25,1},{2,26},{10... | collective-permute-start | bytes 442376 | tf_op jit(solution)/shard_map/ppermute | solution.py:451
  8.9 7.3 %collective-permute-start.3 = (f32[36,8,128]{2,1,0:T(8,128)S(1)}, f32[36,8,128]{2,1,0:T(8,128)S(1)}, u32[]{:S(2)}, u32[]{:S(2)}) collective-permute-start(f32[36,8,128]{2,1,0:T(8,128)S(1)} %get-tuple-element.38), channel_id=1, source_target_pairs={{0,8},{8,0},{16,24},{24,16},{1,9},{9,1},{17,25},{25,17},{2,10},{10... | collective-permute-start | bytes 442376 | tf_op jit(solution)/shard_map/ppermute | solution.py:445
  9.5 5.9 %collective-permute-start = (f32[2,64,128]{2,1,0:T(8,128)S(1)}, f32[2,64,128]{2,1,0:T(8,128)S(1)}, u32[]{:S(2)}, u32[]{:S(2)}) collective-permute-start(f32[2,64,128]{2,1,0:T(8,128)S(1)} %get-tuple-element.35), channel_id=1, source_target_pairs={{0,7},{1,2},{2,1},{3,4},{4,3},{5,6},{6,5},{7,0},{8,15},{9,10},{10,... | collective-permute-start | bytes 196616 | tf_op jit(solution)/shard_map/ppermute | solution.py:451
  12.0 3.4 %collective-permute-start.1 = (f32[2,64,128]{2,1,0:T(8,128)S(1)}, f32[2,64,128]{2,1,0:T(8,128)S(1)}, u32[]{:S(2)}, u32[]{:S(2)}) collective-permute-start(f32[2,64,128]{2,1,0:T(8,128)S(1)} %get-tuple-element.36), channel_id=1, source_target_pairs={{0,1},{1,0},{2,3},{3,2},{4,5},{5,4},{6,7},{7,6},{8,9},{9,8},{10,11... | collective-permute-start | bytes 196616 | tf_op jit(solution)/shard_map/ppermute | solution.py:445
  24.1 10.5 %collective-permute-start.6 = (f32[36,8,128]{2,1,0:T(8,128)S(1)}, f32[36,8,128]{2,1,0:T(8,128)S(1)}, u32[]{:S(2)}, u32[]{:S(2)}) collective-permute-start(f32[36,8,128]{2,1,0:T(8,128)S(1)} %get-tuple-element.46), channel_id=1, source_target_pairs={{0,24},{8,16},{16,8},{24,0},{1,25},{9,17},{17,9},{25,1},{2,26},{10... | collective-permute-start | bytes 442376 | tf_op jit(solution)/shard_map/ppermute | solution.py:451
  25.6 9.0 %collective-permute-start.7 = (f32[36,8,128]{2,1,0:T(8,128)S(1)}, f32[36,8,128]{2,1,0:T(8,128)S(1)}, u32[]{:S(2)}, u32[]{:S(2)}) collective-permute-start(f32[36,8,128]{2,1,0:T(8,128)S(1)} %get-tuple-element.47), channel_id=1, source_target_pairs={{0,8},{8,0},{16,24},{24,16},{1,9},{9,1},{17,25},{25,17},{2,10},{10... | collective-permute-start | bytes 442376 | tf_op jit(solution)/shard_map/ppermute | solution.py:445
  26.0 5.7 %collective-permute-start.4 = (f32[2,64,128]{2,1,0:T(8,128)S(1)}, f32[2,64,128]{2,1,0:T(8,128)S(1)}, u32[]{:S(2)}, u32[]{:S(2)}) collective-permute-start(f32[2,64,128]{2,1,0:T(8,128)S(1)} %get-tuple-element.43), channel_id=1, source_target_pairs={{0,7},{1,2},{2,1},{3,4},{4,3},{5,6},{6,5},{7,0},{8,15},{9,10},{10,... | collective-permute-start | bytes 196616 | tf_op jit(solution)/shard_map/ppermute | solution.py:451
  27.8 3.9 %collective-permute-start.5 = (f32[2,64,128]{2,1,0:T(8,128)S(1)}, f32[2,64,128]{2,1,0:T(8,128)S(1)}, u32[]{:S(2)}, u32[]{:S(2)}) collective-permute-start(f32[2,64,128]{2,1,0:T(8,128)S(1)} %get-tuple-element.44), channel_id=1, source_target_pairs={{0,1},{1,0},{2,3},{3,2},{4,5},{5,4},{6,7},{7,6},{8,9},{9,8},{10,11... | collective-permute-start | bytes 196616 | tf_op jit(solution)/shard_map/ppermute | solution.py:445
  37.6 6.6 %collective-permute-start.10 = (f32[4,64,128]{2,1,0:T(8,128)S(1)}, f32[4,64,128]{2,1,0:T(8,128)S(1)}, u32[]{:S(2)}, u32[]{:S(2)}) collective-permute-start(f32[4,64,128]{2,1,0:T(8,128)S(1)} %get-tuple-element.53.refs_0_), channel_id=1, source_target_pairs={{0,24},{8,16},{16,8},{24,0},{1,25},{9,17},{17,9},{25,1},{2,26},{10... | collective-permute-start | bytes 393224 | tf_op jit(solution)/shard_map/ppermute | solution.py:445
  40.5 5.0 %collective-permute-start.8 = (f32[4,64,128]{2,1,0:T(8,128)S(1)}, f32[4,64,128]{2,1,0:T(8,128)S(1)}, u32[]{:S(2)}, u32[]{:S(2)}) collective-permute-start(f32[4,64,128]{2,1,0:T(8,128)S(1)} %get-tuple-element.53.refs_0_), channel_id=1, source_target_pairs={{0,8},{8,0},{16,24},{24,16},{1,9},{9,1},{17,25},{25,17},{2,10},{10... | collective-permute-start | bytes 393224 | tf_op jit(solution)/shard_map/ppermute | solution.py:445
  41.1 5.0 %collective-permute-start.9 = (f32[4,64,128]{2,1,0:T(8,128)S(1)}, f32[4,64,128]{2,1,0:T(8,128)S(1)}, u32[]{:S(2)}, u32[]{:S(2)}) collective-permute-start(f32[4,64,128]{2,1,0:T(8,128)S(1)} %get-tuple-element.53.refs_0_), channel_id=1, source_target_pairs={{0,16},{8,24},{16,0},{24,8},{1,17},{9,25},{17,1},{25,9},{2,18},{10... | collective-permute-start | bytes 393224 | tf_op jit(solution)/shard_map/ppermute | solution.py:445
  41.8 4.2 %copy-start.4 = (f32[1024,128]{1,0:T(8,128)S(1)}, f32[1024,128]{1,0:T(8,128)}, u32[]{:S(2)}) copy-start(f32[1024,128]{1,0:T(8,128)} %constant.10.clone.col_table_ref) | copy-start | bytes 1572868
  41.8 4.2 %copy-start.5 = (f32[128,256]{1,0:T(8,128)S(1)}, f32[128,256]{1,0:T(8,128)}, u32[]{:S(2)}) copy-start(f32[128,256]{1,0:T(8,128)} %constant.9.clone.row_table_ref) | copy-start | bytes 393220
  41.9 4.2 %copy-start.7 = (s32[32]{0:T(128)S(1)}, s32[32]{0:T(128)}, u32[]{:S(2)}) copy-start(s32[32]{0:T(128)} %owner_ref.1) | copy-start | bytes 388
  47.7 1.4 %collective-permute-start.11 = (f32[256,128]{1,0:T(8,128)S(1)}, f32[256,128]{1,0:T(8,128)S(1)}, u32[]{:S(2)}, u32[]{:S(2)}) collective-permute-start(f32[256,128]{1,0:T(8,128)S(1)} %get-tuple-element.55), channel_id=1, source_target_pairs={{0,1},{1,0},{2,3},{3,2},{4,5},{5,4},{6,7},{7,6},{8,9},{9,8},{10,11... | collective-permute-start | bytes 393224 | tf_op jit(solution)/shard_map/ppermute | solution.py:445
  49.1 4.3 %collective-permute-start.12 = (f32[128,128]{1,0:T(8,128)S(1)}, f32[128,128]{1,0:T(8,128)S(1)}, u32[]{:S(2)}, u32[]{:S(2)}) collective-permute-start(f32[128,128]{1,0:T(8,128)S(1)} %slice.17), channel_id=1, source_target_pairs={{0,2},{1,3},{2,0},{3,1},{4,6},{5,7},{6,4},{7,5},{8,10},{9,11},{10,... | collective-permute-start | bytes 196616 | tf_op jit(solution)/shard_map/ppermute | solution.py:445
  53.5 4.9 %collective-permute-start.13 = (f32[64,128]{1,0:T(8,128)S(1)}, f32[64,128]{1,0:T(8,128)S(1)}, u32[]{:S(2)}, u32[]{:S(2)}) collective-permute-start(f32[64,128]{1,0:T(8,128)S(1)} %slice.19), channel_id=1, source_target_pairs={{0,4},{1,5},{2,6},{3,7},{4,0},{5,1},{6,2},{7,3},{8,12},{9,13},{10,... | collective-permute-start | bytes 98312 | tf_op jit(solution)/shard_map/ppermute | solution.py:445

commit v7 on v6

--- a/solution.py
+++ b/solution.py
@@ -72,16 +72,27 @@
     return cosine, sine
 
 
-def pack_columns(acc, k, fields, lane):
-    at = 3 * k
-    first, second, third = lane >= at, lane >= at + 1, lane >= at + 2
-    east, west = [], []
+def pack_columns(acc, k, fields, lane, split):
+    tracer, flow = (lane >= 4 * k) & (lane < split), lane >= split + 2 * k
+    packed = []
     for g in range(2):
-        tracer, flow = fields[g], fields[g + 2]
-        rolled = pltpu.roll(tracer, at + 2, 1)
-        east.append(jnp.where(first, jnp.where(third, pltpu.roll(flow, at + 3, 1), rolled), acc[g]))
-        west.append(jnp.where(second, jnp.where(third, rolled, pltpu.roll(flow, at + 1, 1)), acc[g + 2]))
-    return tuple(east + west)
+        rolled = jnp.where(tracer, pltpu.roll(fields[g], 4 * k + 2, 1), acc[g])
+        packed.append(jnp.where(flow, pltpu.roll(fields[g + 2], split + 1 + 2 * k, 1), rolled))
+    return tuple(packed)
+
+
+def lane_moves(height, split):
+    lane = lanes_of(height)
+    tracer = lane < split
+    first = jnp.where(tracer, lane % 4, 2 * (lane % 2)) < 2
+
+    def up(x):
+        return jnp.where(tracer, pltpu.roll(x, 2, 1), pltpu.roll(x, 1, 1))
+
+    def down(x):
+        return jnp.where(tracer, pltpu.roll(x, LANES - 2, 1), pltpu.roll(x, LANES - 1, 1))
+
+    return first, up, down
 
 
 def store_edge_rows(k, fields, ends, south_ref, north_ref):
@@ -100,10 +111,14 @@
     row_b[...] = jnp.where(even, south, north)
 
 
-def write_columns(col_a, col_b, east, west):
+def write_columns(col_a, col_b, low, high, split):
     even = lax.axis_index("tx") % 2 == 0
-    col_a[...] = jnp.where(even, east, west)
-    col_b[...] = jnp.where(even, west, east)
+    first, up, down = lane_moves(low[0].shape[0], split)
+    for g in range(2):
+        east = jnp.where(first, low[g], up(high[g]))
+        west = jnp.where(first, down(low[g]), high[g])
+        col_a[g] = jnp.where(even, east, west)
+        col_b[g] = jnp.where(even, west, east)
 
 
 def read_rows(row_a, row_b, south_ref, north_ref):
@@ -114,11 +129,14 @@
     north_ref[...] = jnp.where(here == lax.axis_size("ty") - 1, 0.0, jnp.where(even, first, second))
 
 
-def read_columns(col_a, col_b, east_ref, west_ref):
+def read_columns(col_a, col_b, halo_ref, split):
     even = lax.axis_index("tx") % 2 == 0
-    first, second = col_a[...], col_b[...]
-    east_ref[...] = jnp.where(even, first, second)
-    west_ref[...] = jnp.where(even, second, first)
+    first, up, down = lane_moves(col_a.shape[1], split)
+    for g in range(2):
+        from_east = jnp.where(even, col_a[g], col_b[g])
+        from_west = jnp.where(even, col_b[g], col_a[g])
+        halo_ref[g, 0] = jnp.where(first, from_west, up(from_east))
+        halo_ref[g, 1] = jnp.where(first, down(from_west), from_east)
 
 
 def prep_kernel(rot_ref, adj_ref, ts_ref, uv_ref, col_a, col_b, row_a, row_b, raw_ref, south_ref, north_ref, sems):
@@ -135,7 +153,8 @@
             copies.append(copy)
     lane = lanes_of(height)
     zero = jnp.zeros((height, LANES), F32)
-    acc = (zero,) * 4
+    half = levels // 2
+    accs = [(zero,) * 2, (zero,) * 2]
     for i in range(chunks):
         copies[2 * i].wait()
         copies[2 * i + 1].wait()
@@ -144,14 +163,14 @@
         stores = []
         for k, (t, s, a, b) in zip(group, loaded):
             fields = (t, s, cosine * a - sine * b, sine * a + cosine * b)
-            acc = pack_columns(acc, k, fields, lane)
+            accs[k // half] = pack_columns(accs[k // half], k % half, fields, lane, 4 * half)
             stores.append((k, fields))
         for k, fields in stores:
             uv_ref[0, k] = fields[2]
             uv_ref[1, k] = fields[3]
             store_edge_rows(k, fields, (True, True), south_ref, north_ref)
     write_rows(row_a, row_b, south_ref, north_ref)
-    write_columns(col_a, col_b, jnp.stack(acc[:2]), jnp.stack(acc[2:]))
+    write_columns(col_a, col_b, *accs, 4 * half)
 
 
 def factor_kernel(vd_ref, wet_ref, w1_ref, w2_ref, h1_ref, h2_ref, g1_ref, g2_ref):
@@ -208,8 +227,10 @@
         south_out, north_out, value_ref = take(3)
     else:
         value_ref, surface_ref = take(2)
-    east_ref, west_ref = take(2)
-    read_columns(col_a, col_b, east_ref, west_ref)
+    (halo_ref,) = take(1)
+    half = ts_ref.shape[1] // 2
+    split = 4 * half
+    read_columns(col_a, col_b, halo_ref, split)
     if stage != "inner":
         south_ref, north_ref = take(2)
         read_rows(row_a, row_b, south_ref, north_ref)
@@ -252,17 +273,19 @@
         def load_up(i, rows=rows, ends=(south_end, north_end), fetch=fetch):
             k = levels - 1 - i
             halos = (south_ref[k] if ends[0] else None, north_ref[k] if ends[1] else None)
-            turn = LANES - 2 - 3 * k
-            east = [pltpu.roll(east_ref[g, rows, :], turn, 1) for g in range(2)]
-            west = [pltpu.roll(west_ref[g, rows, :], turn, 1) for g in range(2)]
+            part = jnp.where(k >= half, 1, 0)
+            place = k - half * part
+            packed = [halo_ref[g, part, rows, :] for g in range(2)]
+            edges = [pltpu.roll(x, LANES - 2 - 4 * place, 1) for x in packed]
+            edges += [pltpu.roll(x, LANES - 1 - split - 2 * place, 1) for x in packed]
             lines = [{s: fetch(c, k, s, halos) for s in ((0, 1, -1, 2, -2) if c < 2 else (0, 1, -1))} for c in range(4)]
             flow = [flow_ref[i, k, rows, :] for i in range(2)]
             factors = [ref[k, rows, :] for ref in (w1_ref, w2_ref, h1_ref, h2_ref)]
-            return east, west, lines, flow, factors
-
-        def along_x(loaded, lane=lane, size=size):
+            return edges, lines, flow, factors
+
+        def along_x(loaded, size=size):
             fields = [
-                jnp.concatenate([item[2][c][0], jnp.where(lane < LANES // 2, item[0][c], item[1][c])], axis=1)
+                jnp.concatenate([item[1][c][0], item[0][c]], axis=1)
                 for item in loaded
                 for c in range(2)
             ]
@@ -278,7 +301,7 @@
 
         def upward(i, loaded, below, cor=cor, rows=kept_rows):
             k = levels - 1 - i
-            east, west, lines, flow, factors, mixed = loaded
+            edges, lines, flow, factors, mixed = loaded
             flow_x = flow[0] * (ADVECT_COEF / 12.0)
             flow_y = flow[1] * (ADVECT_COEF / 12.0)
             rhs, diff_y = [], []
@@ -291,18 +314,16 @@
                 near = near_x + (n1 + s1)
                 rhs.append((1.0 - 4.0 * DIFFUSE_COEF) * mid + DIFFUSE_COEF * near + grad)
                 diff_y.append(dy)
-            buoyant, at_east, at_west = (
-                pair[0] - SALINE_WEIGHT * pair[1] for pair in ((lines[0][0], lines[1][0]), east, west)
-            )
-            diff_x = pltpu.roll(jnp.where(low_one, at_east, buoyant), LANES - 1, 1) - pltpu.roll(
-                jnp.where(high_one, at_west, buoyant), 1, 1
+            buoyant, at_edge = (pair[0] - SALINE_WEIGHT * pair[1] for pair in ((lines[0][0], lines[1][0]), edges))
+            diff_x = pltpu.roll(jnp.where(low_one, at_edge, buoyant), LANES - 1, 1) - pltpu.roll(
+                jnp.where(high_one, at_edge, buoyant), 1, 1
             )
             push = [(0.5 * PRESSURE_COEF) * d for d in (diff_x, diff_y[0] - SALINE_WEIGHT * diff_y[1])]
             sides = []
             for c in range(2, 4):
                 mid = lines[c][0]
-                e1 = jnp.where(high_one, east[c - 2], pltpu.roll(mid, LANES - 1, 1))
-                w1 = jnp.where(low_one, west[c - 2], pltpu.roll(mid, 1, 1))
+                e1 = pltpu.roll(jnp.where(low_one, edges[c], mid), LANES - 1, 1)
+                w1 = pltpu.roll(jnp.where(high_one, edges[c], mid), 1, 1)
                 n1, s1 = lines[c][1], lines[c][-1]
                 near = (e1 + w1) + (n1 + s1)
                 sides.append(e1 - w1 if c == 2 else n1 - s1)
@@ -331,11 +352,13 @@
         if stage != "whole":
             continue
 
-        def load_down(k, rows=rows, kept_rows=kept_rows):
+        def load_down(k, rows=rows, kept_rows=kept_rows, base=0):
+            k = base + k
             values = [value_ref[c, k, kept_rows, :] for c in range(4)]
             return values, (g1_ref[k, rows, :], g2_ref[k, rows, :])
 
-        def downward(k, loaded, carry, rows=rows, ends=(south_end, north_end), lane=lane):
+        def downward(place, loaded, carry, rows=rows, ends=(south_end, north_end), lane=lane, base=0):
+            k = base + place
             above, acc = carry
             values, gains = loaded
             fields = tuple(values[c] + gains[c // 2] * above[c] for c in range(4))
@@ -346,11 +369,15 @@
                     uv_out[c, k, rows, :] = fields[c + 2]
                 store_edge_rows(k, fields, ends, south_out, north_out)
 
-            return (fields, pack_columns(acc, k, fields, lane)), store
-
-        _, acc = loop(levels, load_down, downward, ((zero,) * 4, (zero,) * 4), down_unroll)
+            return (fields, pack_columns(acc, place, fields, lane, split)), store
+
+        fields, accs = (zero,) * 4, []
+        for base in (0, half):
+            load, sweep = functools.partial(load_down, base=base), functools.partial(downward, base=base)
+            fields, acc = loop(half, load, sweep, (fields, (zero,) * 2), down_unroll)
+            accs.append(acc)
         write_rows(sent[2], sent[3], south_out, north_out)
-        write_columns(sent[0], sent[1], jnp.stack(acc[:2]), jnp.stack(acc[2:]))
+        write_columns(sent[0], sent[1], *accs, split)
     if stage == "outer":
         surface_ref[0:2] = first_ref[...]
         for c in range(2):
@@ -475,7 +502,7 @@
     pair = shape(2, levels, height, width)
     row_pair, col_pair = [shape(levels, TILE, width)] * 2, [shape(2, height, LANES)] * 2
     rows_scratch = [pltpu.VMEM((levels, TILE, width), F32)] * 2
-    cols_scratch = [pltpu.VMEM((2, height, LANES), F32)] * 2
+    cols_scratch = [pltpu.VMEM((2, 2, height, LANES), F32)]
     surface = shape(2, height, width)
 
     def kept(rows):

time: 59.2 us -> 58.1 us (0.981)
  Pallas kernels: 22.6 us -> 21.6 us
    pallas_call x1, Pallas kernels: 7.9 us -> 7.29 us  [body(): call(functools.partial(step_kernel, 'whole', ((0, height),)), [pair, pair...]
where the time goes in v7:
time: 58.1 us; the launch traced here: 58 us
  Pallas kernels  21.6 us (37%)
  starting transfers between devices  18.1 us (31%)
  waiting for transfers between devices  15.5 us (27%)
  between operations  2.12 us (4%)
  other arithmetic  0.64 us (1%)
    ppermute x4, starting transfers between devices, exchange(): return (lax.ppermute(second, axis, others), swap(first, axis, 1))  9.74 us
    ppermute x10, waiting for transfers between devices, swap(): lax.ppermute(block, axis, [(i, i ^ bit) for i in range(lax.axis_size(axis...  9.42 us
    ppermute x10, starting transfers between devices, swap(): lax.ppermute(block, axis, [(i, i ^ bit) for i in range(lax.axis_size(axis...  8.35 us
    pallas_call x1, Pallas kernels, body(): call(functools.partial(step_kernel, 'whole', ((0, height),)), [pair, pair...  7.29 us
    ppermute x4, waiting for transfers between devices, exchange(): return (lax.ppermute(second, axis, others), swap(first, axis, 1))  6.04 us
    pallas_call x1, Pallas kernels, body(): call(prep_kernel, [pair, pair] + col_pair + row_pair, [SMEM, ANY], [pltpu...  3.15 us
    pallas_call x1, Pallas kernels, body(): call(functools.partial(step_kernel, 'outer', ((0, EDGE), (height - EDGE,...  3.01 us
    pallas_call x1, Pallas kernels, body(): call(functools.partial(step_kernel, 'inner', ((EDGE, middle),)), [shape(4...  2.98 us
  transfers between devices with their start and end apart: 14, of which 8 were waited for; matrix products, arithmetic and copies ran while one was open for 0% of the time, Pallas kernels for 11%

profile of v7, /device:TPU:0, one launch (start us, length us, event | category | flops | bytes accessed | tf_op | source)
XLA Modules:
  0.0 58.0 jit_solution(7661833653654660452)
XLA Ops:
  1.3 0.0 copy-start.1
  1.3 0.0 copy-start.2
  1.3 3.2 %shard_map.122 = (f32[2,36,64,128]{3,2,1,0:T(8,128)S(1)}, f32[2,36,64,128]{3,2,1,0:T(8,128)S(1)}, f32[2,64,128]{2,1,0:T(8,128)S(1)}, f32[2,64,128]{2,1,0:T(8,128...) custom-call(s32[1,1]{1,0:T(1,128)S(6)} %copy.13.rot_ref, f32[4,36,64,128]{3,2,1,0:T(8,128)} %adj_ref.1), custom_call_target="tpu_custom_call" | custom-call | flops 8388608 | bytes 8388608 | tf_op jit(solution)/shard_map/pallas_call | solution.py:520
  4.5 4.0 %collective-permute-start.2 = (f32[36,8,128]{2,1,0:T(8,128)S(1)}, f32[36,8,128]{2,1,0:T(8,128)S(1)}, u32[]{:S(2)}, u32[]{:S(2)}) collective-permute-start(f32[36,8,128]{2,1,0:T(8,128)S(1)} %get-tuple-element.37), channel_id=1, source_target_pairs={{0,24},{8,16},{16,8},{24,0},{1,25},{9,17},{17,9},{25,1},{2,26},{10... | collective-permute-start | bytes 442376 | tf_op jit(solution)/shard_map/ppermute | solution.py:478
  8.5 0.5 collective-permute-start.3
  9.0 2.5 %collective-permute-start = (f32[2,64,128]{2,1,0:T(8,128)S(1)}, f32[2,64,128]{2,1,0:T(8,128)S(1)}, u32[]{:S(2)}, u32[]{:S(2)}) collective-permute-start(f32[2,64,128]{2,1,0:T(8,128)S(1)} %get-tuple-element.35), channel_id=1, source_target_pairs={{0,7},{1,2},{2,1},{3,4},{4,3},{5,6},{6,5},{7,0},{8,15},{9,10},{10,... | collective-permute-start | bytes 196616 | tf_op jit(solution)/shard_map/ppermute | solution.py:478
  11.5 1.2 %shard_map.123 = (f32[36,64,128]{2,1,0:T(8,128)S(1)}, f32[36,64,128]{2,1,0:T(8,128)S(1)}, f32[36,64,128]{2,1,0:T(8,128)S(1)}, f32[36,64,128]{2,1,0:T(8,128)S(1)}...) custom-call(f32[36,64,128]{2,1,0:T(8,128)S(1)} %copy-done.3, s32[64,128]{1,0:T(8,128)S(1)} %copy-done.6), custom_call_target="tpu_custom_call" | custom-call | flops 4194304 | bytes 4194304 | tf_op jit(solution)/shard_map/pallas_call | solution.py:529
  12.7 2.2 %collective-permute-done.refs_9_ = f32[2,64,128]{2,1,0:T(8,128)S(1)} collective-permute-done((f32[2,64,128]{2,1,0:T(8,128)S(1)}, f32[2,64,128]{2,1,0:T(8,128)S(1)}, u32[]{:S(2)}, u32[]{:S(2)}) %collective-permute-start) | collective-permute-done | bytes 65568 | tf_op jit(solution)/shard_map/ppermute | solution.py:478
  14.9 0.8 %collective-permute-done.3.refs_12_ = f32[36,8,128]{2,1,0:T(8,128)S(1)} collective-permute-done((f32[36,8,128]{2,1,0:T(8,128)S(1)}, f32[36,8,128]{2,1,0:T(8,128)S(1)}, u32[]{:S(2)}, u32[]{:S(2)}) %collective-permute-start.3) | collective-permute-done | bytes 147488 | tf_op jit(solution)/shard_map/ppermute | solution.py:472
  15.7 7.3 %shard_map.124 = (f32[2,36,64,128]{3,2,1,0:T(8,128)S(1)}, f32[2,36,64,128]{3,2,1,0:T(8,128)S(1)}, f32[2,64,128]{2,1,0:T(8,128)S(1)}, f32[2,64,128]{2,1,0:T(8,128...) custom-call(f32[2,36,64,128]{3,2,1,0:T(8,128)S(1)} %get-tuple-element.29.refs_0_, ...), custom_call_target="tpu_custom_call" | custom-call | tf_op jit(solution)/shard_map/pallas_call | solution.py:531
  23.0 1.5 %collective-permute-start.6 = (f32[36,8,128]{2,1,0:T(8,128)S(1)}, f32[36,8,128]{2,1,0:T(8,128)S(1)}, u32[]{:S(2)}, u32[]{:S(2)}) collective-permute-start(f32[36,8,128]{2,1,0:T(8,128)S(1)} %get-tuple-element.46), channel_id=1, source_target_pairs={{0,24},{8,16},{16,8},{24,0},{1,25},{9,17},{17,9},{25,1},{2,26},{10... | collective-permute-start | bytes 442376 | tf_op jit(solution)/shard_map/ppermute | solution.py:478
  24.5 0.3 collective-permute-start.7
  24.9 1.8 %collective-permute-start.4 = (f32[2,64,128]{2,1,0:T(8,128)S(1)}, f32[2,64,128]{2,1,0:T(8,128)S(1)}, u32[]{:S(2)}, u32[]{:S(2)}) collective-permute-start(f32[2,64,128]{2,1,0:T(8,128)S(1)} %get-tuple-element.43), channel_id=1, source_target_pairs={{0,7},{1,2},{2,1},{3,4},{4,3},{5,6},{6,5},{7,0},{8,15},{9,10},{10,... | collective-permute-start | bytes 196616 | tf_op jit(solution)/shard_map/ppermute | solution.py:478
  26.7 0.1 collective-permute-start.5
  26.7 3.8 %collective-permute-done.4.refs_9_ = f32[2,64,128]{2,1,0:T(8,128)S(1)} collective-permute-done((f32[2,64,128]{2,1,0:T(8,128)S(1)}, f32[2,64,128]{2,1,0:T(8,128)S(1)}, u32[]{:S(2)}, u32[]{:S(2)}) %collective-permute-start.4) | collective-permute-done | bytes 65568 | tf_op jit(solution)/shard_map/ppermute | solution.py:478
  30.6 3.0 %shard_map.125 = (f32[4,36,32,128]{3,2,1,0:T(8,128)S(1)}, f32[2,32,128]{2,1,0:T(8,128)S(1)}) custom-call(f32[2,36,64,128]{3,2,1,0:T(8,128)S(1)} %get-tuple-element.41.refs_0_, f32[2,36,64,128]{3,2,1,0:T(8,128)S(1)} %get-tuple-element.42.refs_1_, f32[2,36,64,128]{3,2,1,0:T(8,128)S(1)} %copy-done, f32[36,64,128]{2,1,0:T(8,128)S(1)} %get-tuple-element.31.refs_3_, ...), custom_call_target="tpu_custom_call" | custom-call | flops 16777216 | bytes 16777216 | tf_op jit(solution)/shard_map/pallas_call | solution.py:540
  33.6 3.0 %shard_map.126 = (f32[4,36,32,128]{3,2,1,0:T(8,128)S(1)}, f32[4,64,128]{2,1,0:T(8,128)S(1)}) custom-call(f32[2,36,64,128]{3,2,1,0:T(8,128)S(1)} %get-tuple-element.41.refs_0_, f32[2,36,64,128]{3,2,1,0:T(8,128)S(1)} %get-tuple-element.42.refs_1_, f32[2,36,64,128]{3,2,1,0:T(8,128)S(1)} %copy-done, f32[36,64,128]{2,1,0:T(8,128)S(1)} %get-tuple-element.31.refs_3_, ...), custom_call_target="tpu_custom_call" | custom-call | tf_op jit(solution)/shard_map/pallas_call | solution.py:547
  36.6 2.9 %collective-permute-start.10 = (f32[4,64,128]{2,1,0:T(8,128)S(1)}, f32[4,64,128]{2,1,0:T(8,128)S(1)}, u32[]{:S(2)}, u32[]{:S(2)}) collective-permute-start(f32[4,64,128]{2,1,0:T(8,128)S(1)} %get-tuple-element.53.refs_0_), channel_id=1, source_target_pairs={{0,24},{8,16},{16,8},{24,0},{1,25},{9,17},{17,9},{25,1},{2,26},{10... | collective-permute-start | bytes 393224 | tf_op jit(solution)/shard_map/ppermute | solution.py:472
  39.5 0.5 collective-permute-start.8
  40.0 0.1 collective-permute-start.9
  40.8 0.0 copy-start.5
  40.8 2.3 %shard_map.127 = (f32[4,36,64,128]{3,2,1,0:T(8,128)}, f32[8,128]{1,0:T(8,128)S(1)}) custom-call(s32[1,1]{1,0:T(1,128)S(6)} %copy.13.rot_ref, f32[4,36,32,128]{3,2,1,0:T(8,128)S(1)} %get-tuple-element.45.inner_ref, f32[4,36,32,128]{3,2,1,0:T(8,128)S(1)} %get-tuple-element.50.outer_ref, f32[36,64,128]{2,1,0:T(8,128)S(1)} %get-tuple-element.39.refs_13_.g1_ref, ...), custom_call_target="tpu_custom_call" | custom-call | flops 8388608 | bytes 8388608 | tf_op jit(solution)/shard_map/pallas_call | solution.py:554
  43.2 1.3 %collective-permute-done.8.refs_1_ = f32[4,64,128]{2,1,0:T(8,128)S(1)} collective-permute-done((f32[4,64,128]{2,1,0:T(8,128)S(1)}, f32[4,64,128]{2,1,0:T(8,128)S(1)}, u32[]{:S(2)}, u32[]{:S(2)}) %collective-permute-start.8) | collective-permute-done | bytes 131104 | tf_op jit(solution)/shard_map/ppermute | solution.py:472
  44.5 0.5 collective-permute-done.9.refs_2_
  45.0 1.7 %shard_map.128 = (f32[256,128]{1,0:T(8,128)S(1)}, f32[256,128]{1,0:T(8,128)S(1)}) custom-call(s32[32]{0:T(128)S(1)} %copy-done.7, s32[1,1]{1,0:T(1,128)S(6)} %copy.14.face_ref, f32[128,256]{1,0:T(8,128)S(1)} %copy-done.5, f32[1024,128]{1,0:T(8,128)S(1)} %copy-done.4, f32[8,128]{1,0:T(8,128)S(1)} %get-tuple-element.52._, ...), custom_call_target="tpu_custom_call" | custom-call | tf_op jit(solution)/shard_map/pallas_call | solution.py:564
  46.7 0.1 collective-permute-start.11
  46.8 1.3 %collective-permute-done.11 = f32[256,128]{1,0:T(8,128)S(1)} collective-permute-done((f32[256,128]{1,0:T(8,128)S(1)}, f32[256,128]{1,0:T(8,128)S(1)}, u32[]{:S(2)}, u32[]{:S(2)}) %collective-permute-start.11) | collective-permute-done | bytes 131104 | tf_op jit(solution)/shard_map/ppermute | solution.py:472
  48.1 1.5 %collective-permute-start.12 = (f32[128,128]{1,0:T(8,128)S(1)}, f32[128,128]{1,0:T(8,128)S(1)}, u32[]{:S(2)}, u32[]{:S(2)}) collective-permute-start(f32[128,128]{1,0:T(8,128)S(1)} %slice.17), channel_id=1, source_target_pairs={{0,2},{1,3},{2,0},{3,1},{4,6},{5,7},{6,4},{7,5},{8,10},{9,11},{10,... | collective-permute-start | bytes 196616 | tf_op jit(solution)/shard_map/ppermute | solution.py:472
  49.6 2.8 %collective-permute-done.12 = f32[128,128]{1,0:T(8,128)S(1)} collective-permute-done((f32[128,128]{1,0:T(8,128)S(1)}, f32[128,128]{1,0:T(8,128)S(1)}, u32[]{:S(2)}, u32[]{:S(2)}) %collective-permute-start.12) | collective-permute-done | bytes 65568 | tf_op jit(solution)/shard_map/ppermute | solution.py:472
  52.5 2.2 %collective-permute-start.13 = (f32[64,128]{1,0:T(8,128)S(1)}, f32[64,128]{1,0:T(8,128)S(1)}, u32[]{:S(2)}, u32[]{:S(2)}) collective-permute-start(f32[64,128]{1,0:T(8,128)S(1)} %slice.19), channel_id=1, source_target_pairs={{0,4},{1,5},{2,6},{3,7},{4,0},{5,1},{6,2},{7,3},{8,12},{9,13},{10,... | collective-permute-start | bytes 98312 | tf_op jit(solution)/shard_map/ppermute | solution.py:472
  54.7 2.6 %collective-permute-done.13 = f32[64,128]{1,0:T(8,128)S(1)} collective-permute-done((f32[64,128]{1,0:T(8,128)S(1)}, f32[64,128]{1,0:T(8,128)S(1)}, u32[]{:S(2)}, u32[]{:S(2)}) %collective-permute-start.13) | collective-permute-done | bytes 32800 | tf_op jit(solution)/shard_map/ppermute | solution.py:472
  57.4 0.6 %slice_add_fusion.1 = f32[64,128]{1,0:T(8,128)} fusion(f32[64,128]{1,0:T(8,128)S(1)} %collective-permute-done.13, f32[128,128]{1,0:T(8,128)S(1)} %slice_add_fusion), kind=kLoop, calls=%fused_computation.1 | loop fusion | flops 8192 | bytes 98304 | tf_op jit(solution)/shard_map/add | solution.py:573
  (24 shorter events, 0.1 us)
Async XLA Ops:
  1.3 10.2 %copy-start.3 = (f32[36,64,128]{2,1,0:T(8,128)S(1)}, f32[36,64,128]{2,1,0:T(8,128)}, u32[]{:S(2)}) copy-start(f32[36,64,128]{2,1,0:T(8,128)} %vd_ref.1) | copy-start | bytes 3538948
  1.3 10.2 %copy-start.6 = (s32[64,128]{1,0:T(8,128)S(1)}, s32[64,128]{1,0:T(8,128)}, u32[]{:S(2)}) copy-start(s32[64,128]{1,0:T(8,128)} %wet_ref.1) | copy-start | bytes 98308
  1.3 14.4 %copy-start = (f32[2,36,64,128]{3,2,1,0:T(8,128)S(1)}, f32[2,36,64,128]{3,2,1,0:T(8,128)}, u32[]{:S(2)}) copy-start(f32[2,36,64,128]{3,2,1,0:T(8,128)} %refs_2_.5) | copy-start | bytes 7077892
  1.3 14.4 %copy-start.1 = (bf16[256,256]{1,0:T(8,128)(2,1)S(1)}, bf16[256,256]{1,0:T(8,128)(2,1)}, u32[]{:S(2)}) copy-start(bf16[256,256]{1,0:T(8,128)(2,1)} %constant.11.clone.refs_8_) | copy-start | bytes 393220
  1.3 14.4 %copy-start.2 = (f32[256,128]{1,0:T(8,128)S(1)}, f32[256,128]{1,0:T(8,128)}, u32[]{:S(2)}) copy-start(f32[256,128]{1,0:T(8,128)} %constant.8.clone.refs_7_) | copy-start | bytes 393220
  4.5 10.4 %collective-permute-start.2 = (f32[36,8,128]{2,1,0:T(8,128)S(1)}, f32[36,8,128]{2,1,0:T(8,128)S(1)}, u32[]{:S(2)}, u32[]{:S(2)}) collective-permute-start(f32[36,8,128]{2,1,0:T(8,128)S(1)} %get-tuple-element.37), channel_id=1, source_target_pairs={{0,24},{8,16},{16,8},{24,0},{1,25},{9,17},{17,9},{25,1},{2,26},{10... | collective-permute-start | bytes 442376 | tf_op jit(solution)/shard_map/ppermute | solution.py:478
  8.5 7.3 %collective-permute-start.3 = (f32[36,8,128]{2,1,0:T(8,128)S(1)}, f32[36,8,128]{2,1,0:T(8,128)S(1)}, u32[]{:S(2)}, u32[]{:S(2)}) collective-permute-start(f32[36,8,128]{2,1,0:T(8,128)S(1)} %get-tuple-element.38), channel_id=1, source_target_pairs={{0,8},{8,0},{16,24},{24,16},{1,9},{9,1},{17,25},{25,17},{2,10},{10... | collective-permute-start | bytes 442376 | tf_op jit(solution)/shard_map/ppermute | solution.py:472
  9.0 5.9 %collective-permute-start = (f32[2,64,128]{2,1,0:T(8,128)S(1)}, f32[2,64,128]{2,1,0:T(8,128)S(1)}, u32[]{:S(2)}, u32[]{:S(2)}) collective-permute-start(f32[2,64,128]{2,1,0:T(8,128)S(1)} %get-tuple-element.35), channel_id=1, source_target_pairs={{0,7},{1,2},{2,1},{3,4},{4,3},{5,6},{6,5},{7,0},{8,15},{9,10},{10,... | collective-permute-start | bytes 196616 | tf_op jit(solution)/shard_map/ppermute | solution.py:478
  11.5 3.4 %collective-permute-start.1 = (f32[2,64,128]{2,1,0:T(8,128)S(1)}, f32[2,64,128]{2,1,0:T(8,128)S(1)}, u32[]{:S(2)}, u32[]{:S(2)}) collective-permute-start(f32[2,64,128]{2,1,0:T(8,128)S(1)} %get-tuple-element.36), channel_id=1, source_target_pairs={{0,1},{1,0},{2,3},{3,2},{4,5},{5,4},{6,7},{7,6},{8,9},{9,8},{10,11... | collective-permute-start | bytes 196616 | tf_op jit(solution)/shard_map/ppermute | solution.py:472
  23.0 10.5 %collective-permute-start.6 = (f32[36,8,128]{2,1,0:T(8,128)S(1)}, f32[36,8,128]{2,1,0:T(8,128)S(1)}, u32[]{:S(2)}, u32[]{:S(2)}) collective-permute-start(f32[36,8,128]{2,1,0:T(8,128)S(1)} %get-tuple-element.46), channel_id=1, source_target_pairs={{0,24},{8,16},{16,8},{24,0},{1,25},{9,17},{17,9},{25,1},{2,26},{10... | collective-permute-start | bytes 442376 | tf_op jit(solution)/shard_map/ppermute | solution.py:478
  24.5 9.0 %collective-permute-start.7 = (f32[36,8,128]{2,1,0:T(8,128)S(1)}, f32[36,8,128]{2,1,0:T(8,128)S(1)}, u32[]{:S(2)}, u32[]{:S(2)}) collective-permute-start(f32[36,8,128]{2,1,0:T(8,128)S(1)} %get-tuple-element.47), channel_id=1, source_target_pairs={{0,8},{8,0},{16,24},{24,16},{1,9},{9,1},{17,25},{25,17},{2,10},{10... | collective-permute-start | bytes 442376 | tf_op jit(solution)/shard_map/ppermute | solution.py:472
  24.9 5.7 %collective-permute-start.4 = (f32[2,64,128]{2,1,0:T(8,128)S(1)}, f32[2,64,128]{2,1,0:T(8,128)S(1)}, u32[]{:S(2)}, u32[]{:S(2)}) collective-permute-start(f32[2,64,128]{2,1,0:T(8,128)S(1)} %get-tuple-element.43), channel_id=1, source_target_pairs={{0,7},{1,2},{2,1},{3,4},{4,3},{5,6},{6,5},{7,0},{8,15},{9,10},{10,... | collective-permute-start | bytes 196616 | tf_op jit(solution)/shard_map/ppermute | solution.py:478
  26.7 3.9 %collective-permute-start.5 = (f32[2,64,128]{2,1,0:T(8,128)S(1)}, f32[2,64,128]{2,1,0:T(8,128)S(1)}, u32[]{:S(2)}, u32[]{:S(2)}) collective-permute-start(f32[2,64,128]{2,1,0:T(8,128)S(1)} %get-tuple-element.44), channel_id=1, source_target_pairs={{0,1},{1,0},{2,3},{3,2},{4,5},{5,4},{6,7},{7,6},{8,9},{9,8},{10,11... | collective-permute-start | bytes 196616 | tf_op jit(solution)/shard_map/ppermute | solution.py:472
  36.6 6.6 %collective-permute-start.10 = (f32[4,64,128]{2,1,0:T(8,128)S(1)}, f32[4,64,128]{2,1,0:T(8,128)S(1)}, u32[]{:S(2)}, u32[]{:S(2)}) collective-permute-start(f32[4,64,128]{2,1,0:T(8,128)S(1)} %get-tuple-element.53.refs_0_), channel_id=1, source_target_pairs={{0,24},{8,16},{16,8},{24,0},{1,25},{9,17},{17,9},{25,1},{2,26},{10... | collective-permute-start | bytes 393224 | tf_op jit(solution)/shard_map/ppermute | solution.py:472
  39.5 5.0 %collective-permute-start.8 = (f32[4,64,128]{2,1,0:T(8,128)S(1)}, f32[4,64,128]{2,1,0:T(8,128)S(1)}, u32[]{:S(2)}, u32[]{:S(2)}) collective-permute-start(f32[4,64,128]{2,1,0:T(8,128)S(1)} %get-tuple-element.53.refs_0_), channel_id=1, source_target_pairs={{0,8},{8,0},{16,24},{24,16},{1,9},{9,1},{17,25},{25,17},{2,10},{10... | collective-permute-start | bytes 393224 | tf_op jit(solution)/shard_map/ppermute | solution.py:472
  40.0 5.0 %collective-permute-start.9 = (f32[4,64,128]{2,1,0:T(8,128)S(1)}, f32[4,64,128]{2,1,0:T(8,128)S(1)}, u32[]{:S(2)}, u32[]{:S(2)}) collective-permute-start(f32[4,64,128]{2,1,0:T(8,128)S(1)} %get-tuple-element.53.refs_0_), channel_id=1, source_target_pairs={{0,16},{8,24},{16,0},{24,8},{1,17},{9,25},{17,1},{25,9},{2,18},{10... | collective-permute-start | bytes 393224 | tf_op jit(solution)/shard_map/ppermute | solution.py:472
  40.8 4.2 %copy-start.4 = (f32[1024,128]{1,0:T(8,128)S(1)}, f32[1024,128]{1,0:T(8,128)}, u32[]{:S(2)}) copy-start(f32[1024,128]{1,0:T(8,128)} %constant.10.clone.col_table_ref) | copy-start | bytes 1572868
  40.8 4.2 %copy-start.5 = (f32[128,256]{1,0:T(8,128)S(1)}, f32[128,256]{1,0:T(8,128)}, u32[]{:S(2)}) copy-start(f32[128,256]{1,0:T(8,128)} %constant.9.clone.row_table_ref) | copy-start | bytes 393220
  40.8 4.2 %copy-start.7 = (s32[32]{0:T(128)S(1)}, s32[32]{0:T(128)}, u32[]{:S(2)}) copy-start(s32[32]{0:T(128)} %owner_ref.1) | copy-start | bytes 388
  46.7 1.4 %collective-permute-start.11 = (f32[256,128]{1,0:T(8,128)S(1)}, f32[256,128]{1,0:T(8,128)S(1)}, u32[]{:S(2)}, u32[]{:S(2)}) collective-permute-start(f32[256,128]{1,0:T(8,128)S(1)} %get-tuple-element.55), channel_id=1, source_target_pairs={{0,1},{1,0},{2,3},{3,2},{4,5},{5,4},{6,7},{7,6},{8,9},{9,8},{10,11... | collective-permute-start | bytes 393224 | tf_op jit(solution)/shard_map/ppermute | solution.py:472
  48.1 4.3 %collective-permute-start.12 = (f32[128,128]{1,0:T(8,128)S(1)}, f32[128,128]{1,0:T(8,128)S(1)}, u32[]{:S(2)}, u32[]{:S(2)}) collective-permute-start(f32[128,128]{1,0:T(8,128)S(1)} %slice.17), channel_id=1, source_target_pairs={{0,2},{1,3},{2,0},{3,1},{4,6},{5,7},{6,4},{7,5},{8,10},{9,11},{10,... | collective-permute-start | bytes 196616 | tf_op jit(solution)/shard_map/ppermute | solution.py:472
  52.5 4.9 %collective-permute-start.13 = (f32[64,128]{1,0:T(8,128)S(1)}, f32[64,128]{1,0:T(8,128)S(1)}, u32[]{:S(2)}, u32[]{:S(2)}) collective-permute-start(f32[64,128]{1,0:T(8,128)S(1)} %slice.19), channel_id=1, source_target_pairs={{0,4},{1,5},{2,6},{3,7},{4,0},{5,1},{6,2},{7,3},{8,12},{9,13},{10,... | collective-permute-start | bytes 98312 | tf_op jit(solution)/shard_map/ppermute | solution.py:472

commit v8 on v7

--- a/solution.py
+++ b/solution.py
@@ -30,8 +30,8 @@
 SMEM = pl.BlockSpec(memory_space=pltpu.SMEM)
 F32 = jnp.float32
 PREP_UNROLL = 6
-FACTOR_ROWS, FACTOR_UNROLL = 64, 2
-UNROLLS = {16: (12, 9), 32: (6, 6), 64: (6, 9)}
+FACTOR_ROWS, FACTOR_UNROLL = 64, 4
+UNROLLS = {16: (18, 9), 32: (12, 6), 64: (9, 18)}
 DOWN_UNROLL = 6
 EDGE = 16
 
@@ -97,18 +97,21 @@
 
 def store_edge_rows(k, fields, ends, south_ref, north_ref):
     size = fields[0].shape[0]
-    for c in range(4):
+    for c, (at, count) in enumerate(((0, 2), (2, 2), (4, 1), (5, 1))):
         if ends[0]:
-            south_ref[k, 2 * c : 2 * c + 2, :] = fields[c][0:2, :]
+            south_ref[k, at : at + count, :] = fields[c][0:count, :]
         if ends[1]:
-            north_ref[k, 2 * c : 2 * c + 2, :] = fields[c][size - 2 : size, :]
+            north_ref[k, at : at + count, :] = fields[c][size - count : size, :]
 
 
 def write_rows(row_a, row_b, south_ref, north_ref):
     even = lax.axis_index("ty") % 2 == 0
-    south, north = south_ref[...], north_ref[...]
-    row_a[...] = jnp.where(even, north, south)
-    row_b[...] = jnp.where(even, south, north)
+    row = rows_of(TILE)
+    for group in range(south_ref.shape[0] // 4):
+        for message, choose in ((row_a, (north_ref, south_ref)), (row_b, (south_ref, north_ref))):
+            tiles = [jnp.where(even, choose[0][4 * group + i], choose[1][4 * group + i]) for i in range(4)]
+            for i in range(3):
+                message[3 * group + i] = jnp.where(row < 6, tiles[i], pltpu.roll(tiles[3], 6 - 2 * i, 0))
 
 
 def write_columns(col_a, col_b, low, high, split):
@@ -117,24 +120,33 @@
     for g in range(2):
         east = jnp.where(first, low[g], up(high[g]))
         west = jnp.where(first, down(low[g]), high[g])
-        col_a[g] = jnp.where(even, east, west)
-        col_b[g] = jnp.where(even, west, east)
+        col_a[g, : low[0].shape[0]] = jnp.where(even, east, west)
+        col_b[g, : low[0].shape[0]] = jnp.where(even, west, east)
 
 
 def read_rows(row_a, row_b, south_ref, north_ref):
     here = lax.axis_index("ty")
     even = here % 2 == 0
-    first, second = row_a[...], row_b[...]
-    south_ref[...] = jnp.where(here == 0, 0.0, jnp.where(even, second, first))
-    north_ref[...] = jnp.where(here == lax.axis_size("ty") - 1, 0.0, jnp.where(even, first, second))
+    row = rows_of(TILE)
+    at_south, at_north = here == 0, here == lax.axis_size("ty") - 1
+    for group in range(south_ref.shape[0] // 4):
+        first, second = ([ref[3 * group + i] for i in range(3)] for ref in (row_a, row_b))
+        for ref, end, pair in ((south_ref, at_south, (second, first)), (north_ref, at_north, (first, second))):
+            tiles = [jnp.where(end, 0.0, jnp.where(even, x, y)) for x, y in zip(*pair)]
+            turned = [pltpu.roll(tile, 2 * i + 2, 0) for i, tile in enumerate(tiles)]
+            tiles.append(jnp.where(row < 2, turned[0], jnp.where(row < 4, turned[1], turned[2])))
+            for i in range(4):
+                ref[4 * group + i] = tiles[i]
 
 
 def read_columns(col_a, col_b, halo_ref, split):
     even = lax.axis_index("tx") % 2 == 0
-    first, up, down = lane_moves(col_a.shape[1], split)
+    height = halo_ref.shape[2]
+    first, up, down = lane_moves(height, split)
     for g in range(2):
-        from_east = jnp.where(even, col_a[g], col_b[g])
-        from_west = jnp.where(even, col_b[g], col_a[g])
+        from_a, from_b = col_a[g, :height], col_b[g, :height]
+        from_east = jnp.where(even, from_a, from_b)
+        from_west = jnp.where(even, from_b, from_a)
         halo_ref[g, 0] = jnp.where(first, from_west, up(from_east))
         halo_ref[g, 1] = jnp.where(first, down(from_west), from_east)
 
@@ -246,10 +258,10 @@
         south, north = halos
         part = rows_of(TILE)
         if start < 0:
-            halo = pltpu.roll(south, (-2 * c - 2 - start) % TILE, 0)
+            halo = pltpu.roll(south, (-2 * c - 2 - start if c < 2 else -2 - c) % TILE, 0)
             return jnp.where(part < -start, halo, pltpu.roll(get(c, k, 0), -start, 0))
         over = start + TILE - height
-        halo = pltpu.roll(north, (TILE - over - 2 * c) % TILE, 0)
+        halo = pltpu.roll(north, (-over - 2 * c if c < 2 else -3 - c) % TILE, 0)
         return jnp.where(part >= TILE - over, halo, pltpu.roll(get(c, k, height - TILE), TILE - over, 0))
 
     for block, (first_row, size) in enumerate(blocks):
@@ -500,7 +512,7 @@
     rows_total, cols_total = height * ty, width * tx
     full = shape(levels, height, width)
     pair = shape(2, levels, height, width)
-    row_pair, col_pair = [shape(levels, TILE, width)] * 2, [shape(2, height, LANES)] * 2
+    row_pair, col_pair = [shape(3 * levels // 4, TILE, width)] * 2, [shape(2, height, LANES)] * 2
     rows_scratch = [pltpu.VMEM((levels, TILE, width), F32)] * 2
     cols_scratch = [pltpu.VMEM((2, 2, height, LANES), F32)]
     surface = shape(2, height, width)
@@ -530,7 +542,7 @@
     coefficients = (background_flow, w1, w2, h1, h2, coriolis, jnp.asarray(band_matrix(), jnp.bfloat16))
     ts, uv, first, *sent = call(
         functools.partial(step_kernel, "whole", ((0, height),)),
-        [pair, pair, surface] + col_pair + row_pair,
+        [pair, pair, surface] + [shape(2, 7 * height // 4, LANES)] * 2 + row_pair,
         [VMEM] * 15,
         rows_scratch + [kept(height)] + cols_scratch + rows_scratch,
         limit=12,

time: 58.1 us -> 57.3 us (0.986)
  starting transfers between devices: 18.1 us -> 15.6 us
  waiting for transfers between devices: 15.5 us -> 16.8 us
    ppermute x10, starting transfers between devices: 8.35 us -> 5.58 us  [swap(): lax.ppermute(block, axis, [(i, i ^ bit) for i in range(lax.axis_size(axis...]
    ppermute x10, waiting for transfers between devices: 9.42 us -> 11.9 us  [swap(): lax.ppermute(block, axis, [(i, i ^ bit) for i in range(lax.axis_size(axis...]
    ppermute x4, waiting for transfers between devices: 6.04 us -> 4.91 us  [exchange(): return (lax.ppermute(second, axis, others), swap(first, axis, 1))]
  transfers between devices with their start and end apart: 14 -> 14, of which waited for: 8 -> 8; matrix products, arithmetic and copies ran while one was open for 0% -> 0% of each run, Pallas kernels for 11% -> 12%
where the time goes in v8:
time: 57.3 us; the launch traced here: 57.1 us
  Pallas kernels  21.9 us (38%)
  waiting for transfers between devices  16.8 us (29%)
  starting transfers between devices  15.6 us (27%)
  between operations  2.15 us (4%)
  other arithmetic  0.64 us (1%)
    ppermute x10, waiting for transfers between devices, swap(): lax.ppermute(block, axis, [(i, i ^ bit) for i in range(lax.axis_size(axis...  11.9 us
    ppermute x4, starting transfers between devices, exchange(): return (lax.ppermute(second, axis, others), swap(first, axis, 1))  9.98 us
    pallas_call x1, Pallas kernels, body(): call(functools.partial(step_kernel, 'whole', ((0, height),)), [pair, pair...  7.18 us
    ppermute x10, starting transfers between devices, swap(): lax.ppermute(block, axis, [(i, i ^ bit) for i in range(lax.axis_size(axis...  5.58 us
    ppermute x4, waiting for transfers between devices, exchange(): return (lax.ppermute(second, axis, others), swap(first, axis, 1))  4.91 us
    pallas_call x1, Pallas kernels, body(): call(functools.partial(step_kernel, 'inner', ((EDGE, middle),)), [shape(4...  3.21 us
    pallas_call x1, Pallas kernels, body(): call(prep_kernel, [pair, pair] + col_pair + row_pair, [SMEM, ANY], [pltpu...  3.14 us
    pallas_call x1, Pallas kernels, body(): call(functools.partial(step_kernel, 'outer', ((0, EDGE), (height - EDGE,...  3.1 us
  transfers between devices with their start and end apart: 14, of which 8 were waited for; matrix products, arithmetic and copies ran while one was open for 0% of the time, Pallas kernels for 12%

profile of v8, /device:TPU:0, one launch (start us, length us, event | category | flops | bytes accessed | tf_op | source)
XLA Modules:
  0.0 57.1 jit_solution(13569912658173493789)
XLA Ops:
  1.3 0.0 copy-start.1
  1.3 0.0 copy-start.2
  1.3 3.1 %shard_map.122 = (f32[2,36,64,128]{3,2,1,0:T(8,128)S(1)}, f32[2,36,64,128]{3,2,1,0:T(8,128)S(1)}, f32[2,64,128]{2,1,0:T(8,128)S(1)}, f32[2,64,128]{2,1,0:T(8,128...) custom-call(s32[1,1]{1,0:T(1,128)S(6)} %copy.13.rot_ref, f32[4,36,64,128]{3,2,1,0:T(8,128)} %adj_ref.1), custom_call_target="tpu_custom_call" | custom-call | flops 8388608 | bytes 8388608 | tf_op jit(solution)/shard_map/pallas_call | solution.py:532
  4.5 4.0 %collective-permute-start.2 = (f32[27,8,128]{2,1,0:T(8,128)S(1)}, f32[27,8,128]{2,1,0:T(8,128)S(1)}, u32[]{:S(2)}, u32[]{:S(2)}) collective-permute-start(f32[27,8,128]{2,1,0:T(8,128)S(1)} %get-tuple-element.37), channel_id=1, source_target_pairs={{0,24},{8,16},{16,8},{24,0},{1,25},{9,17},{17,9},{25,1},{2,26},{10... | collective-permute-start | bytes 331784 | tf_op jit(solution)/shard_map/ppermute | solution.py:490
  8.4 0.5 collective-permute-start.3
  9.0 2.5 %collective-permute-start = (f32[2,64,128]{2,1,0:T(8,128)S(1)}, f32[2,64,128]{2,1,0:T(8,128)S(1)}, u32[]{:S(2)}, u32[]{:S(2)}) collective-permute-start(f32[2,64,128]{2,1,0:T(8,128)S(1)} %get-tuple-element.35), channel_id=1, source_target_pairs={{0,7},{1,2},{2,1},{3,4},{4,3},{5,6},{6,5},{7,0},{8,15},{9,10},{10,... | collective-permute-start | bytes 196616 | tf_op jit(solution)/shard_map/ppermute | solution.py:490
  11.5 1.3 %shard_map.123 = (f32[36,64,128]{2,1,0:T(8,128)S(1)}, f32[36,64,128]{2,1,0:T(8,128)S(1)}, f32[36,64,128]{2,1,0:T(8,128)S(1)}, f32[36,64,128]{2,1,0:T(8,128)S(1)}...) custom-call(f32[36,64,128]{2,1,0:T(8,128)S(1)} %copy-done.3, s32[64,128]{1,0:T(8,128)S(1)} %copy-done.6), custom_call_target="tpu_custom_call" | custom-call | flops 4194304 | bytes 4194304 | tf_op jit(solution)/shard_map/pallas_call | solution.py:541
  12.8 2.1 %collective-permute-done.refs_9_ = f32[2,64,128]{2,1,0:T(8,128)S(1)} collective-permute-done((f32[2,64,128]{2,1,0:T(8,128)S(1)}, f32[2,64,128]{2,1,0:T(8,128)S(1)}, u32[]{:S(2)}, u32[]{:S(2)}) %collective-permute-start) | collective-permute-done | bytes 65568 | tf_op jit(solution)/shard_map/ppermute | solution.py:490
  14.9 7.2 %shard_map.124 = (f32[2,36,64,128]{3,2,1,0:T(8,128)S(1)}, f32[2,36,64,128]{3,2,1,0:T(8,128)S(1)}, f32[2,64,128]{2,1,0:T(8,128)S(1)}, f32[2,112,128]{2,1,0:T(8,12...) custom-call(f32[2,36,64,128]{3,2,1,0:T(8,128)S(1)} %get-tuple-element.29.refs_0_, ...), custom_call_target="tpu_custom_call" | custom-call | tf_op jit(solution)/shard_map/pallas_call | solution.py:543
  22.1 2.1 %collective-permute-start.4 = (f32[2,112,128]{2,1,0:T(8,128)S(1)}, f32[2,112,128]{2,1,0:T(8,128)S(1)}, u32[]{:S(2)}, u32[]{:S(2)}) collective-permute-start(f32[2,112,128]{2,1,0:T(8,128)S(1)} %get-tuple-element.43), channel_id=1, source_target_pairs={{0,7},{1,2},{2,1},{3,4},{4,3},{5,6},{6,5},{7,0},{8,15},{9,10},{10,... | collective-permute-start | bytes 344072 | tf_op jit(solution)/shard_map/ppermute | solution.py:490
  24.2 1.4 %collective-permute-start.6 = (f32[27,8,128]{2,1,0:T(8,128)S(1)}, f32[27,8,128]{2,1,0:T(8,128)S(1)}, u32[]{:S(2)}, u32[]{:S(2)}) collective-permute-start(f32[27,8,128]{2,1,0:T(8,128)S(1)} %get-tuple-element.46), channel_id=1, source_target_pairs={{0,24},{8,16},{16,8},{24,0},{1,25},{9,17},{17,9},{25,1},{2,26},{10... | collective-permute-start | bytes 331784 | tf_op jit(solution)/shard_map/ppermute | solution.py:490
  25.7 0.5 collective-permute-start.7
  26.2 2.8 %collective-permute-done.4.refs_9_ = f32[2,112,128]{2,1,0:T(8,128)S(1)} collective-permute-done((f32[2,112,128]{2,1,0:T(8,128)S(1)}, f32[2,112,128]{2,1,0:T(8,128)S(1)}, u32[]{:S(2)}, u32[]{:S(2)}) %collective-permute-start.4) | collective-permute-done | bytes 114720 | tf_op jit(solution)/shard_map/ppermute | solution.py:490
  29.0 3.2 %shard_map.125 = (f32[4,36,32,128]{3,2,1,0:T(8,128)S(1)}, f32[2,32,128]{2,1,0:T(8,128)S(1)}) custom-call(f32[2,36,64,128]{3,2,1,0:T(8,128)S(1)} %get-tuple-element.41.refs_0_, f32[2,36,64,128]{3,2,1,0:T(8,128)S(1)} %get-tuple-element.42.refs_1_, f32[2,36,64,128]{3,2,1,0:T(8,128)S(1)} %copy-done, f32[36,64,128]{2,1,0:T(8,128)S(1)} %get-tuple-element.31.refs_3_, ...), custom_call_target="tpu_custom_call" | custom-call | flops 16777216 | bytes 16777216 | tf_op jit(solution)/shard_map/pallas_call | solution.py:552
  32.2 3.1 %shard_map.126 = (f32[4,36,32,128]{3,2,1,0:T(8,128)S(1)}, f32[4,64,128]{2,1,0:T(8,128)S(1)}) custom-call(f32[2,36,64,128]{3,2,1,0:T(8,128)S(1)} %get-tuple-element.41.refs_0_, f32[2,36,64,128]{3,2,1,0:T(8,128)S(1)} %get-tuple-element.42.refs_1_, f32[2,36,64,128]{3,2,1,0:T(8,128)S(1)} %copy-done, f32[36,64,128]{2,1,0:T(8,128)S(1)} %get-tuple-element.31.refs_3_, ...), custom_call_target="tpu_custom_call" | custom-call | tf_op jit(solution)/shard_map/pallas_call | solution.py:559
  35.3 2.3 %collective-permute-start.10 = (f32[4,64,128]{2,1,0:T(8,128)S(1)}, f32[4,64,128]{2,1,0:T(8,128)S(1)}, u32[]{:S(2)}, u32[]{:S(2)}) collective-permute-start(f32[4,64,128]{2,1,0:T(8,128)S(1)} %get-tuple-element.53.refs_0_), channel_id=1, source_target_pairs={{0,24},{8,16},{16,8},{24,0},{1,25},{9,17},{17,9},{25,1},{2,26},{10... | collective-permute-start | bytes 393224 | tf_op jit(solution)/shard_map/ppermute | solution.py:484
  37.6 0.5 collective-permute-start.8
  38.2 0.7 %collective-permute-start.9 = (f32[4,64,128]{2,1,0:T(8,128)S(1)}, f32[4,64,128]{2,1,0:T(8,128)S(1)}, u32[]{:S(2)}, u32[]{:S(2)}) collective-permute-start(f32[4,64,128]{2,1,0:T(8,128)S(1)} %get-tuple-element.53.refs_0_), channel_id=1, source_target_pairs={{0,16},{8,24},{16,0},{24,8},{1,17},{9,25},{17,1},{25,9},{2,18},{10... | collective-permute-start | bytes 393224 | tf_op jit(solution)/shard_map/ppermute | solution.py:484
  39.5 0.0 copy-start.4
  39.6 0.0 copy-start.5
  39.6 2.3 %shard_map.127 = (f32[4,36,64,128]{3,2,1,0:T(8,128)}, f32[8,128]{1,0:T(8,128)S(1)}) custom-call(s32[1,1]{1,0:T(1,128)S(6)} %copy.13.rot_ref, f32[4,36,32,128]{3,2,1,0:T(8,128)S(1)} %get-tuple-element.45.inner_ref, f32[4,36,32,128]{3,2,1,0:T(8,128)S(1)} %get-tuple-element.50.outer_ref, f32[36,64,128]{2,1,0:T(8,128)S(1)} %get-tuple-element.39.refs_13_.g1_ref, ...), custom_call_target="tpu_custom_call" | custom-call | flops 8388608 | bytes 8388608 | tf_op jit(solution)/shard_map/pallas_call | solution.py:566
  41.9 0.8 %collective-permute-done.10.refs_3_ = f32[4,64,128]{2,1,0:T(8,128)S(1)} collective-permute-done((f32[4,64,128]{2,1,0:T(8,128)S(1)}, f32[4,64,128]{2,1,0:T(8,128)S(1)}, u32[]{:S(2)}, u32[]{:S(2)}) %collective-permute-start.10) | collective-permute-done | bytes 131104 | tf_op jit(solution)/shard_map/ppermute | solution.py:484
  42.7 1.4 %collective-permute-done.8.refs_1_ = f32[4,64,128]{2,1,0:T(8,128)S(1)} collective-permute-done((f32[4,64,128]{2,1,0:T(8,128)S(1)}, f32[4,64,128]{2,1,0:T(8,128)S(1)}, u32[]{:S(2)}, u32[]{:S(2)}) %collective-permute-start.8) | collective-permute-done | bytes 131104 | tf_op jit(solution)/shard_map/ppermute | solution.py:484
  44.1 0.1 collective-permute-done.9.refs_2_
  44.2 1.7 %shard_map.128 = (f32[256,128]{1,0:T(8,128)S(1)}, f32[256,128]{1,0:T(8,128)S(1)}) custom-call(s32[32]{0:T(128)S(1)} %copy-done.7, s32[1,1]{1,0:T(1,128)S(6)} %copy.14.face_ref, f32[128,256]{1,0:T(8,128)S(1)} %copy-done.5, f32[1024,128]{1,0:T(8,128)S(1)} %copy-done.4, f32[8,128]{1,0:T(8,128)S(1)} %get-tuple-element.52._, ...), custom_call_target="tpu_custom_call" | custom-call | tf_op jit(solution)/shard_map/pallas_call | solution.py:576
  45.8 0.1 collective-permute-start.11
  45.9 1.3 %collective-permute-done.11 = f32[256,128]{1,0:T(8,128)S(1)} collective-permute-done((f32[256,128]{1,0:T(8,128)S(1)}, f32[256,128]{1,0:T(8,128)S(1)}, u32[]{:S(2)}, u32[]{:S(2)}) %collective-permute-start.11) | collective-permute-done | bytes 131104 | tf_op jit(solution)/shard_map/ppermute | solution.py:484
  47.3 0.1 collective-permute-start.12
  47.3 4.3 %collective-permute-done.12 = f32[128,128]{1,0:T(8,128)S(1)} collective-permute-done((f32[128,128]{1,0:T(8,128)S(1)}, f32[128,128]{1,0:T(8,128)S(1)}, u32[]{:S(2)}, u32[]{:S(2)}) %collective-permute-start.12) | collective-permute-done | bytes 65568 | tf_op jit(solution)/shard_map/ppermute | solution.py:484
  51.6 0.8 %collective-permute-start.13 = (f32[64,128]{1,0:T(8,128)S(1)}, f32[64,128]{1,0:T(8,128)S(1)}, u32[]{:S(2)}, u32[]{:S(2)}) collective-permute-start(f32[64,128]{1,0:T(8,128)S(1)} %slice.19), channel_id=1, source_target_pairs={{0,4},{1,5},{2,6},{3,7},{4,0},{5,1},{6,2},{7,3},{8,12},{9,13},{10,... | collective-permute-start | bytes 98312 | tf_op jit(solution)/shard_map/ppermute | solution.py:484
  52.4 4.1 %collective-permute-done.13 = f32[64,128]{1,0:T(8,128)S(1)} collective-permute-done((f32[64,128]{1,0:T(8,128)S(1)}, f32[64,128]{1,0:T(8,128)S(1)}, u32[]{:S(2)}, u32[]{:S(2)}) %collective-permute-start.13) | collective-permute-done | bytes 32800 | tf_op jit(solution)/shard_map/ppermute | solution.py:484
  56.5 0.6 %slice_add_fusion.1 = f32[64,128]{1,0:T(8,128)} fusion(f32[64,128]{1,0:T(8,128)S(1)} %collective-permute-done.13, f32[128,128]{1,0:T(8,128)S(1)} %slice_add_fusion), kind=kLoop, calls=%fused_computation.1 | loop fusion | flops 8192 | bytes 98304 | tf_op jit(solution)/shard_map/add | solution.py:585
  (24 shorter events, 0.1 us)
Async XLA Ops:
  1.3 10.2 %copy-start.3 = (f32[36,64,128]{2,1,0:T(8,128)S(1)}, f32[36,64,128]{2,1,0:T(8,128)}, u32[]{:S(2)}) copy-start(f32[36,64,128]{2,1,0:T(8,128)} %vd_ref.1) | copy-start | bytes 3538948
  1.3 10.2 %copy-start.6 = (s32[64,128]{1,0:T(8,128)S(1)}, s32[64,128]{1,0:T(8,128)}, u32[]{:S(2)}) copy-start(s32[64,128]{1,0:T(8,128)} %wet_ref.1) | copy-start | bytes 98308
  1.3 13.6 %copy-start = (f32[2,36,64,128]{3,2,1,0:T(8,128)S(1)}, f32[2,36,64,128]{3,2,1,0:T(8,128)}, u32[]{:S(2)}) copy-start(f32[2,36,64,128]{3,2,1,0:T(8,128)} %refs_2_.5) | copy-start | bytes 7077892
  1.3 13.6 %copy-start.1 = (bf16[256,256]{1,0:T(8,128)(2,1)S(1)}, bf16[256,256]{1,0:T(8,128)(2,1)}, u32[]{:S(2)}) copy-start(bf16[256,256]{1,0:T(8,128)(2,1)} %constant.11.clone.refs_8_) | copy-start | bytes 393220
  1.3 13.6 %copy-start.2 = (f32[256,128]{1,0:T(8,128)S(1)}, f32[256,128]{1,0:T(8,128)}, u32[]{:S(2)}) copy-start(f32[256,128]{1,0:T(8,128)} %constant.8.clone.refs_7_) | copy-start | bytes 393220
  4.5 10.4 %collective-permute-start.2 = (f32[27,8,128]{2,1,0:T(8,128)S(1)}, f32[27,8,128]{2,1,0:T(8,128)S(1)}, u32[]{:S(2)}, u32[]{:S(2)}) collective-permute-start(f32[27,8,128]{2,1,0:T(8,128)S(1)} %get-tuple-element.37), channel_id=1, source_target_pairs={{0,24},{8,16},{16,8},{24,0},{1,25},{9,17},{17,9},{25,1},{2,26},{10... | collective-permute-start | bytes 331784 | tf_op jit(solution)/shard_map/ppermute | solution.py:490
  8.4 6.5 %collective-permute-start.3 = (f32[27,8,128]{2,1,0:T(8,128)S(1)}, f32[27,8,128]{2,1,0:T(8,128)S(1)}, u32[]{:S(2)}, u32[]{:S(2)}) collective-permute-start(f32[27,8,128]{2,1,0:T(8,128)S(1)} %get-tuple-element.38), channel_id=1, source_target_pairs={{0,8},{8,0},{16,24},{24,16},{1,9},{9,1},{17,25},{25,17},{2,10},{10... | collective-permute-start | bytes 331784 | tf_op jit(solution)/shard_map/ppermute | solution.py:484
  9.0 5.9 %collective-permute-start = (f32[2,64,128]{2,1,0:T(8,128)S(1)}, f32[2,64,128]{2,1,0:T(8,128)S(1)}, u32[]{:S(2)}, u32[]{:S(2)}) collective-permute-start(f32[2,64,128]{2,1,0:T(8,128)S(1)} %get-tuple-element.35), channel_id=1, source_target_pairs={{0,7},{1,2},{2,1},{3,4},{4,3},{5,6},{6,5},{7,0},{8,15},{9,10},{10,... | collective-permute-start | bytes 196616 | tf_op jit(solution)/shard_map/ppermute | solution.py:490
  11.5 3.4 %collective-permute-start.1 = (f32[2,64,128]{2,1,0:T(8,128)S(1)}, f32[2,64,128]{2,1,0:T(8,128)S(1)}, u32[]{:S(2)}, u32[]{:S(2)}) collective-permute-start(f32[2,64,128]{2,1,0:T(8,128)S(1)} %get-tuple-element.36), channel_id=1, source_target_pairs={{0,1},{1,0},{2,3},{3,2},{4,5},{5,4},{6,7},{7,6},{8,9},{9,8},{10,11... | collective-permute-start | bytes 196616 | tf_op jit(solution)/shard_map/ppermute | solution.py:484
  22.1 6.8 %collective-permute-start.4 = (f32[2,112,128]{2,1,0:T(8,128)S(1)}, f32[2,112,128]{2,1,0:T(8,128)S(1)}, u32[]{:S(2)}, u32[]{:S(2)}) collective-permute-start(f32[2,112,128]{2,1,0:T(8,128)S(1)} %get-tuple-element.43), channel_id=1, source_target_pairs={{0,7},{1,2},{2,1},{3,4},{4,3},{5,6},{6,5},{7,0},{8,15},{9,10},{10,... | collective-permute-start | bytes 344072 | tf_op jit(solution)/shard_map/ppermute | solution.py:490
  24.2 4.7 %collective-permute-start.5 = (f32[2,112,128]{2,1,0:T(8,128)S(1)}, f32[2,112,128]{2,1,0:T(8,128)S(1)}, u32[]{:S(2)}, u32[]{:S(2)}) collective-permute-start(f32[2,112,128]{2,1,0:T(8,128)S(1)} %get-tuple-element.44), channel_id=1, source_target_pairs={{0,1},{1,0},{2,3},{3,2},{4,5},{5,4},{6,7},{7,6},{8,9},{9,8},{10,11... | collective-permute-start | bytes 344072 | tf_op jit(solution)/shard_map/ppermute | solution.py:484
  24.2 8.0 %collective-permute-start.6 = (f32[27,8,128]{2,1,0:T(8,128)S(1)}, f32[27,8,128]{2,1,0:T(8,128)S(1)}, u32[]{:S(2)}, u32[]{:S(2)}) collective-permute-start(f32[27,8,128]{2,1,0:T(8,128)S(1)} %get-tuple-element.46), channel_id=1, source_target_pairs={{0,24},{8,16},{16,8},{24,0},{1,25},{9,17},{17,9},{25,1},{2,26},{10... | collective-permute-start | bytes 331784 | tf_op jit(solution)/shard_map/ppermute | solution.py:490
  25.7 6.5 %collective-permute-start.7 = (f32[27,8,128]{2,1,0:T(8,128)S(1)}, f32[27,8,128]{2,1,0:T(8,128)S(1)}, u32[]{:S(2)}, u32[]{:S(2)}) collective-permute-start(f32[27,8,128]{2,1,0:T(8,128)S(1)} %get-tuple-element.47), channel_id=1, source_target_pairs={{0,8},{8,0},{16,24},{24,16},{1,9},{9,1},{17,25},{25,17},{2,10},{10... | collective-permute-start | bytes 331784 | tf_op jit(solution)/shard_map/ppermute | solution.py:484
  35.3 7.4 %collective-permute-start.10 = (f32[4,64,128]{2,1,0:T(8,128)S(1)}, f32[4,64,128]{2,1,0:T(8,128)S(1)}, u32[]{:S(2)}, u32[]{:S(2)}) collective-permute-start(f32[4,64,128]{2,1,0:T(8,128)S(1)} %get-tuple-element.53.refs_0_), channel_id=1, source_target_pairs={{0,24},{8,16},{16,8},{24,0},{1,25},{9,17},{17,9},{25,1},{2,26},{10... | collective-permute-start | bytes 393224 | tf_op jit(solution)/shard_map/ppermute | solution.py:484
  37.6 6.4 %collective-permute-start.8 = (f32[4,64,128]{2,1,0:T(8,128)S(1)}, f32[4,64,128]{2,1,0:T(8,128)S(1)}, u32[]{:S(2)}, u32[]{:S(2)}) collective-permute-start(f32[4,64,128]{2,1,0:T(8,128)S(1)} %get-tuple-element.53.refs_0_), channel_id=1, source_target_pairs={{0,8},{8,0},{16,24},{24,16},{1,9},{9,1},{17,25},{25,17},{2,10},{10... | collective-permute-start | bytes 393224 | tf_op jit(solution)/shard_map/ppermute | solution.py:484
  38.2 6.0 %collective-permute-start.9 = (f32[4,64,128]{2,1,0:T(8,128)S(1)}, f32[4,64,128]{2,1,0:T(8,128)S(1)}, u32[]{:S(2)}, u32[]{:S(2)}) collective-permute-start(f32[4,64,128]{2,1,0:T(8,128)S(1)} %get-tuple-element.53.refs_0_), channel_id=1, source_target_pairs={{0,16},{8,24},{16,0},{24,8},{1,17},{9,25},{17,1},{25,9},{2,18},{10... | collective-permute-start | bytes 393224 | tf_op jit(solution)/shard_map/ppermute | solution.py:484
  39.5 4.6 %copy-start.4 = (f32[1024,128]{1,0:T(8,128)S(1)}, f32[1024,128]{1,0:T(8,128)}, u32[]{:S(2)}) copy-start(f32[1024,128]{1,0:T(8,128)} %constant.10.clone.col_table_ref) | copy-start | bytes 1572868
  39.6 4.6 %copy-start.5 = (f32[128,256]{1,0:T(8,128)S(1)}, f32[128,256]{1,0:T(8,128)}, u32[]{:S(2)}) copy-start(f32[128,256]{1,0:T(8,128)} %constant.9.clone.row_table_ref) | copy-start | bytes 393220
  39.6 4.6 %copy-start.7 = (s32[32]{0:T(128)S(1)}, s32[32]{0:T(128)}, u32[]{:S(2)}) copy-start(s32[32]{0:T(128)} %owner_ref.1) | copy-start | bytes 388
  45.8 1.4 %collective-permute-start.11 = (f32[256,128]{1,0:T(8,128)S(1)}, f32[256,128]{1,0:T(8,128)S(1)}, u32[]{:S(2)}, u32[]{:S(2)}) collective-permute-start(f32[256,128]{1,0:T(8,128)S(1)} %get-tuple-element.55), channel_id=1, source_target_pairs={{0,1},{1,0},{2,3},{3,2},{4,5},{5,4},{6,7},{7,6},{8,9},{9,8},{10,11... | collective-permute-start | bytes 393224 | tf_op jit(solution)/shard_map/ppermute | solution.py:484
  47.3 4.3 %collective-permute-start.12 = (f32[128,128]{1,0:T(8,128)S(1)}, f32[128,128]{1,0:T(8,128)S(1)}, u32[]{:S(2)}, u32[]{:S(2)}) collective-permute-start(f32[128,128]{1,0:T(8,128)S(1)} %slice.17), channel_id=1, source_target_pairs={{0,2},{1,3},{2,0},{3,1},{4,6},{5,7},{6,4},{7,5},{8,10},{9,11},{10,... | collective-permute-start | bytes 196616 | tf_op jit(solution)/shard_map/ppermute | solution.py:484
  51.6 4.9 %collective-permute-start.13 = (f32[64,128]{1,0:T(8,128)S(1)}, f32[64,128]{1,0:T(8,128)S(1)}, u32[]{:S(2)}, u32[]{:S(2)}) collective-permute-start(f32[64,128]{1,0:T(8,128)S(1)} %slice.19), channel_id=1, source_target_pairs={{0,4},{1,5},{2,6},{3,7},{4,0},{5,1},{6,2},{7,3},{8,12},{9,13},{10,... | collective-permute-start | bytes 98312 | tf_op jit(solution)/shard_map/ppermute | solution.py:484

commit v9 on v8

--- a/solution.py
+++ b/solution.py
@@ -31,7 +31,7 @@
 F32 = jnp.float32
 PREP_UNROLL = 6
 FACTOR_ROWS, FACTOR_UNROLL = 64, 4
-UNROLLS = {16: (18, 9), 32: (12, 6), 64: (9, 18)}
+UNROLLS = {16: (18, 9), 32: (18, 6), 64: (9, 18)}
 DOWN_UNROLL = 6
 EDGE = 16
 
@@ -554,6 +554,7 @@
         [shape(4, levels, middle, width), shape(2, middle, width)],
         [VMEM] * 11,
         cols_scratch,
+        limit=8,
         work=1 << 24,
     )(ts, uv, *coefficients, *cols)
     outer, surfaces = call(

time: 57.3 us -> 57.1 us (level)
  no operation moved by 1% of the time
where the time goes in v9:
time: 57.1 us; the launch traced here: 56.9 us
  Pallas kernels  21.7 us (38%)
  waiting for transfers between devices  16.8 us (29%)
  starting transfers between devices  15.6 us (27%)
  between operations  2.15 us (4%)
  other arithmetic  0.64 us (1%)
    ppermute x10, waiting for transfers between devices, swap(): lax.ppermute(block, axis, [(i, i ^ bit) for i in range(lax.axis_size(axis...  11.9 us
    ppermute x4, starting transfers between devices, exchange(): return (lax.ppermute(second, axis, others), swap(first, axis, 1))  9.98 us
    pallas_call x1, Pallas kernels, body(): call(functools.partial(step_kernel, 'whole', ((0, height),)), [pair, pair...  7.01 us
    ppermute x10, starting transfers between devices, swap(): lax.ppermute(block, axis, [(i, i ^ bit) for i in range(lax.axis_size(axis...  5.58 us
    ppermute x4, waiting for transfers between devices, exchange(): return (lax.ppermute(second, axis, others), swap(first, axis, 1))  4.91 us
    pallas_call x1, Pallas kernels, body(): call(functools.partial(step_kernel, 'inner', ((EDGE, middle),)), [shape(4...  3.21 us
    pallas_call x1, Pallas kernels, body(): call(prep_kernel, [pair, pair] + col_pair + row_pair, [SMEM, ANY], [pltpu...  3.14 us
    pallas_call x1, Pallas kernels, body(): call(functools.partial(step_kernel, 'outer', ((0, EDGE), (height - EDGE,...  3.09 us
  transfers between devices with their start and end apart: 14, of which 8 were waited for; matrix products, arithmetic and copies ran while one was open for 0% of the time, Pallas kernels for 12%

profile of v9, /device:TPU:0, one launch (start us, length us, event | category | flops | bytes accessed | tf_op | source)
XLA Modules:
  0.0 56.9 jit_solution(14200137972968844890)
XLA Ops:
  1.3 0.0 copy-start.1
  1.3 0.0 copy-start.2
  1.3 3.1 %shard_map.122 = (f32[2,36,64,128]{3,2,1,0:T(8,128)S(1)}, f32[2,36,64,128]{3,2,1,0:T(8,128)S(1)}, f32[2,64,128]{2,1,0:T(8,128)S(1)}, f32[2,64,128]{2,1,0:T(8,128...) custom-call(s32[1,1]{1,0:T(1,128)S(6)} %copy.13.rot_ref, f32[4,36,64,128]{3,2,1,0:T(8,128)} %adj_ref.1), custom_call_target="tpu_custom_call" | custom-call | flops 8388608 | bytes 8388608 | tf_op jit(solution)/shard_map/pallas_call | solution.py:532
  4.5 4.0 %collective-permute-start.2 = (f32[27,8,128]{2,1,0:T(8,128)S(1)}, f32[27,8,128]{2,1,0:T(8,128)S(1)}, u32[]{:S(2)}, u32[]{:S(2)}) collective-permute-start(f32[27,8,128]{2,1,0:T(8,128)S(1)} %get-tuple-element.37), channel_id=1, source_target_pairs={{0,24},{8,16},{16,8},{24,0},{1,25},{9,17},{17,9},{25,1},{2,26},{10... | collective-permute-start | bytes 331784 | tf_op jit(solution)/shard_map/ppermute | solution.py:490
  8.4 0.5 collective-permute-start.3
  9.0 2.5 %collective-permute-start = (f32[2,64,128]{2,1,0:T(8,128)S(1)}, f32[2,64,128]{2,1,0:T(8,128)S(1)}, u32[]{:S(2)}, u32[]{:S(2)}) collective-permute-start(f32[2,64,128]{2,1,0:T(8,128)S(1)} %get-tuple-element.35), channel_id=1, source_target_pairs={{0,7},{1,2},{2,1},{3,4},{4,3},{5,6},{6,5},{7,0},{8,15},{9,10},{10,... | collective-permute-start | bytes 196616 | tf_op jit(solution)/shard_map/ppermute | solution.py:490
  11.5 1.3 %shard_map.123 = (f32[36,64,128]{2,1,0:T(8,128)S(1)}, f32[36,64,128]{2,1,0:T(8,128)S(1)}, f32[36,64,128]{2,1,0:T(8,128)S(1)}, f32[36,64,128]{2,1,0:T(8,128)S(1)}...) custom-call(f32[36,64,128]{2,1,0:T(8,128)S(1)} %copy-done.3, s32[64,128]{1,0:T(8,128)S(1)} %copy-done.6), custom_call_target="tpu_custom_call" | custom-call | flops 4194304 | bytes 4194304 | tf_op jit(solution)/shard_map/pallas_call | solution.py:541
  12.8 2.1 %collective-permute-done.refs_9_ = f32[2,64,128]{2,1,0:T(8,128)S(1)} collective-permute-done((f32[2,64,128]{2,1,0:T(8,128)S(1)}, f32[2,64,128]{2,1,0:T(8,128)S(1)}, u32[]{:S(2)}, u32[]{:S(2)}) %collective-permute-start) | collective-permute-done | bytes 65568 | tf_op jit(solution)/shard_map/ppermute | solution.py:490
  14.9 7.0 %shard_map.124 = (f32[2,36,64,128]{3,2,1,0:T(8,128)S(1)}, f32[2,36,64,128]{3,2,1,0:T(8,128)S(1)}, f32[2,64,128]{2,1,0:T(8,128)S(1)}, f32[2,112,128]{2,1,0:T(8,12...) custom-call(f32[2,36,64,128]{3,2,1,0:T(8,128)S(1)} %get-tuple-element.29.refs_0_, ...), custom_call_target="tpu_custom_call" | custom-call | tf_op jit(solution)/shard_map/pallas_call | solution.py:543
  22.0 2.1 %collective-permute-start.4 = (f32[2,112,128]{2,1,0:T(8,128)S(1)}, f32[2,112,128]{2,1,0:T(8,128)S(1)}, u32[]{:S(2)}, u32[]{:S(2)}) collective-permute-start(f32[2,112,128]{2,1,0:T(8,128)S(1)} %get-tuple-element.43), channel_id=1, source_target_pairs={{0,7},{1,2},{2,1},{3,4},{4,3},{5,6},{6,5},{7,0},{8,15},{9,10},{10,... | collective-permute-start | bytes 344072 | tf_op jit(solution)/shard_map/ppermute | solution.py:490
  24.1 1.4 %collective-permute-start.6 = (f32[27,8,128]{2,1,0:T(8,128)S(1)}, f32[27,8,128]{2,1,0:T(8,128)S(1)}, u32[]{:S(2)}, u32[]{:S(2)}) collective-permute-start(f32[27,8,128]{2,1,0:T(8,128)S(1)} %get-tuple-element.46), channel_id=1, source_target_pairs={{0,24},{8,16},{16,8},{24,0},{1,25},{9,17},{17,9},{25,1},{2,26},{10... | collective-permute-start | bytes 331784 | tf_op jit(solution)/shard_map/ppermute | solution.py:490
  25.5 0.5 collective-permute-start.7
  26.0 2.8 %collective-permute-done.4.refs_9_ = f32[2,112,128]{2,1,0:T(8,128)S(1)} collective-permute-done((f32[2,112,128]{2,1,0:T(8,128)S(1)}, f32[2,112,128]{2,1,0:T(8,128)S(1)}, u32[]{:S(2)}, u32[]{:S(2)}) %collective-permute-start.4) | collective-permute-done | bytes 114720 | tf_op jit(solution)/shard_map/ppermute | solution.py:490
  28.8 3.2 %shard_map.125 = (f32[4,36,32,128]{3,2,1,0:T(8,128)S(1)}, f32[2,32,128]{2,1,0:T(8,128)S(1)}) custom-call(f32[2,36,64,128]{3,2,1,0:T(8,128)S(1)} %get-tuple-element.41.refs_0_, f32[2,36,64,128]{3,2,1,0:T(8,128)S(1)} %get-tuple-element.42.refs_1_, f32[2,36,64,128]{3,2,1,0:T(8,128)S(1)} %copy-done, f32[36,64,128]{2,1,0:T(8,128)S(1)} %get-tuple-element.31.refs_3_, ...), custom_call_target="tpu_custom_call" | custom-call | flops 16777216 | bytes 16777216 | tf_op jit(solution)/shard_map/pallas_call | solution.py:552
  32.0 3.1 %shard_map.126 = (f32[4,36,32,128]{3,2,1,0:T(8,128)S(1)}, f32[4,64,128]{2,1,0:T(8,128)S(1)}) custom-call(f32[2,36,64,128]{3,2,1,0:T(8,128)S(1)} %get-tuple-element.41.refs_0_, f32[2,36,64,128]{3,2,1,0:T(8,128)S(1)} %get-tuple-element.42.refs_1_, f32[2,36,64,128]{3,2,1,0:T(8,128)S(1)} %copy-done, f32[36,64,128]{2,1,0:T(8,128)S(1)} %get-tuple-element.31.refs_3_, ...), custom_call_target="tpu_custom_call" | custom-call | tf_op jit(solution)/shard_map/pallas_call | solution.py:560
  35.1 2.3 %collective-permute-start.10 = (f32[4,64,128]{2,1,0:T(8,128)S(1)}, f32[4,64,128]{2,1,0:T(8,128)S(1)}, u32[]{:S(2)}, u32[]{:S(2)}) collective-permute-start(f32[4,64,128]{2,1,0:T(8,128)S(1)} %get-tuple-element.53.refs_0_), channel_id=1, source_target_pairs={{0,24},{8,16},{16,8},{24,0},{1,25},{9,17},{17,9},{25,1},{2,26},{10... | collective-permute-start | bytes 393224 | tf_op jit(solution)/shard_map/ppermute | solution.py:484
  37.5 0.5 collective-permute-start.8
  38.0 0.7 %collective-permute-start.9 = (f32[4,64,128]{2,1,0:T(8,128)S(1)}, f32[4,64,128]{2,1,0:T(8,128)S(1)}, u32[]{:S(2)}, u32[]{:S(2)}) collective-permute-start(f32[4,64,128]{2,1,0:T(8,128)S(1)} %get-tuple-element.53.refs_0_), channel_id=1, source_target_pairs={{0,16},{8,24},{16,0},{24,8},{1,17},{9,25},{17,1},{25,9},{2,18},{10... | collective-permute-start | bytes 393224 | tf_op jit(solution)/shard_map/ppermute | solution.py:484
  39.3 0.0 copy-start.4
  39.4 0.0 copy-start.5
  39.4 2.3 %shard_map.127 = (f32[4,36,64,128]{3,2,1,0:T(8,128)}, f32[8,128]{1,0:T(8,128)S(1)}) custom-call(s32[1,1]{1,0:T(1,128)S(6)} %copy.13.rot_ref, f32[4,36,32,128]{3,2,1,0:T(8,128)S(1)} %get-tuple-element.45.inner_ref, f32[4,36,32,128]{3,2,1,0:T(8,128)S(1)} %get-tuple-element.50.outer_ref, f32[36,64,128]{2,1,0:T(8,128)S(1)} %get-tuple-element.39.refs_13_.g1_ref, ...), custom_call_target="tpu_custom_call" | custom-call | flops 8388608 | bytes 8388608 | tf_op jit(solution)/shard_map/pallas_call | solution.py:567
  41.7 0.8 %collective-permute-done.10.refs_3_ = f32[4,64,128]{2,1,0:T(8,128)S(1)} collective-permute-done((f32[4,64,128]{2,1,0:T(8,128)S(1)}, f32[4,64,128]{2,1,0:T(8,128)S(1)}, u32[]{:S(2)}, u32[]{:S(2)}) %collective-permute-start.10) | collective-permute-done | bytes 131104 | tf_op jit(solution)/shard_map/ppermute | solution.py:484
  42.5 1.4 %collective-permute-done.8.refs_1_ = f32[4,64,128]{2,1,0:T(8,128)S(1)} collective-permute-done((f32[4,64,128]{2,1,0:T(8,128)S(1)}, f32[4,64,128]{2,1,0:T(8,128)S(1)}, u32[]{:S(2)}, u32[]{:S(2)}) %collective-permute-start.8) | collective-permute-done | bytes 131104 | tf_op jit(solution)/shard_map/ppermute | solution.py:484
  43.9 0.1 collective-permute-done.9.refs_2_
  44.0 1.7 %shard_map.128 = (f32[256,128]{1,0:T(8,128)S(1)}, f32[256,128]{1,0:T(8,128)S(1)}) custom-call(s32[32]{0:T(128)S(1)} %copy-done.7, s32[1,1]{1,0:T(1,128)S(6)} %copy.14.face_ref, f32[128,256]{1,0:T(8,128)S(1)} %copy-done.5, f32[1024,128]{1,0:T(8,128)S(1)} %copy-done.4, f32[8,128]{1,0:T(8,128)S(1)} %get-tuple-element.52._, ...), custom_call_target="tpu_custom_call" | custom-call | tf_op jit(solution)/shard_map/pallas_call | solution.py:577
  45.6 0.1 collective-permute-start.11
  45.7 1.3 %collective-permute-done.11 = f32[256,128]{1,0:T(8,128)S(1)} collective-permute-done((f32[256,128]{1,0:T(8,128)S(1)}, f32[256,128]{1,0:T(8,128)S(1)}, u32[]{:S(2)}, u32[]{:S(2)}) %collective-permute-start.11) | collective-permute-done | bytes 131104 | tf_op jit(solution)/shard_map/ppermute | solution.py:484
  47.1 0.1 collective-permute-start.12
  47.2 4.3 %collective-permute-done.12 = f32[128,128]{1,0:T(8,128)S(1)} collective-permute-done((f32[128,128]{1,0:T(8,128)S(1)}, f32[128,128]{1,0:T(8,128)S(1)}, u32[]{:S(2)}, u32[]{:S(2)}) %collective-permute-start.12) | collective-permute-done | bytes 65568 | tf_op jit(solution)/shard_map/ppermute | solution.py:484
  51.4 0.8 %collective-permute-start.13 = (f32[64,128]{1,0:T(8,128)S(1)}, f32[64,128]{1,0:T(8,128)S(1)}, u32[]{:S(2)}, u32[]{:S(2)}) collective-permute-start(f32[64,128]{1,0:T(8,128)S(1)} %slice.19), channel_id=1, source_target_pairs={{0,4},{1,5},{2,6},{3,7},{4,0},{5,1},{6,2},{7,3},{8,12},{9,13},{10,... | collective-permute-start | bytes 98312 | tf_op jit(solution)/shard_map/ppermute | solution.py:484
  52.2 4.1 %collective-permute-done.13 = f32[64,128]{1,0:T(8,128)S(1)} collective-permute-done((f32[64,128]{1,0:T(8,128)S(1)}, f32[64,128]{1,0:T(8,128)S(1)}, u32[]{:S(2)}, u32[]{:S(2)}) %collective-permute-start.13) | collective-permute-done | bytes 32800 | tf_op jit(solution)/shard_map/ppermute | solution.py:484
  56.3 0.6 %slice_add_fusion.1 = f32[64,128]{1,0:T(8,128)} fusion(f32[64,128]{1,0:T(8,128)S(1)} %collective-permute-done.13, f32[128,128]{1,0:T(8,128)S(1)} %slice_add_fusion), kind=kLoop, calls=%fused_computation.1 | loop fusion | flops 8192 | bytes 98304 | tf_op jit(solution)/shard_map/add | solution.py:586
  (24 shorter events, 0.1 us)
Async XLA Ops:
  1.3 10.2 %copy-start.3 = (f32[36,64,128]{2,1,0:T(8,128)S(1)}, f32[36,64,128]{2,1,0:T(8,128)}, u32[]{:S(2)}) copy-start(f32[36,64,128]{2,1,0:T(8,128)} %vd_ref.1) | copy-start | bytes 3538948
  1.3 10.2 %copy-start.6 = (s32[64,128]{1,0:T(8,128)S(1)}, s32[64,128]{1,0:T(8,128)}, u32[]{:S(2)}) copy-start(s32[64,128]{1,0:T(8,128)} %wet_ref.1) | copy-start | bytes 98308
  1.3 13.6 %copy-start = (f32[2,36,64,128]{3,2,1,0:T(8,128)S(1)}, f32[2,36,64,128]{3,2,1,0:T(8,128)}, u32[]{:S(2)}) copy-start(f32[2,36,64,128]{3,2,1,0:T(8,128)} %refs_2_.5) | copy-start | bytes 7077892
  1.3 13.6 %copy-start.1 = (bf16[256,256]{1,0:T(8,128)(2,1)S(1)}, bf16[256,256]{1,0:T(8,128)(2,1)}, u32[]{:S(2)}) copy-start(bf16[256,256]{1,0:T(8,128)(2,1)} %constant.11.clone.refs_8_) | copy-start | bytes 393220
  1.3 13.6 %copy-start.2 = (f32[256,128]{1,0:T(8,128)S(1)}, f32[256,128]{1,0:T(8,128)}, u32[]{:S(2)}) copy-start(f32[256,128]{1,0:T(8,128)} %constant.8.clone.refs_7_) | copy-start | bytes 393220
  4.5 10.4 %collective-permute-start.2 = (f32[27,8,128]{2,1,0:T(8,128)S(1)}, f32[27,8,128]{2,1,0:T(8,128)S(1)}, u32[]{:S(2)}, u32[]{:S(2)}) collective-permute-start(f32[27,8,128]{2,1,0:T(8,128)S(1)} %get-tuple-element.37), channel_id=1, source_target_pairs={{0,24},{8,16},{16,8},{24,0},{1,25},{9,17},{17,9},{25,1},{2,26},{10... | collective-permute-start | bytes 331784 | tf_op jit(solution)/shard_map/ppermute | solution.py:490
  8.4 6.5 %collective-permute-start.3 = (f32[27,8,128]{2,1,0:T(8,128)S(1)}, f32[27,8,128]{2,1,0:T(8,128)S(1)}, u32[]{:S(2)}, u32[]{:S(2)}) collective-permute-start(f32[27,8,128]{2,1,0:T(8,128)S(1)} %get-tuple-element.38), channel_id=1, source_target_pairs={{0,8},{8,0},{16,24},{24,16},{1,9},{9,1},{17,25},{25,17},{2,10},{10... | collective-permute-start | bytes 331784 | tf_op jit(solution)/shard_map/ppermute | solution.py:484
  9.0 5.9 %collective-permute-start = (f32[2,64,128]{2,1,0:T(8,128)S(1)}, f32[2,64,128]{2,1,0:T(8,128)S(1)}, u32[]{:S(2)}, u32[]{:S(2)}) collective-permute-start(f32[2,64,128]{2,1,0:T(8,128)S(1)} %get-tuple-element.35), channel_id=1, source_target_pairs={{0,7},{1,2},{2,1},{3,4},{4,3},{5,6},{6,5},{7,0},{8,15},{9,10},{10,... | collective-permute-start | bytes 196616 | tf_op jit(solution)/shard_map/ppermute | solution.py:490
  11.5 3.4 %collective-permute-start.1 = (f32[2,64,128]{2,1,0:T(8,128)S(1)}, f32[2,64,128]{2,1,0:T(8,128)S(1)}, u32[]{:S(2)}, u32[]{:S(2)}) collective-permute-start(f32[2,64,128]{2,1,0:T(8,128)S(1)} %get-tuple-element.36), channel_id=1, source_target_pairs={{0,1},{1,0},{2,3},{3,2},{4,5},{5,4},{6,7},{7,6},{8,9},{9,8},{10,11... | collective-permute-start | bytes 196616 | tf_op jit(solution)/shard_map/ppermute | solution.py:484
  22.0 6.8 %collective-permute-start.4 = (f32[2,112,128]{2,1,0:T(8,128)S(1)}, f32[2,112,128]{2,1,0:T(8,128)S(1)}, u32[]{:S(2)}, u32[]{:S(2)}) collective-permute-start(f32[2,112,128]{2,1,0:T(8,128)S(1)} %get-tuple-element.43), channel_id=1, source_target_pairs={{0,7},{1,2},{2,1},{3,4},{4,3},{5,6},{6,5},{7,0},{8,15},{9,10},{10,... | collective-permute-start | bytes 344072 | tf_op jit(solution)/shard_map/ppermute | solution.py:490
  24.1 4.7 %collective-permute-start.5 = (f32[2,112,128]{2,1,0:T(8,128)S(1)}, f32[2,112,128]{2,1,0:T(8,128)S(1)}, u32[]{:S(2)}, u32[]{:S(2)}) collective-permute-start(f32[2,112,128]{2,1,0:T(8,128)S(1)} %get-tuple-element.44), channel_id=1, source_target_pairs={{0,1},{1,0},{2,3},{3,2},{4,5},{5,4},{6,7},{7,6},{8,9},{9,8},{10,11... | collective-permute-start | bytes 344072 | tf_op jit(solution)/shard_map/ppermute | solution.py:484
  24.1 8.0 %collective-permute-start.6 = (f32[27,8,128]{2,1,0:T(8,128)S(1)}, f32[27,8,128]{2,1,0:T(8,128)S(1)}, u32[]{:S(2)}, u32[]{:S(2)}) collective-permute-start(f32[27,8,128]{2,1,0:T(8,128)S(1)} %get-tuple-element.46), channel_id=1, source_target_pairs={{0,24},{8,16},{16,8},{24,0},{1,25},{9,17},{17,9},{25,1},{2,26},{10... | collective-permute-start | bytes 331784 | tf_op jit(solution)/shard_map/ppermute | solution.py:490
  25.5 6.5 %collective-permute-start.7 = (f32[27,8,128]{2,1,0:T(8,128)S(1)}, f32[27,8,128]{2,1,0:T(8,128)S(1)}, u32[]{:S(2)}, u32[]{:S(2)}) collective-permute-start(f32[27,8,128]{2,1,0:T(8,128)S(1)} %get-tuple-element.47), channel_id=1, source_target_pairs={{0,8},{8,0},{16,24},{24,16},{1,9},{9,1},{17,25},{25,17},{2,10},{10... | collective-permute-start | bytes 331784 | tf_op jit(solution)/shard_map/ppermute | solution.py:484
  35.1 7.4 %collective-permute-start.10 = (f32[4,64,128]{2,1,0:T(8,128)S(1)}, f32[4,64,128]{2,1,0:T(8,128)S(1)}, u32[]{:S(2)}, u32[]{:S(2)}) collective-permute-start(f32[4,64,128]{2,1,0:T(8,128)S(1)} %get-tuple-element.53.refs_0_), channel_id=1, source_target_pairs={{0,24},{8,16},{16,8},{24,0},{1,25},{9,17},{17,9},{25,1},{2,26},{10... | collective-permute-start | bytes 393224 | tf_op jit(solution)/shard_map/ppermute | solution.py:484
  37.5 6.4 %collective-permute-start.8 = (f32[4,64,128]{2,1,0:T(8,128)S(1)}, f32[4,64,128]{2,1,0:T(8,128)S(1)}, u32[]{:S(2)}, u32[]{:S(2)}) collective-permute-start(f32[4,64,128]{2,1,0:T(8,128)S(1)} %get-tuple-element.53.refs_0_), channel_id=1, source_target_pairs={{0,8},{8,0},{16,24},{24,16},{1,9},{9,1},{17,25},{25,17},{2,10},{10... | collective-permute-start | bytes 393224 | tf_op jit(solution)/shard_map/ppermute | solution.py:484
  38.0 6.0 %collective-permute-start.9 = (f32[4,64,128]{2,1,0:T(8,128)S(1)}, f32[4,64,128]{2,1,0:T(8,128)S(1)}, u32[]{:S(2)}, u32[]{:S(2)}) collective-permute-start(f32[4,64,128]{2,1,0:T(8,128)S(1)} %get-tuple-element.53.refs_0_), channel_id=1, source_target_pairs={{0,16},{8,24},{16,0},{24,8},{1,17},{9,25},{17,1},{25,9},{2,18},{10... | collective-permute-start | bytes 393224 | tf_op jit(solution)/shard_map/ppermute | solution.py:484
  39.3 4.6 %copy-start.4 = (f32[1024,128]{1,0:T(8,128)S(1)}, f32[1024,128]{1,0:T(8,128)}, u32[]{:S(2)}) copy-start(f32[1024,128]{1,0:T(8,128)} %constant.10.clone.col_table_ref) | copy-start | bytes 1572868
  39.4 4.6 %copy-start.5 = (f32[128,256]{1,0:T(8,128)S(1)}, f32[128,256]{1,0:T(8,128)}, u32[]{:S(2)}) copy-start(f32[128,256]{1,0:T(8,128)} %constant.9.clone.row_table_ref) | copy-start | bytes 393220
  39.4 4.6 %copy-start.7 = (s32[32]{0:T(128)S(1)}, s32[32]{0:T(128)}, u32[]{:S(2)}) copy-start(s32[32]{0:T(128)} %owner_ref.1) | copy-start | bytes 388
  45.6 1.4 %collective-permute-start.11 = (f32[256,128]{1,0:T(8,128)S(1)}, f32[256,128]{1,0:T(8,128)S(1)}, u32[]{:S(2)}, u32[]{:S(2)}) collective-permute-start(f32[256,128]{1,0:T(8,128)S(1)} %get-tuple-element.55), channel_id=1, source_target_pairs={{0,1},{1,0},{2,3},{3,2},{4,5},{5,4},{6,7},{7,6},{8,9},{9,8},{10,11... | collective-permute-start | bytes 393224 | tf_op jit(solution)/shard_map/ppermute | solution.py:484
  47.1 4.3 %collective-permute-start.12 = (f32[128,128]{1,0:T(8,128)S(1)}, f32[128,128]{1,0:T(8,128)S(1)}, u32[]{:S(2)}, u32[]{:S(2)}) collective-permute-start(f32[128,128]{1,0:T(8,128)S(1)} %slice.17), channel_id=1, source_target_pairs={{0,2},{1,3},{2,0},{3,1},{4,6},{5,7},{6,4},{7,5},{8,10},{9,11},{10,... | collective-permute-start | bytes 196616 | tf_op jit(solution)/shard_map/ppermute | solution.py:484
  51.4 4.9 %collective-permute-start.13 = (f32[64,128]{1,0:T(8,128)S(1)}, f32[64,128]{1,0:T(8,128)S(1)}, u32[]{:S(2)}, u32[]{:S(2)}) collective-permute-start(f32[64,128]{1,0:T(8,128)S(1)} %slice.19), channel_id=1, source_target_pairs={{0,4},{1,5},{2,6},{3,7},{4,0},{5,1},{6,2},{7,3},{8,12},{9,13},{10,... | collective-permute-start | bytes 98312 | tf_op jit(solution)/shard_map/ppermute | solution.py:484
